TPU v7x, 32 devices: a whole 2x2x4 slice. The times are simulated.
32 devices in a mesh: grp: 2 (over x), det: 16 (over z, y, core).
Axes of the slice: x: 2, y: 2, z: 4, core: 2. Of those that a mesh axis runs over, the one named last changes fastest.
Arguments:
- timestream: float32 [2, 1024, 16384], P('grp', 'det'), parts along dimension 0, may hold values from -6 to 6
- gains: float32 [2, 1024], P('grp', 'det'), parts along dimension 0, may hold values from 0.5 to 2
- mode_pattern: float32 [2048, 256], P('grp'), parts along dimension 0, may hold values from -0.375 to 0.375
- mode_weights: float32 [2048, 256], P('grp'), parts along dimension 0, may hold values from -0.1875 to 0.1875
- noise_weight: float32 [2048, 16384], P(('grp', 'det')), parts along dimension 0, may hold values from 0.05 to 1
- block_ids: int32 [2, 1024, 64], P('grp', 'det'), parts along dimension 0, may hold values from 0 to 255
- hits: int32 [2, 1024, 64], P('grp', 'det'), parts along dimension 0, may hold values from 0 to 3
- sky_rows: int32 [512], P('grp'), parts along dimension 0, may hold values from 0 to 255, each once
Outputs:
- filtered: float32 [2, 1024, 16384], P('grp', 'det'), parts along dimension 0
- sky_map: float32 [512, 256], P(('grp', 'det')), parts along dimension 0
There are 2 independent parts, one for each index of `grp`. A program takes and returns all parts, laid end to end along the dimension named above; each array names one. Nothing has to cross between parts.
Inputs may be any that keep to these rules, and one draw needn't show every extreme that they name: `sky_rows`: each row number appears exactly once.
All inputs are finite; a program needn't handle non-finite values.
Results may differ from a plain program's by a relative error of at most 0.000078.
Values sent between devices are 32-bit elements; how exact they have to be, the bound alone decides.
No kernel may reach another device: no remote copies, remote signals or barrier semaphores. Data moves between devices by JAX's collectives and lax.ppermute only.
A program may use at most 128 MiB of HBM per device.

v0:
```python
import functools
import math

import jax
import jax.numpy as jnp
from jax import lax
from jax.experimental import pallas as pl
from jax.experimental.pallas import tpu as pltpu
from jax.sharding import PartitionSpec as P


F32, BF16 = jnp.float32, jnp.bfloat16
ROWS = 8
UNITS = 8
PARTS = (1, 1)
LIMIT = pltpu.CompilerParams(vmem_limit_bytes=16 << 20)


def halves(value):
    high = value.astype(BF16)
    return high, (value - high.astype(F32)).astype(BF16)


def table_halves(table):
    high = lax.reduce_precision(table, exponent_bits=8, mantissa_bits=7)
    return high.astype(BF16), (table - high).astype(BF16)


def mm(a, b):
    return jnp.dot(a, b, preferred_element_type=F32)


def mm3(a_pair, b_pair):
    return mm(a_pair[0], b_pair[0]) + (mm(a_pair[1], b_pair[0]) + mm(a_pair[0], b_pair[1]))


def angles(count, first, second):
    return (first * second % count).astype(F32) * (2.0 * math.pi / count)


def section_table(side, unit_of_slot):
    unit = unit_of_slot[:, None, None]
    sample = lax.broadcasted_iota(jnp.int32, (1, 1, side), 2)
    part = lax.broadcasted_iota(jnp.int32, (1, 2, 1), 1)
    nyquist = (unit == 0) & (part == 1)
    angle = angles(side, jnp.where(nyquist, side // 2, unit), sample)
    table = jnp.where((part == 0) | nyquist, jnp.cos(angle), -jnp.sin(angle))
    return table.reshape(-1, side)


def inner_tables(side):
    first = lax.broadcasted_iota(jnp.int32, (side, side), 0)
    second = lax.broadcasted_iota(jnp.int32, (side, side), 1)
    angle = angles(side, first, second)
    cos, sin = jnp.cos(angle), jnp.sin(angle)
    forward = jnp.concatenate([jnp.concatenate([cos, -sin], 1), jnp.concatenate([sin, cos], 1)], 0)
    backward = jnp.concatenate([jnp.concatenate([cos, sin], 1), jnp.concatenate([-sin, cos], 1)], 0)
    return forward, backward


def twiddles(side):
    unit = lax.broadcasted_iota(jnp.int32, (side // 2 + 8, side), 0)
    sample = lax.broadcasted_iota(jnp.int32, (side // 2 + 8, side), 1)
    angle = angles(side * side, unit, sample)
    return jnp.cos(angle), jnp.sin(angle)


def section_kernel(side, x_ref, scale_ref, high_ref, low_ref, *refs):
    out_refs, (rows, turned) = refs[:-2], refs[-2:]
    scale = scale_ref[...]
    for n in range(side):
        rows[n * ROWS : (n + 1) * ROWS, :] = x_ref[:, n * side : (n + 1) * side] * scale
    table = (high_ref[...], low_ref[...])
    for d in range(0, ROWS, 2):
        pair = jnp.concatenate([rows[pl.ds(d, side, stride=ROWS), :], rows[pl.ds(d + 1, side, stride=ROWS), :]], axis=1)
        result = mm3(table, halves(pair))
        turned[pl.ds(d, side, stride=ROWS), :] = result[:, :side]
        turned[pl.ds(d + 1, side, stride=ROWS), :] = result[:, side:]
    lines = [(out_ref, row) for out_ref in out_refs for row in range(out_ref.shape[0])]
    for k, (out_ref, row) in enumerate(lines):
        out_ref[row] = turned[k * ROWS : (k + 1) * ROWS, :]


def sections(signal, scale, table, shares):
    dets, samples = signal.shape
    side = table.shape[0]
    high, low = table_halves(table)
    whole = pl.BlockSpec((side, side), lambda i: (0, 0))
    return pl.pallas_call(
        functools.partial(section_kernel, side),
        grid=(dets // ROWS,),
        in_specs=[pl.BlockSpec((ROWS, samples), lambda i: (i, 0)), pl.BlockSpec((ROWS, side), lambda i: (i, 0)), whole, whole],
        out_specs=[pl.BlockSpec((share, ROWS, side), lambda i: (0, i, 0)) for share in shares],
        out_shape=[jax.ShapeDtypeStruct((share, dets, side), F32) for share in shares],
        scratch_shapes=[pltpu.VMEM((side * ROWS, side), F32), pltpu.VMEM((side * ROWS, side), F32)],
        compiler_params=LIMIT,
        name="sections",
    )(signal, scale, high, low)


def cost(passes, rows, depth, columns, *arrays):
    moved = sum(array.size * array.dtype.itemsize for array in arrays)
    return pl.CostEstimate(flops=2 * passes * rows * depth * columns, bytes_accessed=moved, transcendentals=0)


def coeff_kernel(z_ref, high_ref, low_ref, out_ref, z_high, z_low):
    blocks, rows, dets, side = z_ref.shape
    for b in range(blocks):
        for k in range(rows):
            high, low = halves(z_ref[b, k])
            z_high[b * dets : (b + 1) * dets, k * side : (k + 1) * side] = high
            z_low[b * dets : (b + 1) * dets, k * side : (k + 1) * side] = low
    total = mm3((high_ref[...], low_ref[...]), (z_high[...], z_low[...]))
    for k in range(rows):
        out_ref[k] = total[:, k * side : (k + 1) * side]


def coefficients(slab, weights):
    blocks, rows, dets, side = slab.shape
    rank = weights[0].shape[0]
    out = jax.ShapeDtypeStruct((rows, rank, side), F32)
    step = math.gcd(2, rows)
    whole = pl.BlockSpec((rank, blocks * dets), lambda i: (0, 0))
    return pl.pallas_call(
        coeff_kernel,
        grid=(rows // step,),
        in_specs=[pl.BlockSpec((blocks, step, dets, side), lambda i: (0, i, 0, 0)), whole, whole],
        out_specs=pl.BlockSpec((step, rank, side), lambda i: (i, 0, 0)),
        out_shape=out,
        scratch_shapes=[pltpu.VMEM((blocks * dets, step * side), BF16)] * 2,
        compiler_params=LIMIT,
        cost_estimate=cost(3, rank, blocks * dets, rows * side, slab, out),
        name="coefficients",
    )(slab, *weights)


def correct_kernel(terms, z_ref, *refs):
    c_refs, (high_ref, low_ref, out_ref) = refs[:terms], refs[terms:]
    blocks, rows, dets, side = z_ref.shape
    coeff = halves(jnp.concatenate([sum(c_ref[k] for c_ref in c_refs) for k in range(rows)], axis=1))
    share = mm3((high_ref[...], low_ref[...]), coeff)
    for b in range(blocks):
        for k in range(rows):
            out_ref[b, k] = z_ref[b, k] - share[b * dets : (b + 1) * dets, k * side : (k + 1) * side]


def corrected(slab, coeffs, pattern):
    blocks, rows, dets, side = slab.shape
    rank = pattern[0].shape[1]
    step = math.gcd(2, rows)
    whole = pl.BlockSpec((blocks * dets, rank), lambda i: (0, 0))
    block = pl.BlockSpec((blocks, step, dets, side), lambda i: (0, i, 0, 0))
    return pl.pallas_call(
        functools.partial(correct_kernel, len(coeffs)),
        grid=(rows // step,),
        in_specs=[block] + [pl.BlockSpec((step, rank, side), lambda i: (i, 0, 0)) for _ in coeffs] + [whole, whole],
        out_specs=block,
        out_shape=jax.ShapeDtypeStruct(slab.shape, F32),
        compiler_params=LIMIT,
        cost_estimate=cost(3, rank, blocks * dets, rows * side, slab, slab, *coeffs),
        name="corrected",
    )(slab, *coeffs, *pattern)


def filter_kernel(base, count, z_ref, w_ref, extra_ref, cos_ref, sin_ref, fh_ref, fl_ref, bh_ref, bl_ref, out_ref, t_high, t_low, result):
    _, dets, side = z_ref.shape
    step = pl.program_id(0)
    first = base + step * count
    half_cos, half_sin = cos_ref[pl.ds(side // 2, 1), :], sin_ref[pl.ds(side // 2, 1), :]
    turns = [(cos_ref[pl.ds(first + i, 1), :], sin_ref[pl.ds(first + i, 1), :]) for i in range(count)]
    has_zero = base == 0

    def put(slot, real, imag):
        for part, value in ((0, real), (1, imag)):
            high, low = halves(value)
            t_high[slot * dets : (slot + 1) * dets, part * side : (part + 1) * side] = high
            t_low[slot * dets : (slot + 1) * dets, part * side : (part + 1) * side] = low

    for i in range(count):
        real, imag = z_ref[2 * i], z_ref[2 * i + 1]
        if has_zero and i == 0:
            put(count, imag * half_cos, -imag * half_sin)
            imag = jnp.where(first == 0, 0.0, imag)
        cos, sin = turns[i]
        put(i, real * cos + imag * sin, imag * cos - real * sin)
    result[...] = mm3((t_high[...], t_low[...]), (fh_ref[...], fl_ref[...]))
    for i in range(count + has_zero):
        weight = extra_ref[...] if i == count else w_ref[i]
        at = slice(i * dets, (i + 1) * dets)
        put(i, result[at, :side] * weight, result[at, side:] * weight)
    result[...] = mm3((t_high[...], t_low[...]), (bh_ref[...], bl_ref[...]))
    for i in range(count):
        at = slice(i * dets, (i + 1) * dets)
        real, imag = result[at, :side], result[at, side:]
        cos, sin = turns[i]
        turned = imag * cos + real * sin
        if has_zero and i == 0:
            at = slice(count * dets, (count + 1) * dets)
            nyquist = result[at, :side] * half_cos - result[at, side:] * half_sin
            turned = jnp.where(first == 0, nyquist, turned)
        out_ref[2 * i] = real * cos - imag * sin
        out_ref[2 * i + 1] = turned


def filter_units(base, slab, weight, extra, tables):
    rows, dets, side = slab.shape
    count = math.gcd(math.gcd(rows // 2, UNITS), base) if base else math.gcd(rows // 2, UNITS)
    held = (count + (base == 0)) * dets
    whole = lambda a: pl.BlockSpec(a.shape, lambda i: (0,) * a.ndim)
    block = pl.BlockSpec((2 * count, dets, side), lambda i: (i, 0, 0))
    return pl.pallas_call(
        functools.partial(filter_kernel, base, count),
        grid=(rows // (2 * count),),
        in_specs=[block, pl.BlockSpec((count, dets, side), lambda i: (base // count + i, 0, 0)), whole(extra)]
        + [whole(t) for t in tables],
        out_specs=block,
        out_shape=jax.ShapeDtypeStruct(slab.shape, F32),
        scratch_shapes=[pltpu.VMEM((held, 2 * side), BF16)] * 2 + [pltpu.VMEM((held, 2 * side), F32)],
        compiler_params=LIMIT,
        cost_estimate=cost(6, rows // 2 * dets, 2 * side, 2 * side, slab, slab, slab),
        name="filter_units",
    )(slab, weight, extra, *tables)


def finish_kernel(side, tiles, chunks, *refs):
    f_refs, refs = refs[:chunks], refs[chunks:]
    high_ref, low_ref, rows_ref, hits_ref, out_ref, sums_ref, turned, lined, one, t_high, t_low = refs
    step = pl.program_id(0)
    blocks = sums_ref.shape[0]

    @pl.when(step == 0)
    def _():
        sums_ref[...] = jnp.zeros_like(sums_ref)

    lines = [f_ref[row] for f_ref in f_refs for row in range(f_ref.shape[0])]
    for k in range(side):
        turned[k * ROWS : (k + 1) * ROWS, :] = lines[k]
    table = (high_ref[...], low_ref[...])
    for d in range(0, ROWS, 2):
        pair = jnp.concatenate(
            [turned[pl.ds(d, side, stride=ROWS), :], turned[pl.ds(d + 1, side, stride=ROWS), :]], axis=1
        )
        result = mm3(table, halves(pair))
        for e in (0, 1):
            value = result[:, e * side : (e + 1) * side]
            lined[pl.ds(d + e, side, stride=ROWS), :] = value
            one[...] = value
            for half in (0, 1):
                high, low = halves(one[pl.ds(half, side // 2, stride=2), :])
                at = slice((d + e) * tiles, (d + e + 1) * tiles)
                t_high[at, half * side : (half + 1) * side] = high
                t_low[at, half * side : (half + 1) * side] = low
    for n in range(side):
        out_ref[:, n * side : (n + 1) * side] = lined[n * ROWS : (n + 1) * ROWS, :]
    ladder = lax.broadcasted_iota(jnp.int32, (blocks, ROWS * tiles), 0)
    chosen = jnp.where(rows_ref[0] == ladder, hits_ref[0], 0.0).astype(BF16)
    sums_ref[...] += mm(chosen, t_high[...]) + mm(chosen, t_low[...])


def finish(units, table, rows, hits, blocks):
    _, dets, side = units[0].shape
    tiles = rows.size // dets
    high, low = table_halves(table)
    whole = pl.BlockSpec((side, side), lambda i: (0, 0))
    line = pl.BlockSpec((1, 1, ROWS * tiles), lambda i: (i, 0, 0))
    steps = dets // ROWS
    return pl.pallas_call(
        functools.partial(finish_kernel, side, tiles, len(units)),
        grid=(steps,),
        in_specs=[pl.BlockSpec((u.shape[0], ROWS, side), lambda i: (0, i, 0)) for u in units] + [whole, whole, line, line],
        out_specs=[pl.BlockSpec((ROWS, side * side), lambda i: (i, 0)), pl.BlockSpec((blocks, 2 * side), lambda i: (0, 0))],
        out_shape=[jax.ShapeDtypeStruct((dets, side * side), F32), jax.ShapeDtypeStruct((blocks, 2 * side), F32)],
        scratch_shapes=[pltpu.VMEM((side * ROWS, side), F32)] * 2
        + [pltpu.VMEM((side, side), F32)]
        + [pltpu.VMEM((ROWS * tiles, 2 * side), BF16)] * 2,
        compiler_params=LIMIT,
        name="finish",
    )(*units, high, low, rows.reshape(steps, 1, ROWS * tiles), hits.reshape(steps, 1, ROWS * tiles))


def shards(size, timestream, gains, mode_pattern, mode_weights, noise_weight, block_ids, hits, sky_rows):
    _, dets, samples = timestream.shape
    side = math.isqrt(samples)
    units = side // 2
    blocks = sky_rows.shape[0]
    half = size // 2
    groups = [list(range(half)), list(range(half, size))]
    opposite = [(i, (i + half) % size) for i in range(size)]
    mine = lax.axis_index("det") // half

    starts = [side * sum(PARTS[:c]) // sum(PARTS) for c in range(len(PARTS) + 1)]
    shares = [b - a for a, b in zip(starts, starts[1:])]
    chunks = range(len(PARTS))

    scale = jnp.broadcast_to(1.0 / gains.reshape(dets, 1), (dets, side))
    table = section_table(side, lax.iota(jnp.int32, units))
    z = sections(timestream.reshape(dets, samples), scale, table, shares)

    def of_half(modes):
        return lax.dynamic_index_in_dim(modes.reshape(2, half * dets, -1), mine, 0, keepdims=False)

    weights = table_halves(of_half(mode_weights).T)
    pattern = table_halves(of_half(mode_pattern))
    w = jnp.transpose(noise_weight.reshape(dets, side, side), (2, 0, 1))
    mirror = w[:units:-1, :, ::-1]
    weight = jnp.concatenate([w[:1], w[1:units] + mirror], axis=0)
    extra = w[units]
    forward, backward = inner_tables(side)
    tables = [*twiddles(side), *table_halves(forward), *table_halves(backward)]

    last = [None]

    def exchange(value):
        if last[0] is not None:
            value, _ = lax.optimization_barrier((value, last[0]))
        last[0] = lax.all_to_all(value, "det", split_axis=0, concat_axis=0, axis_index_groups=groups, tiled=True)
        return last[0]

    slabs, coeffs, others = [], [], []
    for c in chunks:
        slabs.append(exchange(z[c]).reshape(half, shares[c] // half, dets, side))
        coeffs.append(coefficients(slabs[c], weights))
        last[0] = coeffs[c]
        others.append(lax.ppermute(coeffs[c], "det", opposite))
    done = []
    for c in chunks:
        slab = corrected(slabs[c], [coeffs[c], others[c]], pattern)
        back = exchange(slab.reshape(shares[c], dets, side))
        done.append(filter_units(starts[c] // 2, back, weight, extra, tables))

    ids_flat = block_ids.reshape(-1)
    ladder = lax.broadcasted_iota(jnp.int32, (blocks, ids_flat.shape[0]), 0)
    rows = jnp.sum(jnp.where(ids_flat[None, :] == ladder, sky_rows[:, None], 0), axis=0)
    hit = hits.reshape(-1).astype(F32)
    counts = jnp.sum(jnp.where(rows[None, :] == ladder, hit[None, :], 0.0), axis=1)
    filtered, sums = finish(done, table.T / samples, rows, hit, blocks)

    own = blocks // size
    tail = jnp.pad(counts.reshape(size, 1, own), ((0, 0), (0, ROWS - 1), (0, 2 * side - own)))
    parcel = jnp.concatenate([sums.reshape(size, own, 2 * side), tail], axis=1)
    parcel = lax.all_to_all(parcel, "det", split_axis=0, concat_axis=0, tiled=True)
    parcel = jnp.sum(parcel, axis=0)
    sky_map = parcel[:own] / jnp.sqrt(1.0 + parcel[own, :own])[:, None]
    return filtered.reshape(timestream.shape), sky_map


def solution(mesh):
    in_specs = (
        P("grp", "det", None),
        P("grp", "det"),
        P("grp", None),
        P("grp", None),
        P(("grp", "det"), None),
        P("grp", "det", None),
        P("grp", "det", None),
        P("grp"),
    )
    out_specs = (P("grp", "det", None), P(("grp", "det"), None))
    body = functools.partial(shards, mesh.shape["det"])

    return jax.shard_map(body, mesh=mesh, in_specs=in_specs, out_specs=out_specs, check_vma=False)
```

profile of v0, /device:TPU:0, one launch (start us, length us, event | category | flops | bytes accessed | tf_op | source)
XLA Modules:
  0.0 242.8 jit_solution(5881439412492637070)
XLA Ops:
  3.3 2.2 copy-done.5
  5.5 4.4 %sections.1 = (f32[64,64,128]{2,1,0:T(8,128)S(1)}, f32[64,64,128]{2,1,0:T(8,128)S(1)}) custom-call(f32[64,16384]{1,0:T(8,128)S(1)} %bitcast.34, f32[64,128]{1,0:T(8,128)S(1)} %broadcast_in_dim.74.scale_ref, bf16[128,128]{1,0:T(8,128)(2,1)S(1)} %get-tuple-element.29.high_ref, bf16[128,128]{1,0:T(8,128)(2,1)S(1)} %get-tuple-element.27.low_ref), custom_call_target="tpu_custom_call" | custom-call | tf_op jit(solution)/shard_map/sections/pallas_call | solution.py:89
  12.6 5.3 %all-to-all-start = ((f32[64,64,128]{2,1,0:T(8,128)}), f32[64,64,128]{2,1,0:T(8,128)S(1)}, u32[]{:S(2)}, u32[]{:S(2)}) async-start(f32[64,64,128]{2,1,0:T(8,128)} %copy-done.17), calls=%async_computation | async-start | bytes 4194304 | tf_op jit(solution)/shard_map/all_to_all | solution.py:316
  18.7 2.0 copy.15
  22.6 21.0 %all-to-all-done = f32[64,64,128]{2,1,0:T(8,128)S(1)} async-done(((f32[64,64,128]{2,1,0:T(8,128)}), f32[64,64,128]{2,1,0:T(8,128)S(1)}, u32[]{:S(2)}, u32[]{:S(2)}) %all-to-all-start) | async-done | bytes 2097184 | tf_op jit(solution)/shard_map/all_to_all | solution.py:316
  47.4 4.3 %all-to-all-start.1 = ((f32[64,64,128]{2,1,0:T(8,128)}), f32[64,64,128]{2,1,0:T(8,128)}, u32[]{:S(2)}, u32[]{:S(2)}) async-start(f32[64,64,128]{2,1,0:T(8,128)} %copy-done.16), calls=%async_computation.1 | async-start | bytes 4194304 | tf_op jit(solution)/shard_map/all_to_all | solution.py:316
  51.7 2.7 %collective-permute-start = (f32[8,256,128]{2,1,0:T(8,128)}, f32[8,256,128]{2,1,0:T(8,128)S(1)}, u32[]{:S(2)}, u32[]{:S(2)}) collective-permute-start(f32[8,256,128]{2,1,0:T(8,128)} %copy-done.6), channel_id=1, source_target_pairs={{0,8},{1,9},{2,10},{3,11},{4,12},{5,13},{6,14},{7,15},{8,0},{9,1},... | collective-permute-start | bytes 3145736 | tf_op jit(solution)/shard_map/ppermute | solution.py:324
  55.5 42.3 %collective-permute-done.refs_1_ = f32[8,256,128]{2,1,0:T(8,128)S(1)} collective-permute-done((f32[8,256,128]{2,1,0:T(8,128)}, f32[8,256,128]{2,1,0:T(8,128)S(1)}, u32[]{:S(2)}, u32[]{:S(2)}) %collective-permute-start) | collective-permute-done | bytes 1048608 | tf_op jit(solution)/shard_map/ppermute | solution.py:324
  99.1 2.9 %corrected.2 = f32[8,8,64,128]{3,2,1,0:T(8,128)} custom-call(f32[8,8,64,128]{3,2,1,0:T(8,128)S(1)} %bitcast.33, f32[8,256,128]{2,1,0:T(8,128)S(1)} %copy-done.7, f32[8,256,128]{2,1,0:T(8,128)S(1)} %collective-permute-done.refs_1_, bf16[512,256]{1,0:T(8,128)(2,1)S(1)} %get-tuple-element.19.refs_2_, bf16[512,256]{1,0:T(8,128)(2,1)S(1)} %get-tuple-element.18.refs_3_), custom_call_target="tpu_custom_call" | custom-call | flops 805306368 | bytes 6291456 | tf_op jit(solution)/shard_map/corrected/pallas_call | solution.py:153
  104.3 3.4 %coefficients.3.refs_0_ = f32[8,256,128]{2,1,0:T(8,128)S(1)} custom-call(f32[8,8,64,128]{3,2,1,0:T(8,128)} %bitcast.10.z_ref, bf16[256,512]{1,0:T(8,128)(2,1)S(1)} %copy-done.11, bf16[256,512]{1,0:T(8,128)(2,1)S(1)} %get-tuple-element.20.low_ref), custom_call_target="tpu_custom_call" | custom-call | flops 805306368 | bytes 3145728 | tf_op jit(solution)/shard_map/coefficients/pallas_call | solution.py:124
  108.7 6.9 %all-to-all-start.2 = ((f32[64,64,128]{2,1,0:T(8,128)}), f32[64,64,128]{2,1,0:T(8,128)S(1)}, u32[]{:S(2)}, u32[]{:S(2)}) async-start(f32[64,64,128]{2,1,0:T(8,128)} %bitcast.9), calls=%async_computation.2 | async-start | bytes 4194304 | tf_op jit(solution)/shard_map/all_to_all | solution.py:316
  115.6 2.7 %collective-permute-start.1 = (f32[8,256,128]{2,1,0:T(8,128)}, f32[8,256,128]{2,1,0:T(8,128)S(1)}, u32[]{:S(2)}, u32[]{:S(2)}) collective-permute-start(f32[8,256,128]{2,1,0:T(8,128)} %copy-done.8), channel_id=1, source_target_pairs={{0,8},{1,9},{2,10},{3,11},{4,12},{5,13},{6,14},{7,15},{8,0},{9,1},... | collective-permute-start | bytes 3145736 | tf_op jit(solution)/shard_map/ppermute | solution.py:324
  118.2 43.6 %collective-permute-done.1.refs_1_ = f32[8,256,128]{2,1,0:T(8,128)S(1)} collective-permute-done((f32[8,256,128]{2,1,0:T(8,128)}, f32[8,256,128]{2,1,0:T(8,128)S(1)}, u32[]{:S(2)}, u32[]{:S(2)}) %collective-permute-start.1) | collective-permute-done | bytes 1048608 | tf_op jit(solution)/shard_map/ppermute | solution.py:324
  164.0 4.5 %corrected.3 = f32[8,8,64,128]{3,2,1,0:T(8,128)} custom-call(f32[8,8,64,128]{3,2,1,0:T(8,128)} %bitcast.10.z_ref, f32[8,256,128]{2,1,0:T(8,128)S(1)} %copy-done.9, f32[8,256,128]{2,1,0:T(8,128)S(1)} %collective-permute-done.1.refs_1_, bf16[512,256]{1,0:T(8,128)(2,1)S(1)} %copy-done.15, bf16[512,256]{1,0:T(8,128)(2,1)S(1)} %copy-done.13), custom_call_target="tpu_custom_call" | custom-call | flops 805306368 | bytes 6291456 | tf_op jit(solution)/shard_map/corrected/pallas_call | solution.py:153
  169.9 6.8 %all-to-all-start.3 = ((f32[64,64,128]{2,1,0:T(8,128)}), f32[64,64,128]{2,1,0:T(8,128)}, u32[]{:S(2)}, u32[]{:S(2)}) async-start(f32[64,64,128]{2,1,0:T(8,128)} %bitcast.13), calls=%async_computation.3 | async-start | bytes 4194304 | tf_op jit(solution)/shard_map/all_to_all | solution.py:316
  177.4 4.9 %copy.16 = f32[8,8,128,128]{3,2,1,0:T(8,128)} copy(f32[8,8,128,128]{3,1,2,0:T(8,128)} %bitcast.41) | data formatting | bytes 8388608
  182.4 5.4 %copy.14 = f32[64,128,128]{1,0,2:T(8,128)} copy(f32[64,128,128]{2,1,0:T(8,128)} %bitcast.40) | data formatting | bytes 8388608 | tf_op jit(solution)/shard_map/reshape | solution.py:304
  187.7 3.1 %slice.26 = f32[63,64,128]{2,1,0:T(8,128)} slice(f32[128,64,128]{2,1,0:T(8,128)} %bitcast.37), slice={[65:128], [0:64], [0:128]} | slice | bytes 4128768 | tf_op jit(solution)/shard_map/slice | solution.py:305
  190.8 3.2 %rev.3 = f32[63,64,128]{2,1,0:T(8,128)S(1)} reverse(f32[63,64,128]{2,1,0:T(8,128)} %slice.26), dimensions={0,2} | reverse | bytes 4128768 | tf_op jit(solution)/shard_map/rev | solution.py:305
  197.8 2.0 slice_add_fusion
  201.4 4.5 %filter_units.2.refs_0_ = f32[64,64,128]{2,1,0:T(8,128)S(1)} custom-call(f32[64,64,128]{2,1,0:T(8,128)S(1)} %copy-done.2, f32[64,64,128]{2,1,0:T(8,128)S(1)} %pad_maximum_fusion.w_ref, f32[64,128]{1,0:T(8,128)S(1)} %get-tuple-element.16.extra_ref, f32[72,128]{1,0:T(8,128)S(1)} %get-tuple-element.33.cos_ref, f32[72,128]{1,0:T(8,128)S(1)} %get-tuple-element.32.sin_ref, ...), custom_call_target="tpu_custom_call" | custom-call | flops 1610612736 | bytes 6291456 | tf_op jit(solution)/shard_map/filter_units/pallas_call | solution.py:211
  210.4 5.3 %filter_units.3.refs_1_ = f32[64,64,128]{2,1,0:T(8,128)S(1)} custom-call(f32[64,64,128]{2,1,0:T(8,128)} %all-to-all-done.3.z_ref, f32[64,64,128]{2,1,0:T(8,128)S(1)} %pad_maximum_fusion.w_ref, f32[64,128]{1,0:T(8,128)S(1)} %copy-done.25, f32[72,128]{1,0:T(8,128)S(1)} %copy-done.23, f32[72,128]{1,0:T(8,128)S(1)} %copy-done.21, ...), custom_call_target="tpu_custom_call" | custom-call | flops 1610612736 | bytes 6291456 | tf_op jit(solution)/shard_map/filter_units/pallas_call | solution.py:211
  215.7 7.8 %finish.1 = (f32[64,16384]{1,0:T(8,128)}, f32[256,256]{1,0:T(8,128)S(1)}) custom-call(f32[64,64,128]{2,1,0:T(8,128)S(1)} %copy-done.4, f32[64,64,128]{2,1,0:T(8,128)S(1)} %filter_units.3.refs_1_, bf16[128,128]{1,0:T(8,128)(2,1)S(1)} %copy-done.27, bf16[128,128]{1,0:T(8,128)(2,1)S(1)} %copy-done.26, s32[8,1,512]{2,1,0:T(1,128)S(1)} %bitcast.36, ...), custom_call_target="tpu_custom_call" | custom-call | tf_op jit(solution)/shard_map/finish/pallas_call | solution.py:267
  223.6 18.4 %all_to_all.25 = f32[16,24,256]{2,1,0:T(8,128)S(1)} all-to-all(f32[16,24,256]{2,1,0:T(8,128)S(1)} %select_maximum_fusion), channel_id=1, replica_groups=mesh['grp'=2,'det'=16] {'det'}, dimensions={0} | all-to-all | bytes 786432 | tf_op jit(solution)/shard_map/all_to_all | solution.py:341
  (105 shorter events, 32.3 us)
Async XLA Ops:
  0.6 17.2 %copy-start = (f32[1024,256]{1,0:T(8,128)S(1)}, f32[1024,256]{1,0:T(8,128)}, u32[]{:S(2)}) copy-start(f32[1024,256]{1,0:T(8,128)} %param.11) | copy-start | bytes 3145732
  3.3 2.2 copy-start.5
  9.9 1.3 copy-start.16
  12.6 31.0 %all-to-all-start = ((f32[64,64,128]{2,1,0:T(8,128)}), f32[64,64,128]{2,1,0:T(8,128)S(1)}, u32[]{:S(2)}, u32[]{:S(2)}) async-start(f32[64,64,128]{2,1,0:T(8,128)} %copy-done.17), calls=%async_computation | async-start | bytes 4194304 | tf_op jit(solution)/shard_map/all_to_all | solution.py:316
  47.4 56.0 %all-to-all-start.1 = ((f32[64,64,128]{2,1,0:T(8,128)}), f32[64,64,128]{2,1,0:T(8,128)}, u32[]{:S(2)}, u32[]{:S(2)}) async-start(f32[64,64,128]{2,1,0:T(8,128)} %copy-done.16), calls=%async_computation.1 | async-start | bytes 4194304 | tf_op jit(solution)/shard_map/all_to_all | solution.py:316
  51.7 46.1 %collective-permute-start = (f32[8,256,128]{2,1,0:T(8,128)}, f32[8,256,128]{2,1,0:T(8,128)S(1)}, u32[]{:S(2)}, u32[]{:S(2)}) collective-permute-start(f32[8,256,128]{2,1,0:T(8,128)} %copy-done.6), channel_id=1, source_target_pairs={{0,8},{1,9},{2,10},{3,11},{4,12},{5,13},{6,14},{7,15},{8,0},{9,1},... | collective-permute-start | bytes 3145736 | tf_op jit(solution)/shard_map/ppermute | solution.py:324
  108.7 53.1 %copy-start.13 = (bf16[512,256]{1,0:T(8,128)(2,1)S(1)}, bf16[512,256]{1,0:T(8,128)(2,1)}, u32[]{:S(2)}) copy-start(bf16[512,256]{1,0:T(8,128)(2,1)} %copy-done.12) | copy-start | bytes 786436
  108.7 59.8 %all-to-all-start.2 = ((f32[64,64,128]{2,1,0:T(8,128)}), f32[64,64,128]{2,1,0:T(8,128)S(1)}, u32[]{:S(2)}, u32[]{:S(2)}) async-start(f32[64,64,128]{2,1,0:T(8,128)} %bitcast.9), calls=%async_computation.2 | async-start | bytes 4194304 | tf_op jit(solution)/shard_map/all_to_all | solution.py:316
  115.6 46.2 %collective-permute-start.1 = (f32[8,256,128]{2,1,0:T(8,128)}, f32[8,256,128]{2,1,0:T(8,128)S(1)}, u32[]{:S(2)}, u32[]{:S(2)}) collective-permute-start(f32[8,256,128]{2,1,0:T(8,128)} %copy-done.8), channel_id=1, source_target_pairs={{0,8},{1,9},{2,10},{3,11},{4,12},{5,13},{6,14},{7,15},{8,0},{9,1},... | collective-permute-start | bytes 3145736 | tf_op jit(solution)/shard_map/ppermute | solution.py:324
  168.5 1.4 copy-start.1
  168.5 8.1 %copy-start.30 = (s32[1,64,64]{2,1,0:T(8,128)S(1)}, s32[1,64,64]{2,1,0:T(8,128)}, u32[]{:S(2)}) copy-start(s32[1,64,64]{2,1,0:T(8,128)} %param.14) | copy-start | bytes 49156
  169.9 37.3 %all-to-all-start.3 = ((f32[64,64,128]{2,1,0:T(8,128)}), f32[64,64,128]{2,1,0:T(8,128)}, u32[]{:S(2)}, u32[]{:S(2)}) async-start(f32[64,64,128]{2,1,0:T(8,128)} %bitcast.13), calls=%async_computation.3 | async-start | bytes 4194304 | tf_op jit(solution)/shard_map/all_to_all | solution.py:316
  190.8 3.2 %copy-start.29 = (s32[1,64,64]{2,1,0:T(8,128)S(1)}, s32[1,64,64]{2,1,0:T(8,128)}, u32[]{:S(2)}) copy-start(s32[1,64,64]{2,1,0:T(8,128)} %param.13) | copy-start | bytes 49156
  190.8 3.3 %copy-start.32 = (s32[256]{0:T(256)S(1)}, s32[256]{0:T(256)}, u32[]{:S(2)}) copy-start(s32[256]{0:T(256)} %param.15) | copy-start | bytes 3076
  196.6 3.4 %copy-start.20 = (f32[72,128]{1,0:T(8,128)}, f32[72,128]{1,0:T(8,128)S(1)}, u32[]{:S(2)}) copy-start(f32[72,128]{1,0:T(8,128)S(1)} %get-tuple-element.32.sin_ref) | copy-start | bytes 110596
  196.6 3.4 %copy-start.22 = (f32[72,128]{1,0:T(8,128)}, f32[72,128]{1,0:T(8,128)S(1)}, u32[]{:S(2)}) copy-start(f32[72,128]{1,0:T(8,128)S(1)} %get-tuple-element.33.cos_ref) | copy-start | bytes 110596
  197.0 3.1 %copy-start.18 = (bf16[256,256]{1,0:T(8,128)(2,1)}, bf16[256,256]{1,0:T(8,128)(2,1)S(1)}, u32[]{:S(2)}) copy-start(bf16[256,256]{1,0:T(8,128)(2,1)S(1)} %get-tuple-element.25.bh_ref) | copy-start | bytes 393220
  197.8 2.3 copy-start.24
  199.8 1.6 copy-start.2
  210.4 5.3 %copy-start.4 = (f32[64,64,128]{2,1,0:T(8,128)S(1)}, f32[64,64,128]{2,1,0:T(8,128)}, u32[]{:S(2)}) copy-start(f32[64,64,128]{2,1,0:T(8,128)} %copy-done.3) | copy-start | bytes 6291460
  210.4 5.3 %copy-start.26 = (bf16[128,128]{1,0:T(8,128)(2,1)S(1)}, bf16[128,128]{1,0:T(8,128)(2,1)}, u32[]{:S(2)}) copy-start(bf16[128,128]{1,0:T(8,128)(2,1)} %get-tuple-element.26.refs_3_) | copy-start | bytes 98308
  210.4 5.3 %copy-start.27 = (bf16[128,128]{1,0:T(8,128)(2,1)S(1)}, bf16[128,128]{1,0:T(8,128)(2,1)}, u32[]{:S(2)}) copy-start(bf16[128,128]{1,0:T(8,128)(2,1)} %get-tuple-element.28.refs_2_) | copy-start | bytes 98308
  210.4 5.3 %copy-start.28 = (f32[8,1,512]{2,1,0:T(1,128)S(1)}, f32[8,1,512]{2,1,0:T(1,128)}, u32[]{:S(2)}) copy-start(f32[8,1,512]{2,1,0:T(1,128)} %convert_element_type.112.refs_5_) | copy-start | bytes 49156
  215.7 7.8 %copy-start.31 = (f32[16,1,16]{2,1,0:T(1,128)S(1)}, f32[16,1,16]{2,1,0:T(1,128)}, u32[]{:S(2)}) copy-start(f32[16,1,16]{2,1,0:T(1,128)} %reshape.185) | copy-start | bytes 3076
  (15 other events, 14.5 us)
where the time goes:
time: 244 us; the launch traced here: 243 us
  waiting for transfers between devices  107 us (44%)
  local copies, waits for them, and re-layouts  43.3 us (18%)
  Pallas kernels  34.6 us (14%)
  starting transfers between devices  28.6 us (12%)
  blocking collectives  18.4 us (8%)
  other arithmetic  9.9 us (4%)
    ppermute x2, waiting for transfers between devices, shards(): others.append(lax.ppermute(coeffs[c], 'det', opposite))  85.9 us
    unnamed x68, local copies, waits for them, and re-layouts  27.7 us
    all_to_all x4, starting transfers between devices, exchange(): lax.all_to_all(value, 'det', split_axis=0, concat_axis=0, axis_index_grou...  23.3 us
    all_to_all x4, waiting for transfers between devices, exchange(): lax.all_to_all(value, 'det', split_axis=0, concat_axis=0, axis_index_grou...  21 us
    all_to_all x1, blocking collectives, shards(): lax.all_to_all(parcel, 'det', split_axis=0, concat_axis=0, tiled=True)  18.4 us
    pallas_call x2, Pallas kernels, filter_units(): pl.pallas_call(functools.partial(filter_kernel, base, count), grid=(rows...  9.75 us
    pallas_call x1, Pallas kernels, finish(): pl.pallas_call(functools.partial(finish_kernel, side, tiles, len(units)),...  7.83 us
    pallas_call x2, Pallas kernels, corrected(): pl.pallas_call(functools.partial(correct_kernel, len(coeffs)), grid=(rows...  7.38 us
  transfers between devices with their start and end apart: 6, of which 3 were waited for; matrix products, arithmetic and copies ran while one was open for 12% of the time, Pallas kernels for 5%

commit v1 on v0

--- a/solution.py
+++ b/solution.py
@@ -284,8 +284,9 @@
     units = side // 2
     blocks = sky_rows.shape[0]
     half = size // 2
-    groups = [list(range(half)), list(range(half, size))]
-    opposite = [(i, (i + half) % size) for i in range(size)]
+    quarter = size // 4
+    groups = [list(range(half)), [*range(half + quarter, size), *range(half, half + quarter)]]
+    opposite = [*zip(groups[0], groups[1]), *zip(groups[1], groups[0])]
     mine = lax.axis_index("det") // half
 
     starts = [side * sum(PARTS[:c]) // sum(PARTS) for c in range(len(PARTS) + 1)]
@@ -297,7 +298,9 @@
     z = sections(timestream.reshape(dets, samples), scale, table, shares)
 
     def of_half(modes):
-        return lax.dynamic_index_in_dim(modes.reshape(2, half * dets, -1), mine, 0, keepdims=False)
+        modes = modes.reshape(4, quarter * dets, -1)
+        parts = [lax.dynamic_index_in_dim(modes, at, 0, keepdims=False) for at in (3 * mine, 1 + mine)]
+        return jnp.concatenate(parts, axis=0)
 
     weights = table_halves(of_half(mode_weights).T)
     pattern = table_halves(of_half(mode_pattern))
@@ -320,7 +323,6 @@
     for c in chunks:
         slabs.append(exchange(z[c]).reshape(half, shares[c] // half, dets, side))
         coeffs.append(coefficients(slabs[c], weights))
-        last[0] = coeffs[c]
         others.append(lax.ppermute(coeffs[c], "det", opposite))
     done = []
     for c in chunks:

time: 244 us -> 223 us (0.914)
  blocking collectives: 18.4 us -> 48.8 us
  waiting for transfers between devices: 107 us -> 86.1 us
  local copies, waits for them, and re-layouts: 43.3 us -> 27.7 us
  starting transfers between devices: 28.6 us -> 21.7 us
  Pallas kernels: 34.6 us -> 30.5 us
  other arithmetic: 9.9 us -> 6.38 us
    all_to_all x0 -> x1, blocking collectives: none -> 31.2 us  [exchange(): lax.all_to_all(value, 'det', split_axis=0, concat_axis=0, axis_index_grou...]
    all_to_all x4 -> x3, waiting for transfers between devices: 21 us -> 0.01 us  [exchange(): lax.all_to_all(value, 'det', split_axis=0, concat_axis=0, axis_index_grou...]
    unnamed x68 -> x25, local copies, waits for them, and re-layouts: 27.7 us -> 13.1 us
    all_to_all x4 -> x3, starting transfers between devices: 23.3 us -> 15.9 us  [exchange(): lax.all_to_all(value, 'det', split_axis=0, concat_axis=0, axis_index_grou...]
    pallas_call x2, Pallas kernels: 7.38 us -> 3.65 us  [corrected(): pl.pallas_call(functools.partial(correct_kernel, len(coeffs)), grid=(rows...]
    convert_element_type x4, other arithmetic: 4.18 us -> 0.78 us  [table_halves(): return (high.astype(BF16), (table - high).astype(BF16))]
  transfers between devices with their start and end apart: 6 -> 5, of which waited for: 3 -> 2; matrix products, arithmetic and copies ran while one was open for 12% -> 11% of each run, Pallas kernels for 5% -> 6%
where the time goes in v1:
time: 223 us; the launch traced here: 222 us
  waiting for transfers between devices  86.1 us (39%)
  blocking collectives  48.8 us (22%)
  Pallas kernels  30.5 us (14%)
  local copies, waits for them, and re-layouts  27.7 us (12%)
  starting transfers between devices  21.7 us (10%)
  other arithmetic  6.38 us (3%)
    ppermute x2, waiting for transfers between devices, shards(): others.append(lax.ppermute(coeffs[c], 'det', opposite))  86.1 us
    all_to_all x1, blocking collectives, exchange(): lax.all_to_all(value, 'det', split_axis=0, concat_axis=0, axis_index_grou...  31.2 us
    all_to_all x1, blocking collectives, shards(): lax.all_to_all(parcel, 'det', split_axis=0, concat_axis=0, tiled=True)  17.6 us
    all_to_all x3, starting transfers between devices, exchange(): lax.all_to_all(value, 'det', split_axis=0, concat_axis=0, axis_index_grou...  15.9 us
    unnamed x25, local copies, waits for them, and re-layouts  13.1 us
    pallas_call x2, Pallas kernels, filter_units(): pl.pallas_call(functools.partial(filter_kernel, base, count), grid=(rows...  10.9 us
    pallas_call x1, Pallas kernels, finish(): pl.pallas_call(functools.partial(finish_kernel, side, tiles, len(units)),...  7.82 us
    ppermute x2, starting transfers between devices, shards(): others.append(lax.ppermute(coeffs[c], 'det', opposite))  5.81 us
  transfers between devices with their start and end apart: 5, of which 2 were waited for; matrix products, arithmetic and copies ran while one was open for 11% of the time, Pallas kernels for 6%

profile of v1, /device:TPU:0, one launch (start us, length us, event | category | flops | bytes accessed | tf_op | source)
XLA Modules:
  0.0 222.1 jit_solution(13025569499211875150)
XLA Ops:
  2.7 2.2 copy-done.5
  4.9 4.4 %sections.1 = (f32[64,64,128]{2,1,0:T(8,128)S(1)}, f32[64,64,128]{2,1,0:T(8,128)S(1)}) custom-call(f32[64,16384]{1,0:T(8,128)S(1)} %bitcast.41, f32[64,128]{1,0:T(8,128)S(1)} %broadcast_in_dim.74.scale_ref, bf16[128,128]{1,0:T(8,128)(2,1)S(1)} %get-tuple-element.33.high_ref, bf16[128,128]{1,0:T(8,128)(2,1)S(1)} %get-tuple-element.31.low_ref), custom_call_target="tpu_custom_call" | custom-call | tf_op jit(solution)/shard_map/sections/pallas_call | solution.py:89
  9.3 31.2 %all_to_all.25 = f32[64,64,128]{2,1,0:T(8,128)} all-to-all(f32[64,64,128]{2,1,0:T(8,128)S(1)} %get-tuple-element.9), channel_id=1, replica_groups={{0,1,2,3,4,5,6,7},{12,13,14,15,8,9,10,11},{16,17,18,19,20,21,22,23},{28..., dimensions={0} | all-to-all | bytes 4194304 | tf_op jit(solution)/shard_map/all_to_all | solution.py:319
  40.5 3.6 %all-to-all-start.1 = ((f32[64,64,128]{2,1,0:T(8,128)}), f32[64,64,128]{2,1,0:T(8,128)S(1)}, u32[]{:S(2)}, u32[]{:S(2)}) async-start(f32[64,64,128]{2,1,0:T(8,128)} %copy-done.6), calls=%async_computation.1 | async-start | bytes 4194304 | tf_op jit(solution)/shard_map/all_to_all | solution.py:319
  45.6 1.7 copy-done
  47.2 1.9 coefficients.2.refs_0_
  49.1 3.1 %collective-permute-start = (f32[8,256,128]{2,1,0:T(8,128)S(1)}, f32[8,256,128]{2,1,0:T(8,128)S(1)}, u32[]{:S(2)}, u32[]{:S(2)}) collective-permute-start(f32[8,256,128]{2,1,0:T(8,128)S(1)} %coefficients.2.refs_0_), channel_id=1, source_target_pairs={{0,12},{1,13},{2,14},{3,15},{4,8},{5,9},{6,10},{7,11},{12,0},{13,1... | collective-permute-start | bytes 3145736 | tf_op jit(solution)/shard_map/ppermute | solution.py:326
  52.4 41.4 %collective-permute-done.refs_1_ = f32[8,256,128]{2,1,0:T(8,128)S(1)} collective-permute-done((f32[8,256,128]{2,1,0:T(8,128)S(1)}, f32[8,256,128]{2,1,0:T(8,128)S(1)}, u32[]{:S(2)}, u32[]{:S(2)}) %collective-permute-start) | collective-permute-done | bytes 1048608 | tf_op jit(solution)/shard_map/ppermute | solution.py:326
  93.7 1.8 corrected.2
  96.9 7.7 %all-to-all-start.2 = ((f32[64,64,128]{2,1,0:T(8,128)}), f32[64,64,128]{2,1,0:T(8,128)}, u32[]{:S(2)}, u32[]{:S(2)}) async-start(f32[64,64,128]{2,1,0:T(8,128)} %bitcast.40), calls=%async_computation.2 | async-start | bytes 4194304 | tf_op jit(solution)/shard_map/all_to_all | solution.py:319
  104.5 1.9 coefficients.3.refs_0_
  106.4 2.7 %collective-permute-start.1 = (f32[8,256,128]{2,1,0:T(8,128)S(1)}, f32[8,256,128]{2,1,0:T(8,128)S(1)}, u32[]{:S(2)}, u32[]{:S(2)}) collective-permute-start(f32[8,256,128]{2,1,0:T(8,128)S(1)} %coefficients.3.refs_0_), channel_id=1, source_target_pairs={{0,12},{1,13},{2,14},{3,15},{4,8},{5,9},{6,10},{7,11},{12,0},{13,1... | collective-permute-start | bytes 3145736 | tf_op jit(solution)/shard_map/ppermute | solution.py:326
  109.1 44.7 %collective-permute-done.1.refs_1_ = f32[8,256,128]{2,1,0:T(8,128)S(1)} collective-permute-done((f32[8,256,128]{2,1,0:T(8,128)S(1)}, f32[8,256,128]{2,1,0:T(8,128)S(1)}, u32[]{:S(2)}, u32[]{:S(2)}) %collective-permute-start.1) | collective-permute-done | bytes 1048608 | tf_op jit(solution)/shard_map/ppermute | solution.py:326
  153.8 1.8 corrected.3
  157.0 4.7 %all-to-all-start.3 = ((f32[64,64,128]{2,1,0:T(8,128)}), f32[64,64,128]{2,1,0:T(8,128)}, u32[]{:S(2)}, u32[]{:S(2)}) async-start(f32[64,64,128]{2,1,0:T(8,128)} %bitcast.39), calls=%async_computation.3 | async-start | bytes 4194304 | tf_op jit(solution)/shard_map/all_to_all | solution.py:319
  161.9 4.9 %copy.20 = f32[8,8,128,128]{3,2,1,0:T(8,128)} copy(f32[8,8,128,128]{3,1,2,0:T(8,128)} %bitcast.48) | data formatting | bytes 8388608
  166.8 5.4 %copy.17 = f32[64,128,128]{1,0,2:T(8,128)} copy(f32[64,128,128]{2,1,0:T(8,128)} %bitcast.47) | data formatting | bytes 8388608 | tf_op jit(solution)/shard_map/reshape | solution.py:307
  172.2 3.1 %slice.26 = f32[63,64,128]{2,1,0:T(8,128)} slice(f32[128,64,128]{2,1,0:T(8,128)} %bitcast.44), slice={[65:128], [0:64], [0:128]} | slice | bytes 4128768 | tf_op jit(solution)/shard_map/slice | solution.py:308
  175.4 3.2 %rev.3 = f32[63,64,128]{2,1,0:T(8,128)S(1)} reverse(f32[63,64,128]{2,1,0:T(8,128)} %slice.26), dimensions={0,2} | reverse | bytes 4128768 | tf_op jit(solution)/shard_map/rev | solution.py:308
  181.6 2.0 slice_add_fusion
  183.8 5.6 %filter_units.2.refs_0_ = f32[64,64,128]{2,1,0:T(8,128)S(1)} custom-call(f32[64,64,128]{2,1,0:T(8,128)} %all-to-all-done.2.z_ref, f32[64,64,128]{2,1,0:T(8,128)S(1)} %pad_maximum_fusion.w_ref, f32[64,128]{1,0:T(8,128)S(1)} %get-tuple-element.16.extra_ref, f32[72,128]{1,0:T(8,128)S(1)} %get-tuple-element.37.cos_ref, f32[72,128]{1,0:T(8,128)S(1)} %get-tuple-element.36.sin_ref, ...), custom_call_target="tpu_custom_call" | custom-call | flops 1610612736 | bytes 6291456 | tf_op jit(solution)/shard_map/filter_units/pallas_call | solution.py:211
  190.7 5.3 %filter_units.3.refs_1_ = f32[64,64,128]{2,1,0:T(8,128)S(1)} custom-call(f32[64,64,128]{2,1,0:T(8,128)} %all-to-all-done.3.z_ref, f32[64,64,128]{2,1,0:T(8,128)S(1)} %pad_maximum_fusion.w_ref, f32[64,128]{1,0:T(8,128)S(1)} %get-tuple-element.16.extra_ref, f32[72,128]{1,0:T(8,128)S(1)} %get-tuple-element.37.cos_ref, f32[72,128]{1,0:T(8,128)S(1)} %get-tuple-element.36.sin_ref, ...), custom_call_target="tpu_custom_call" | custom-call | flops 1610612736 | bytes 6291456 | tf_op jit(solution)/shard_map/filter_units/pallas_call | solution.py:211
  196.0 7.8 %finish.1 = (f32[64,16384]{1,0:T(8,128)}, f32[256,256]{1,0:T(8,128)S(1)}) custom-call(f32[64,64,128]{2,1,0:T(8,128)S(1)} %copy-done.4, f32[64,64,128]{2,1,0:T(8,128)S(1)} %filter_units.3.refs_1_, bf16[128,128]{1,0:T(8,128)(2,1)S(1)} %get-tuple-element.32.refs_2_, bf16[128,128]{1,0:T(8,128)(2,1)S(1)} %get-tuple-element.30.refs_3_, s32[8,1,512]{2,1,0:T(1,128)S(1)} %bitcast.43, ...), custom_call_target="tpu_custom_call" | custom-call | tf_op jit(solution)/shard_map/finish/pallas_call | solution.py:267
  203.8 17.6 %all_to_all.26 = f32[16,24,256]{2,1,0:T(8,128)S(1)} all-to-all(f32[16,24,256]{2,1,0:T(8,128)S(1)} %select_maximum_fusion), channel_id=1, replica_groups=mesh['grp'=2,'det'=16] {'det'}, dimensions={0} | all-to-all | bytes 786432 | tf_op jit(solution)/shard_map/all_to_all | solution.py:343
  (62 shorter events, 11.7 us)
Async XLA Ops:
  2.7 2.2 copy-start.5
  9.3 31.2 %copy-start.6 = (f32[64,64,128]{2,1,0:T(8,128)}, f32[64,64,128]{2,1,0:T(8,128)S(1)}, u32[]{:S(2)}) copy-start(f32[64,64,128]{2,1,0:T(8,128)S(1)} %get-tuple-element.11) | copy-start | bytes 6291460
  40.5 56.4 %all-to-all-start.1 = ((f32[64,64,128]{2,1,0:T(8,128)}), f32[64,64,128]{2,1,0:T(8,128)S(1)}, u32[]{:S(2)}, u32[]{:S(2)}) async-start(f32[64,64,128]{2,1,0:T(8,128)} %copy-done.6), calls=%async_computation.1 | async-start | bytes 4194304 | tf_op jit(solution)/shard_map/all_to_all | solution.py:319
  45.5 6.8 %copy-start.7 = (f32[1024,256]{1,0:T(8,128)S(1)}, f32[1024,256]{1,0:T(8,128)}, u32[]{:S(2)}) copy-start(f32[1024,256]{1,0:T(8,128)} %param.10) | copy-start | bytes 3145732
  45.6 1.7 copy-start
  49.1 44.6 %collective-permute-start = (f32[8,256,128]{2,1,0:T(8,128)S(1)}, f32[8,256,128]{2,1,0:T(8,128)S(1)}, u32[]{:S(2)}, u32[]{:S(2)}) collective-permute-start(f32[8,256,128]{2,1,0:T(8,128)S(1)} %coefficients.2.refs_0_), channel_id=1, source_target_pairs={{0,12},{1,13},{2,14},{3,15},{4,8},{5,9},{6,10},{7,11},{12,0},{13,1... | collective-permute-start | bytes 3145736 | tf_op jit(solution)/shard_map/ppermute | solution.py:326
  95.6 1.3 copy-start.2
  96.9 60.1 %all-to-all-start.2 = ((f32[64,64,128]{2,1,0:T(8,128)}), f32[64,64,128]{2,1,0:T(8,128)}, u32[]{:S(2)}, u32[]{:S(2)}) async-start(f32[64,64,128]{2,1,0:T(8,128)} %bitcast.40), calls=%async_computation.2 | async-start | bytes 4194304 | tf_op jit(solution)/shard_map/all_to_all | solution.py:319
  106.4 47.4 %collective-permute-start.1 = (f32[8,256,128]{2,1,0:T(8,128)S(1)}, f32[8,256,128]{2,1,0:T(8,128)S(1)}, u32[]{:S(2)}, u32[]{:S(2)}) collective-permute-start(f32[8,256,128]{2,1,0:T(8,128)S(1)} %coefficients.3.refs_0_), channel_id=1, source_target_pairs={{0,12},{1,13},{2,14},{3,15},{4,8},{5,9},{6,10},{7,11},{12,0},{13,1... | collective-permute-start | bytes 3145736 | tf_op jit(solution)/shard_map/ppermute | solution.py:326
  155.6 1.4 copy-start.1
  157.0 4.7 %copy-start.9 = (s32[1,64,64]{2,1,0:T(8,128)S(1)}, s32[1,64,64]{2,1,0:T(8,128)}, u32[]{:S(2)}) copy-start(s32[1,64,64]{2,1,0:T(8,128)} %param.14) | copy-start | bytes 49156
  157.0 33.6 %all-to-all-start.3 = ((f32[64,64,128]{2,1,0:T(8,128)}), f32[64,64,128]{2,1,0:T(8,128)}, u32[]{:S(2)}, u32[]{:S(2)}) async-start(f32[64,64,128]{2,1,0:T(8,128)} %bitcast.39), calls=%async_computation.3 | async-start | bytes 4194304 | tf_op jit(solution)/shard_map/all_to_all | solution.py:319
  175.3 3.2 %copy-start.8 = (s32[1,64,64]{2,1,0:T(8,128)S(1)}, s32[1,64,64]{2,1,0:T(8,128)}, u32[]{:S(2)}) copy-start(s32[1,64,64]{2,1,0:T(8,128)} %param.13) | copy-start | bytes 49156
  175.4 3.3 %copy-start.10 = (s32[256]{0:T(256)S(1)}, s32[256]{0:T(256)}, u32[]{:S(2)}) copy-start(s32[256]{0:T(256)} %param.15) | copy-start | bytes 3076
  189.3 1.3 copy-start.3
  190.7 5.3 %copy-start.4 = (f32[64,64,128]{2,1,0:T(8,128)S(1)}, f32[64,64,128]{2,1,0:T(8,128)}, u32[]{:S(2)}) copy-start(f32[64,64,128]{2,1,0:T(8,128)} %copy-done.3) | copy-start | bytes 6291460

commit v2 on v1

v2 whole, which is shorter than its diff:
```python
import functools
import math

import jax
import jax.numpy as jnp
from jax import lax
from jax.experimental import pallas as pl
from jax.experimental.pallas import tpu as pltpu
from jax.sharding import PartitionSpec as P


F32, BF16 = jnp.float32, jnp.bfloat16
ROWS = 8
UNITS = 8
LIMIT = pltpu.CompilerParams(vmem_limit_bytes=16 << 20)


def halves(value):
    high = value.astype(BF16)
    return high, (value - high.astype(F32)).astype(BF16)


def table_halves(table):
    high = lax.reduce_precision(table, exponent_bits=8, mantissa_bits=7)
    return high.astype(BF16), (table - high).astype(BF16)


def mm(a, b):
    return jnp.dot(a, b, preferred_element_type=F32)


def mm3(a_pair, b_pair):
    return mm(a_pair[0], b_pair[0]) + (mm(a_pair[1], b_pair[0]) + mm(a_pair[0], b_pair[1]))


def angles(count, first, second):
    return (first * second % count).astype(F32) * (2.0 * math.pi / count)


def section_table(side, unit_of_slot):
    unit = unit_of_slot[:, None, None]
    sample = lax.broadcasted_iota(jnp.int32, (1, 1, side), 2)
    part = lax.broadcasted_iota(jnp.int32, (1, 2, 1), 1)
    nyquist = (unit == 0) & (part == 1)
    angle = angles(side, jnp.where(nyquist, side // 2, unit), sample)
    table = jnp.where((part == 0) | nyquist, jnp.cos(angle), -jnp.sin(angle))
    return table.reshape(-1, side)


def inner_tables(side):
    first = lax.broadcasted_iota(jnp.int32, (side, side), 0)
    second = lax.broadcasted_iota(jnp.int32, (side, side), 1)
    angle = angles(side, first, second)
    cos, sin = jnp.cos(angle), jnp.sin(angle)
    forward = jnp.concatenate([jnp.concatenate([cos, -sin], 1), jnp.concatenate([sin, cos], 1)], 0)
    backward = jnp.concatenate([jnp.concatenate([cos, sin], 1), jnp.concatenate([-sin, cos], 1)], 0)
    return forward, backward


def twiddles(side):
    unit = lax.broadcasted_iota(jnp.int32, (side // 2 + 8, side), 0)
    sample = lax.broadcasted_iota(jnp.int32, (side // 2 + 8, side), 1)
    angle = angles(side * side, unit, sample)
    return jnp.cos(angle), jnp.sin(angle)


def section_kernel(side, x_ref, scale_ref, high_ref, low_ref, *refs):
    out_refs, (rows, turned) = refs[:-2], refs[-2:]
    scale = scale_ref[...]
    for n in range(side):
        rows[n * ROWS : (n + 1) * ROWS, :] = x_ref[:, n * side : (n + 1) * side] * scale
    table = (high_ref[...], low_ref[...])
    for d in range(0, ROWS, 2):
        pair = jnp.concatenate([rows[pl.ds(d, side, stride=ROWS), :], rows[pl.ds(d + 1, side, stride=ROWS), :]], axis=1)
        result = mm3(table, halves(pair))
        turned[pl.ds(d, len(result), stride=ROWS), :] = result[:, :side]
        turned[pl.ds(d + 1, len(result), stride=ROWS), :] = result[:, side:]
    lines = [(out_ref, row) for out_ref in out_refs for row in range(out_ref.shape[0])]
    for k, (out_ref, row) in enumerate(lines):
        out_ref[row] = turned[k * ROWS : (k + 1) * ROWS, :]


def sections(signal, scale, table, shares):
    dets, samples = signal.shape
    side = table.shape[1]
    high, low = table_halves(table)
    whole = pl.BlockSpec(table.shape, lambda i: (0, 0))
    return pl.pallas_call(
        functools.partial(section_kernel, side),
        grid=(dets // ROWS,),
        in_specs=[pl.BlockSpec((ROWS, samples), lambda i: (i, 0)), pl.BlockSpec((ROWS, side), lambda i: (i, 0)), whole, whole],
        out_specs=[pl.BlockSpec((share, ROWS, side), lambda i: (0, i, 0)) for share in shares],
        out_shape=[jax.ShapeDtypeStruct((share, dets, side), F32) for share in shares],
        scratch_shapes=[pltpu.VMEM((side * ROWS, side), F32), pltpu.VMEM((sum(shares) * ROWS, side), F32)],
        compiler_params=LIMIT,
        name="sections",
    )(signal, scale, high, low)


def cost(passes, rows, depth, columns, *arrays):
    moved = sum(array.size * array.dtype.itemsize for array in arrays)
    return pl.CostEstimate(flops=2 * passes * rows * depth * columns, bytes_accessed=moved, transcendentals=0)


def coeff_kernel(z_ref, high_ref, low_ref, out_ref, z_high, z_low):
    blocks, rows, dets, side = z_ref.shape
    for b in range(blocks):
        for k in range(rows):
            high, low = halves(z_ref[b, k])
            z_high[b * dets : (b + 1) * dets, k * side : (k + 1) * side] = high
            z_low[b * dets : (b + 1) * dets, k * side : (k + 1) * side] = low
    total = mm3((high_ref[...], low_ref[...]), (z_high[...], z_low[...]))
    for k in range(rows):
        out_ref[k] = total[:, k * side : (k + 1) * side]


def coefficients(slab, weights):
    blocks, rows, dets, side = slab.shape
    rank = weights[0].shape[0]
    out = jax.ShapeDtypeStruct((rows, rank, side), F32)
    step = math.gcd(2, rows)
    whole = pl.BlockSpec((rank, blocks * dets), lambda i: (0, 0))
    return pl.pallas_call(
        coeff_kernel,
        grid=(rows // step,),
        in_specs=[pl.BlockSpec((blocks, step, dets, side), lambda i: (0, i, 0, 0)), whole, whole],
        out_specs=pl.BlockSpec((step, rank, side), lambda i: (i, 0, 0)),
        out_shape=out,
        scratch_shapes=[pltpu.VMEM((blocks * dets, step * side), BF16)] * 2,
        compiler_params=LIMIT,
        cost_estimate=cost(3, rank, blocks * dets, rows * side, slab, out),
        name="coefficients",
    )(slab, *weights)


def correct_kernel(terms, z_ref, *refs):
    c_refs, (high_ref, low_ref, out_ref) = refs[:terms], refs[terms:]
    blocks, rows, dets, side = z_ref.shape
    coeff = halves(jnp.concatenate([sum(c_ref[k] for c_ref in c_refs) for k in range(rows)], axis=1))
    share = mm3((high_ref[...], low_ref[...]), coeff)
    for b in range(blocks):
        for k in range(rows):
            out_ref[b, k] = z_ref[b, k] - share[b * dets : (b + 1) * dets, k * side : (k + 1) * side]


def corrected(slab, coeffs, pattern):
    blocks, rows, dets, side = slab.shape
    rank = pattern[0].shape[1]
    step = math.gcd(2, rows)
    whole = pl.BlockSpec((blocks * dets, rank), lambda i: (0, 0))
    block = pl.BlockSpec((blocks, step, dets, side), lambda i: (0, i, 0, 0))
    return pl.pallas_call(
        functools.partial(correct_kernel, len(coeffs)),
        grid=(rows // step,),
        in_specs=[block] + [pl.BlockSpec((step, rank, side), lambda i: (i, 0, 0)) for _ in coeffs] + [whole, whole],
        out_specs=block,
        out_shape=jax.ShapeDtypeStruct(slab.shape, F32),
        compiler_params=LIMIT,
        cost_estimate=cost(3, rank, blocks * dets, rows * side, slab, slab, *coeffs),
        name="corrected",
    )(slab, *coeffs, *pattern)


def section_lines(group, section_ref, d, rows):
    pair = [group[pl.ds(d + e, rows, stride=ROWS), :] for e in (0, 1)]
    high, low = halves(jnp.concatenate(pair, axis=1))
    return mm(section_ref[...], jnp.concatenate([high, low, high], axis=0))


def synth_kernel(base, count, steps, z_ref, w_ref, extra_ref, turn_ref, tables_ref, section_ref, rows_ref, hits_ref, *refs):
    *ends, t_high, t_low, result, held, tile_high, tile_low, total_ref, one = refs
    ending = len(ends) == 4
    _, dets, side = z_ref.shape
    step = pl.program_id(0)

    @pl.when(step < steps)
    def _():
        first = base + step * count
        has_zero = base == 0

        def turn(unit):
            pair = turn_ref[pl.ds(unit, 1), :]
            return pair[:, :side], pair[:, side:]

        half_cos, half_sin = turn(side // 2)
        turns = [turn(first + i) for i in range(count)]
        table = lambda i: tables_ref[i * 2 * side : (i + 1) * 2 * side, :]

        def put(slot, real, imag):
            for part, value in ((0, real), (1, imag)):
                high, low = halves(value)
                t_high[slot * dets : (slot + 1) * dets, part * side : (part + 1) * side] = high
                t_low[slot * dets : (slot + 1) * dets, part * side : (part + 1) * side] = low

        def transform(high, low):
            middle = result.shape[0] // 2 // 16 * 16
            for at in (slice(0, middle), slice(middle, result.shape[0])):
                result[at] = mm3((t_high[at], t_low[at]), (table(high), table(low)))

        for i in range(count):
            real, imag = z_ref[2 * i], z_ref[2 * i + 1]
            if has_zero and i == 0:
                put(count, imag * half_cos, -imag * half_sin)
                imag = jnp.where(first == 0, 0.0, imag)
            cos, sin = turns[i]
            put(i, real * cos + imag * sin, imag * cos - real * sin)
        transform(0, 1)
        for i in range(count + has_zero):
            weight = extra_ref[...] if i == count else w_ref[i]
            at = slice(i * dets, (i + 1) * dets)
            put(i, result[at, :side] * weight, result[at, side:] * weight)
        transform(2, 3)
        for i in range(count):
            at = slice(i * dets, (i + 1) * dets)
            real, imag = result[at, :side], result[at, side:]
            cos, sin = turns[i]
            turned = imag * cos + real * sin
            if has_zero and i == 0:
                at = slice(count * dets, (count + 1) * dets)
                nyquist = result[at, :side] * half_cos - result[at, side:] * half_sin
                turned = jnp.where(first == 0, nyquist, turned)
            for part, value in ((0, real * cos - imag * sin), (1, turned)):
                row = pl.multiple_of((2 * (step * count + i) + part) * ROWS, ROWS)
                for group in range(dets // ROWS):
                    held[group, pl.ds(row, ROWS), :] = value[group * ROWS : (group + 1) * ROWS]

    @pl.when(step >= steps)
    def _():
        rows = 2 * count * steps
        tiles = tile_high.shape[0] // ROWS
        group = held.at[step - steps]
        lines_ref = one if ending else ends[0]
        for d in range(0, ROWS, 2):
            lines = section_lines(group, section_ref, d, rows)
            for e in (0, 1):
                at = (d + e) * side
                lines_ref[at : at + side, :] = lines[:, e * side : (e + 1) * side]
                for half in (0, 1):
                    high, low = halves(lines_ref[pl.ds(at + half, side // 2, stride=2), :])
                    into = slice((d + e) * tiles, (d + e + 1) * tiles)
                    tile_high[into, half * side : (half + 1) * side] = high
                    tile_low[into, half * side : (half + 1) * side] = low
        if ending:
            ends[2][0] = group[...]
        sums_ref = total_ref if ending else ends[1]
        ladder = lax.broadcasted_iota(jnp.int32, (sums_ref.shape[0], ROWS * tiles), 0)
        chosen = jnp.where(rows_ref[0] == ladder, hits_ref[0], 0.0).astype(BF16)
        total = mm(chosen, tile_high[...]) + mm(chosen, tile_low[...])
        before = ends[0][...] if ending else 0.0
        sums_ref[...] = total + jnp.where(step == steps, before, sums_ref[...])
        if ending:
            _, tail_ref, _, parcel_ref = ends

            @pl.when(step == pl.num_programs(0) - 1)
            def _():
                own = sums_ref.shape[0] // parcel_ref.shape[0]
                for owner in range(parcel_ref.shape[0]):
                    parcel_ref[owner, :own] = sums_ref[owner * own : (owner + 1) * own, :]
                    parcel_ref[owner, own:] = tail_ref[owner]


def stacked(section):
    high, low = table_halves(section)
    return jnp.concatenate([high, high, low], axis=1)


def synth(base, slab, weight, extra, turns, tables, section, rows, hits, blocks, ending=()):
    lines, dets, side = slab.shape
    tiles = rows.size // dets
    count = math.gcd(lines // 2, UNITS)
    steps, groups = lines // (2 * count), dets // ROWS
    room = (count + (base == 0)) * dets
    whole = lambda a: pl.BlockSpec(a.shape, lambda i: (0,) * a.ndim)
    later = lambda i: jnp.maximum(i - steps, 0)
    line = pl.BlockSpec((1, 1, ROWS * tiles), lambda i: (later(i), 0, 0))
    operands = [slab, weight, extra, turns, tables, section, rows.reshape(groups, 1, -1), hits.reshape(groups, 1, -1), *ending]
    in_specs = [
        pl.BlockSpec((2 * count, dets, side), lambda i: (jnp.minimum(i, steps - 1), 0, 0)),
        pl.BlockSpec((count, dets, side), lambda i: (base // count + jnp.minimum(i, steps - 1), 0, 0)),
        *[whole(a) for a in operands[2:6]],
        line,
        line,
        *[whole(a) for a in ending],
    ]
    if ending:
        _, tail = ending
        parcel = (tail.shape[0], blocks // tail.shape[0] + tail.shape[1], tail.shape[2])
        out = [jax.ShapeDtypeStruct((groups, lines * ROWS, side), F32), jax.ShapeDtypeStruct(parcel, F32)]
        out_specs = [pl.BlockSpec((1, lines * ROWS, side), lambda i: (later(i), 0, 0)), whole(out[1])]
    else:
        out = [jax.ShapeDtypeStruct((dets * side, side), F32), jax.ShapeDtypeStruct((blocks, 2 * side), F32)]
        out_specs = [pl.BlockSpec((ROWS * side, side), lambda i: (later(i), 0)), whole(out[1])]
    return pl.pallas_call(
        functools.partial(synth_kernel, base, count, steps),
        grid=(steps + groups,),
        in_specs=in_specs,
        out_specs=out_specs,
        out_shape=out,
        scratch_shapes=[
            *[pltpu.VMEM((room, 2 * side), BF16)] * 2,
            pltpu.VMEM((room, 2 * side), F32),
            pltpu.VMEM((groups, lines * ROWS, side), F32),
            *[pltpu.VMEM((ROWS * tiles, 2 * side), BF16)] * 2,
            pltpu.VMEM((blocks, 2 * side), F32),
            pltpu.VMEM((ROWS * side, side), F32),
        ],
        compiler_params=LIMIT,
        cost_estimate=cost(8, lines // 2 * dets, 2 * side, 2 * side, slab, slab, out[0]),
        name="synth",
    )(*operands)


def emit_kernel(before_ref, held_ref, section_ref, out_ref, lined):
    side = before_ref.shape[1]
    rows = held_ref.shape[1] // ROWS
    for d in range(0, ROWS, 2):
        lines = section_lines(held_ref.at[0], section_ref, d, rows)
        for e in (0, 1):
            at = (d + e) * side
            line = lines[:, e * side : (e + 1) * side] + before_ref[at : at + side, :]
            lined[pl.ds(d + e, side, stride=ROWS), :] = line
    for n in range(side):
        out_ref[:, n * side : (n + 1) * side] = lined[n * ROWS : (n + 1) * ROWS, :]


def emit(before, held, section):
    groups, lines, side = held.shape
    out = jax.ShapeDtypeStruct((groups * ROWS, side * side), F32)
    return pl.pallas_call(
        emit_kernel,
        grid=(groups,),
        in_specs=[
            pl.BlockSpec((ROWS * side, side), lambda i: (i, 0)),
            pl.BlockSpec((1, lines, side), lambda i: (i, 0, 0)),
            pl.BlockSpec(section.shape, lambda i: (0, 0)),
        ],
        out_specs=pl.BlockSpec((ROWS, side * side), lambda i: (i, 0)),
        out_shape=out,
        scratch_shapes=[pltpu.VMEM((ROWS * side, side), F32)],
        compiler_params=LIMIT,
        cost_estimate=cost(1, side, lines // ROWS, ROWS * groups * side, before, held, out),
        name="emit",
    )(before, held, section)


def shards(size, timestream, gains, mode_pattern, mode_weights, noise_weight, block_ids, hits, sky_rows):
    _, dets, samples = timestream.shape
    side = math.isqrt(samples)
    units = side // 2
    blocks = sky_rows.shape[0]
    half = size // 2
    quarter = size // 4
    groups = [list(range(half)), [*range(half + quarter, size), *range(half, half + quarter)]]
    opposite = [*zip(groups[0], groups[1]), *zip(groups[1], groups[0])]
    mine = lax.axis_index("det") // half

    scale = jnp.broadcast_to(1.0 / gains.reshape(dets, 1), (dets, side))
    table = section_table(side, lax.iota(jnp.int32, units))
    share = side // 2
    parts = [table[:share], table[share:]]
    stacks = [stacked(part.T / samples) for part in parts]
    z = []
    for part in parts:
        z += sections(timestream.reshape(dets, samples), scale, part, [share])

    def of_half(modes):
        modes = modes.reshape(4, quarter * dets, -1)
        parts = [lax.dynamic_index_in_dim(modes, at, 0, keepdims=False) for at in (3 * mine, 1 + mine)]
        return jnp.concatenate(parts, axis=0)

    weights = table_halves(of_half(mode_weights).T)
    pattern = table_halves(of_half(mode_pattern))
    w = jnp.transpose(noise_weight.reshape(dets, side, side), (2, 0, 1))
    mirror = w[:units:-1, :, ::-1]
    weight = jnp.concatenate([w[:1], w[1:units] + mirror], axis=0)
    extra = w[units]
    forward, backward = inner_tables(side)
    tables = jnp.concatenate([*table_halves(forward), *table_halves(backward)], axis=0)
    turns = jnp.concatenate(twiddles(side), axis=1)

    ids_flat = block_ids.reshape(-1)
    ladder = lax.broadcasted_iota(jnp.int32, (blocks, ids_flat.shape[0]), 0)
    rows = jnp.sum(jnp.where(ids_flat[None, :] == ladder, sky_rows[:, None], 0), axis=0)
    hit = hits.reshape(-1).astype(F32)
    counts = jnp.sum(jnp.where(rows[None, :] == ladder, hit[None, :], 0.0), axis=1)

    own = blocks // size
    tail = jnp.pad(counts.reshape(size, 1, own), ((0, 0), (0, ROWS - 1), (0, 2 * side - own)))

    last = [None]

    def exchange(value):
        if last[0] is not None:
            value, _ = lax.optimization_barrier((value, last[0]))
        last[0] = lax.all_to_all(value, "det", split_axis=0, concat_axis=0, axis_index_groups=groups, tiled=True)
        return last[0]

    slabs, coeffs, others = [], [], []
    for c in (0, 1):
        slabs.append(exchange(z[c]).reshape(half, share // half, dets, side))
        coeffs.append(coefficients(slabs[c], weights))
        others.append(lax.ppermute(coeffs[c], "det", opposite))
    for c in (0, 1):
        slab = corrected(slabs[c], [coeffs[c], others[c]], pattern)
        back = exchange(slab.reshape(share, dets, side))
        operands = [c * units // 2, back, weight, extra, turns, tables, stacks[c], rows, hit, blocks]
        if c == 0:
            lines, sums = synth(*operands)
        else:
            held, parcel = synth(*operands, ending=(sums, tail))

    parcel = lax.all_to_all(parcel, "det", split_axis=0, concat_axis=0, tiled=True)
    filtered = emit(lines, held, stacks[1])
    parcel = jnp.sum(parcel, axis=0)
    sky_map = parcel[:own] / jnp.sqrt(1.0 + parcel[own, :own])[:, None]
    return filtered.reshape(timestream.shape), sky_map


def solution(mesh):
    in_specs = (
        P("grp", "det", None),
        P("grp", "det"),
        P("grp", None),
        P("grp", None),
        P(("grp", "det"), None),
        P("grp", "det", None),
        P("grp", "det", None),
        P("grp"),
    )
    out_specs = (P("grp", "det", None), P(("grp", "det"), None))
    body = functools.partial(shards, mesh.shape["det"])

    return jax.shard_map(body, mesh=mesh, in_specs=in_specs, out_specs=out_specs, check_vma=False)
```

time: 223 us -> 232 us (1.040)
  blocking collectives: 48.8 us -> 0 us
  waiting for transfers between devices: 86.1 us -> 110 us
  local copies, waits for them, and re-layouts: 27.7 us -> 43.2 us
  starting transfers between devices: 21.7 us -> 32.7 us
  Pallas kernels: 30.5 us -> 36.1 us
    all_to_all x2 -> x0, blocking collectives: 48.8 us -> none  [the longest x1 31.2 us: exchange(): lax.all_to_all(value, 'det', split_axis=0, concat_axis=0, axis_index_grou...]
    all_to_all x3 -> x4, waiting for transfers between devices: 0.01 us -> 18.9 us  [exchange(): lax.all_to_all(value, 'det', split_axis=0, concat_axis=0, axis_index_grou...]
    unnamed x25 -> x41, local copies, waits for them, and re-layouts: 13.1 us -> 28 us
    all_to_all x0 -> x1, starting transfers between devices: none -> 5.46 us  [shards(): lax.all_to_all(parcel, 'det', split_axis=0, concat_axis=0, tiled=True)]
    all_to_all x0 -> x1, waiting for transfers between devices: none -> 5.38 us  [shards(): lax.all_to_all(parcel, 'det', split_axis=0, concat_axis=0, tiled=True)]
    all_to_all x3 -> x4, starting transfers between devices: 15.9 us -> 21.2 us  [exchange(): lax.all_to_all(value, 'det', split_axis=0, concat_axis=0, axis_index_grou...]
    pallas_call x3, Pallas kernels: 18.7 us -> 22.2 us  [the longest x2 17.6 us: synth(): pl.pallas_call(functools.partial(synth_kernel, base, count, steps), grid=...]
    pallas_call x1 -> x2, Pallas kernels: 4.38 us -> 6.49 us  [sections(): pl.pallas_call(functools.partial(section_kernel, side), grid=(dets // ROW...]
  transfers between devices with their start and end apart: 5 -> 7, of which waited for: 2 -> 4; matrix products, arithmetic and copies ran while one was open for 11% -> 11% of each run, Pallas kernels for 6% -> 11%
where the time goes in v2:
time: 232 us; the launch traced here: 231 us
  waiting for transfers between devices  110 us (47%)
  local copies, waits for them, and re-layouts  43.2 us (19%)
  Pallas kernels  36.1 us (16%)
  starting transfers between devices  32.7 us (14%)
  other arithmetic  7.52 us (3%)
    ppermute x2, waiting for transfers between devices, shards(): others.append(lax.ppermute(coeffs[c], 'det', opposite))  86.1 us
    unnamed x41, local copies, waits for them, and re-layouts  28 us
    all_to_all x4, starting transfers between devices, exchange(): lax.all_to_all(value, 'det', split_axis=0, concat_axis=0, axis_index_grou...  21.2 us
    all_to_all x4, waiting for transfers between devices, exchange(): lax.all_to_all(value, 'det', split_axis=0, concat_axis=0, axis_index_grou...  18.9 us
    pallas_call x2, Pallas kernels, synth(): pl.pallas_call(functools.partial(synth_kernel, base, count, steps), grid=...  17.6 us
    pallas_call x2, Pallas kernels, sections(): pl.pallas_call(functools.partial(section_kernel, side), grid=(dets // ROW...  6.49 us
    ppermute x2, starting transfers between devices, shards(): others.append(lax.ppermute(coeffs[c], 'det', opposite))  6.1 us
    all_to_all x1, starting transfers between devices, shards(): lax.all_to_all(parcel, 'det', split_axis=0, concat_axis=0, tiled=True)  5.46 us
  transfers between devices with their start and end apart: 7, of which 4 were waited for; matrix products, arithmetic and copies ran while one was open for 11% of the time, Pallas kernels for 11%

profile of v2, /device:TPU:0, one launch (start us, length us, event | category | flops | bytes accessed | tf_op | source)
XLA Modules:
  0.0 230.9 jit_solution(8828060839347142227)
XLA Ops:
  2.8 2.2 copy-done.2
  5.0 3.3 %sections.2 = f32[64,64,128]{2,1,0:T(8,128)S(1)} custom-call(f32[64,16384]{1,0:T(8,128)S(1)} %bitcast.42, f32[64,128]{1,0:T(8,128)S(1)} %broadcast_in_dim.74.scale_ref, bf16[64,128]{1,0:T(8,128)(2,1)S(1)} %get-tuple-element.39.high_ref, bf16[64,128]{1,0:T(8,128)(2,1)S(1)} %get-tuple-element.38.low_ref), custom_call_target="tpu_custom_call" | custom-call | tf_op jit(solution)/shard_map/sections/pallas_call | solution.py:88
  9.6 5.3 %all-to-all-start = ((f32[64,64,128]{2,1,0:T(8,128)}), f32[64,64,128]{2,1,0:T(8,128)S(1)}, u32[]{:S(2)}, u32[]{:S(2)}) async-start(f32[64,64,128]{2,1,0:T(8,128)} %copy-done.5), calls=%async_computation | async-start | bytes 4194304 | tf_op jit(solution)/shard_map/all_to_all | solution.py:395
  14.9 2.2 copy-done.3
  17.1 3.2 %sections.3 = f32[64,64,128]{2,1,0:T(8,128)S(1)} custom-call(f32[64,16384]{1,0:T(8,128)S(1)} %bitcast.43, f32[64,128]{1,0:T(8,128)S(1)} %broadcast_in_dim.74.scale_ref, bf16[64,128]{1,0:T(8,128)(2,1)S(1)} %get-tuple-element.37.high_ref, bf16[64,128]{1,0:T(8,128)(2,1)S(1)} %get-tuple-element.36.low_ref), custom_call_target="tpu_custom_call" | custom-call | tf_op jit(solution)/shard_map/sections/pallas_call | solution.py:88
  21.7 18.9 %all-to-all-done = f32[64,64,128]{2,1,0:T(8,128)S(1)} async-done(((f32[64,64,128]{2,1,0:T(8,128)}), f32[64,64,128]{2,1,0:T(8,128)S(1)}, u32[]{:S(2)}, u32[]{:S(2)}) %all-to-all-start) | async-done | bytes 2097184 | tf_op jit(solution)/shard_map/all_to_all | solution.py:395
  41.9 3.6 %all-to-all-start.1 = ((f32[64,64,128]{2,1,0:T(8,128)}), f32[64,64,128]{2,1,0:T(8,128)S(1)}, u32[]{:S(2)}, u32[]{:S(2)}) async-start(f32[64,64,128]{2,1,0:T(8,128)} %copy-done.4), calls=%async_computation.1 | async-start | bytes 4194304 | tf_op jit(solution)/shard_map/all_to_all | solution.py:395
  50.5 3.4 %collective-permute-start = (f32[8,256,128]{2,1,0:T(8,128)S(1)}, f32[8,256,128]{2,1,0:T(8,128)S(1)}, u32[]{:S(2)}, u32[]{:S(2)}) collective-permute-start(f32[8,256,128]{2,1,0:T(8,128)S(1)} %coefficients.2.refs_0_), channel_id=1, source_target_pairs={{0,12},{1,13},{2,14},{3,15},{4,8},{5,9},{6,10},{7,11},{12,0},{13,1... | collective-permute-start | bytes 3145736 | tf_op jit(solution)/shard_map/ppermute | solution.py:402
  54.0 41.4 %collective-permute-done.refs_1_ = f32[8,256,128]{2,1,0:T(8,128)S(1)} collective-permute-done((f32[8,256,128]{2,1,0:T(8,128)S(1)}, f32[8,256,128]{2,1,0:T(8,128)S(1)}, u32[]{:S(2)}, u32[]{:S(2)}) %collective-permute-start) | collective-permute-done | bytes 1048608 | tf_op jit(solution)/shard_map/ppermute | solution.py:402
  98.6 7.6 %all-to-all-start.2 = ((f32[64,64,128]{2,1,0:T(8,128)}), f32[64,64,128]{2,1,0:T(8,128)}, u32[]{:S(2)}, u32[]{:S(2)}) async-start(f32[64,64,128]{2,1,0:T(8,128)} %bitcast.45), calls=%async_computation.2 | async-start | bytes 4194304 | tf_op jit(solution)/shard_map/all_to_all | solution.py:395
  108.1 2.7 %collective-permute-start.1 = (f32[8,256,128]{2,1,0:T(8,128)S(1)}, f32[8,256,128]{2,1,0:T(8,128)S(1)}, u32[]{:S(2)}, u32[]{:S(2)}) collective-permute-start(f32[8,256,128]{2,1,0:T(8,128)S(1)} %coefficients.3.refs_0_), channel_id=1, source_target_pairs={{0,12},{1,13},{2,14},{3,15},{4,8},{5,9},{6,10},{7,11},{12,0},{13,1... | collective-permute-start | bytes 3145736 | tf_op jit(solution)/shard_map/ppermute | solution.py:402
  110.8 44.7 %collective-permute-done.1.refs_1_ = f32[8,256,128]{2,1,0:T(8,128)S(1)} collective-permute-done((f32[8,256,128]{2,1,0:T(8,128)S(1)}, f32[8,256,128]{2,1,0:T(8,128)S(1)}, u32[]{:S(2)}, u32[]{:S(2)}) %collective-permute-start.1) | collective-permute-done | bytes 1048608 | tf_op jit(solution)/shard_map/ppermute | solution.py:402
  158.7 4.7 %all-to-all-start.3 = ((f32[64,64,128]{2,1,0:T(8,128)}), f32[64,64,128]{2,1,0:T(8,128)S(1)}, u32[]{:S(2)}, u32[]{:S(2)}) async-start(f32[64,64,128]{2,1,0:T(8,128)} %bitcast.44), calls=%async_computation.3 | async-start | bytes 4194304 | tf_op jit(solution)/shard_map/all_to_all | solution.py:395
  163.7 4.9 %copy.35 = f32[8,8,128,128]{3,2,1,0:T(8,128)} copy(f32[8,8,128,128]{3,1,2,0:T(8,128)} %bitcast.52) | data formatting | bytes 8388608
  168.7 5.4 %copy.28 = f32[64,128,128]{1,0,2:T(8,128)} copy(f32[64,128,128]{2,1,0:T(8,128)} %bitcast.51) | data formatting | bytes 8388608 | tf_op jit(solution)/shard_map/reshape | solution.py:373
  174.1 3.1 %slice.60 = f32[63,64,128]{2,1,0:T(8,128)} slice(f32[128,64,128]{2,1,0:T(8,128)} %bitcast.48), slice={[65:128], [0:64], [0:128]} | slice | bytes 4128768 | tf_op jit(solution)/shard_map/slice | solution.py:374
  177.2 4.2 %rev.3 = f32[63,64,128]{2,1,0:T(8,128)} reverse(f32[63,64,128]{2,1,0:T(8,128)} %slice.60), dimensions={0,2} | reverse | bytes 4128768 | tf_op jit(solution)/shard_map/rev | solution.py:374
  187.0 9.2 %synth.2 = (f32[8192,128]{1,0:T(8,128)S(1)}, f32[256,256]{1,0:T(8,128)S(1)}) custom-call(f32[64,64,128]{2,1,0:T(8,128)} %all-to-all-done.2.z_ref, f32[64,64,128]{2,1,0:T(8,128)S(1)} %pad_maximum_fusion.w_ref, f32[64,128]{1,0:T(8,128)S(1)} %get-tuple-element.16.extra_ref, f32[72,256]{1,0:T(8,128)S(1)} %pad_maximum_fusion.7.turn_ref, ...), custom_call_target="tpu_custom_call" | custom-call | flops 2147483648 | bytes 8388608 | tf_op jit(solution)/shard_map/synth/pallas_call | solution.py:293
  196.3 2.0 copy-done.8
  204.2 8.3 %synth.3 = (f32[8,512,128]{2,1,0:T(8,128)S(1)}, f32[16,24,256]{2,1,0:T(8,128)}) custom-call(f32[64,64,128]{2,1,0:T(8,128)S(1)} %copy-done.11, f32[64,64,128]{2,1,0:T(8,128)S(1)} %copy-done.13, f32[64,128]{1,0:T(8,128)S(1)} %get-tuple-element.16.extra_ref, f32[72,256]{1,0:T(8,128)S(1)} %pad_maximum_fusion.7.turn_ref, ...), custom_call_target="tpu_custom_call" | custom-call | flops 2147483648 | bytes 6291456 | tf_op jit(solution)/shard_map/synth/pallas_call | solution.py:293
  212.5 5.5 %all-to-all-start.4 = ((f32[16,24,256]{2,1,0:T(8,128)}), f32[16,24,256]{2,1,0:T(8,128)S(1)}, u32[]{:S(2)}, u32[]{:S(2)}) async-start(f32[16,24,256]{2,1,0:T(8,128)} %get-tuple-element.15), calls=%async_computation.4 | async-start | bytes 786432 | tf_op jit(solution)/shard_map/all_to_all | solution.py:412
  218.0 2.2 copy-done.9
  220.2 4.6 %emit.1 = f32[64,16384]{1,0:T(8,128)} custom-call(f32[8192,128]{1,0:T(8,128)S(1)} %copy-done.9, f32[8,512,128]{2,1,0:T(8,128)S(1)} %get-tuple-element.14.held_ref, bf16[128,192]{1,0:T(8,128)(2,1)S(1)} %pad_maximum_fusion.9.section_ref), custom_call_target="tpu_custom_call" | custom-call | flops 134217728 | bytes 10485760 | tf_op jit(solution)/shard_map/emit/pallas_call | solution.py:329
  224.8 5.4 %all-to-all-done.4 = f32[16,24,256]{2,1,0:T(8,128)S(1)} async-done(((f32[16,24,256]{2,1,0:T(8,128)}), f32[16,24,256]{2,1,0:T(8,128)S(1)}, u32[]{:S(2)}, u32[]{:S(2)}) %all-to-all-start.4) | async-done | bytes 393248 | tf_op jit(solution)/shard_map/all_to_all | solution.py:412
  (83 shorter events, 31.9 us)
Async XLA Ops:
  2.8 2.2 copy-start.2
  8.3 1.3 copy-start.5
  9.6 31.0 %all-to-all-start = ((f32[64,64,128]{2,1,0:T(8,128)}), f32[64,64,128]{2,1,0:T(8,128)S(1)}, u32[]{:S(2)}, u32[]{:S(2)}) async-start(f32[64,64,128]{2,1,0:T(8,128)} %copy-done.5), calls=%async_computation | async-start | bytes 4194304 | tf_op jit(solution)/shard_map/all_to_all | solution.py:395
  14.9 2.2 copy-start.3
  20.3 1.4 copy-start.4
  41.9 56.6 %all-to-all-start.1 = ((f32[64,64,128]{2,1,0:T(8,128)}), f32[64,64,128]{2,1,0:T(8,128)S(1)}, u32[]{:S(2)}, u32[]{:S(2)}) async-start(f32[64,64,128]{2,1,0:T(8,128)} %copy-done.4), calls=%async_computation.1 | async-start | bytes 4194304 | tf_op jit(solution)/shard_map/all_to_all | solution.py:395
  46.9 7.0 %copy-start.15 = (f32[1024,256]{1,0:T(8,128)S(1)}, f32[1024,256]{1,0:T(8,128)}, u32[]{:S(2)}) copy-start(f32[1024,256]{1,0:T(8,128)} %param.10) | copy-start | bytes 3145732
  47.0 1.7 copy-start.1
  50.5 44.9 %collective-permute-start = (f32[8,256,128]{2,1,0:T(8,128)S(1)}, f32[8,256,128]{2,1,0:T(8,128)S(1)}, u32[]{:S(2)}, u32[]{:S(2)}) collective-permute-start(f32[8,256,128]{2,1,0:T(8,128)S(1)} %coefficients.2.refs_0_), channel_id=1, source_target_pairs={{0,12},{1,13},{2,14},{3,15},{4,8},{5,9},{6,10},{7,11},{12,0},{13,1... | collective-permute-start | bytes 3145736 | tf_op jit(solution)/shard_map/ppermute | solution.py:402
  98.6 60.1 %all-to-all-start.2 = ((f32[64,64,128]{2,1,0:T(8,128)}), f32[64,64,128]{2,1,0:T(8,128)}, u32[]{:S(2)}, u32[]{:S(2)}) async-start(f32[64,64,128]{2,1,0:T(8,128)} %bitcast.45), calls=%async_computation.2 | async-start | bytes 4194304 | tf_op jit(solution)/shard_map/all_to_all | solution.py:395
  108.1 47.4 %collective-permute-start.1 = (f32[8,256,128]{2,1,0:T(8,128)S(1)}, f32[8,256,128]{2,1,0:T(8,128)S(1)}, u32[]{:S(2)}, u32[]{:S(2)}) collective-permute-start(f32[8,256,128]{2,1,0:T(8,128)S(1)} %coefficients.3.refs_0_), channel_id=1, source_target_pairs={{0,12},{1,13},{2,14},{3,15},{4,8},{5,9},{6,10},{7,11},{12,0},{13,1... | collective-permute-start | bytes 3145736 | tf_op jit(solution)/shard_map/ppermute | solution.py:402
  157.3 1.4 copy-start.6
  158.7 4.9 %copy-start.17 = (s32[1,64,64]{2,1,0:T(8,128)S(1)}, s32[1,64,64]{2,1,0:T(8,128)}, u32[]{:S(2)}) copy-start(s32[1,64,64]{2,1,0:T(8,128)} %param.14) | copy-start | bytes 49156
  158.7 40.9 %all-to-all-start.3 = ((f32[64,64,128]{2,1,0:T(8,128)}), f32[64,64,128]{2,1,0:T(8,128)S(1)}, u32[]{:S(2)}, u32[]{:S(2)}) async-start(f32[64,64,128]{2,1,0:T(8,128)} %bitcast.44), calls=%async_computation.3 | async-start | bytes 4194304 | tf_op jit(solution)/shard_map/all_to_all | solution.py:395
  177.2 4.2 %copy-start.16 = (s32[1,64,64]{2,1,0:T(8,128)S(1)}, s32[1,64,64]{2,1,0:T(8,128)}, u32[]{:S(2)}) copy-start(s32[1,64,64]{2,1,0:T(8,128)} %param.13) | copy-start | bytes 49156
  177.2 4.2 %copy-start.18 = (s32[256]{0:T(256)S(1)}, s32[256]{0:T(256)}, u32[]{:S(2)}) copy-start(s32[256]{0:T(256)} %param.15) | copy-start | bytes 3076
  182.9 1.9 copy-start.14
  196.3 2.0 copy-start.8
  198.3 1.4 copy-start.12
  199.6 1.3 copy-start.10
  201.0 1.6 copy-start.11
  202.6 1.6 copy-start.13
  212.5 17.6 %all-to-all-start.4 = ((f32[16,24,256]{2,1,0:T(8,128)}), f32[16,24,256]{2,1,0:T(8,128)S(1)}, u32[]{:S(2)}, u32[]{:S(2)}) async-start(f32[16,24,256]{2,1,0:T(8,128)} %get-tuple-element.15), calls=%async_computation.4 | async-start | bytes 786432 | tf_op jit(solution)/shard_map/all_to_all | solution.py:412
  218.0 2.2 copy-start.9
  (2 other events, 2.6 us)

commit v3 on v2

--- a/solution.py
+++ b/solution.py
@@ -158,7 +158,7 @@
         compiler_params=LIMIT,
         cost_estimate=cost(3, rank, blocks * dets, rows * side, slab, slab, *coeffs),
         name="corrected",
-    )(slab, *coeffs, *pattern)
+    )(pltpu.with_memory_space_constraint(slab, pltpu.HBM), *coeffs, *pattern)
 
 
 def section_lines(group, section_ref, d, rows):
@@ -273,6 +273,7 @@
     whole = lambda a: pl.BlockSpec(a.shape, lambda i: (0,) * a.ndim)
     later = lambda i: jnp.maximum(i - steps, 0)
     line = pl.BlockSpec((1, 1, ROWS * tiles), lambda i: (later(i), 0, 0))
+    slab, weight = [pltpu.with_memory_space_constraint(a, pltpu.HBM) for a in (slab, weight)]
     operands = [slab, weight, extra, turns, tables, section, rows.reshape(groups, 1, -1), hits.reshape(groups, 1, -1), *ending]
     in_specs = [
         pl.BlockSpec((2 * count, dets, side), lambda i: (jnp.minimum(i, steps - 1), 0, 0)),
@@ -340,7 +341,7 @@
         compiler_params=LIMIT,
         cost_estimate=cost(1, side, lines // ROWS, ROWS * groups * side, before, held, out),
         name="emit",
-    )(before, held, section)
+    )(pltpu.with_memory_space_constraint(before, pltpu.HBM), held, section)
 
 
 def shards(size, timestream, gains, mode_pattern, mode_weights, noise_weight, block_ids, hits, sky_rows):

time: 232 us -> 231 us (level)
  local copies, waits for them, and re-layouts: 43.2 us -> 32.7 us
  Pallas kernels: 36.1 us -> 45.1 us
    unnamed x41 -> x29, local copies, waits for them, and re-layouts: 28 us -> 18.5 us
    pallas_call x2, Pallas kernels: 3.66 us -> 7.92 us  [corrected(): pl.pallas_call(functools.partial(correct_kernel, len(coeffs)), grid=(rows...]
    pallas_call x1, Pallas kernels: 4.59 us -> 7.45 us  [emit(): pl.pallas_call(emit_kernel, grid=(groups,), in_specs=[pl.BlockSpec((ROWS...]
  transfers between devices with their start and end apart: 7 -> 7, of which waited for: 4 -> 4; matrix products, arithmetic and copies ran while one was open for 11% -> 11% of each run, Pallas kernels for 11% -> 14%
where the time goes in v3:
time: 231 us; the launch traced here: 230 us
  waiting for transfers between devices  110 us (48%)
  Pallas kernels  45.1 us (20%)
  starting transfers between devices  32.9 us (14%)
  local copies, waits for them, and re-layouts  32.7 us (14%)
  other arithmetic  8.75 us (4%)
    ppermute x2, waiting for transfers between devices, shards(): others.append(lax.ppermute(coeffs[c], 'det', opposite))  86 us
    all_to_all x4, starting transfers between devices, exchange(): lax.all_to_all(value, 'det', split_axis=0, concat_axis=0, axis_index_grou...  21.2 us
    pallas_call x2, Pallas kernels, synth(): pl.pallas_call(functools.partial(synth_kernel, base, count, steps), grid=...  19.5 us
    all_to_all x4, waiting for transfers between devices, exchange(): lax.all_to_all(value, 'det', split_axis=0, concat_axis=0, axis_index_grou...  18.9 us
    unnamed x29, local copies, waits for them, and re-layouts  18.5 us
    pallas_call x2, Pallas kernels, corrected(): pl.pallas_call(functools.partial(correct_kernel, len(coeffs)), grid=(rows...  7.92 us
    pallas_call x1, Pallas kernels, emit(): pl.pallas_call(emit_kernel, grid=(groups,), in_specs=[pl.BlockSpec((ROWS...  7.45 us
    pallas_call x2, Pallas kernels, sections(): pl.pallas_call(functools.partial(section_kernel, side), grid=(dets // ROW...  6.49 us
  transfers between devices with their start and end apart: 7, of which 4 were waited for; matrix products, arithmetic and copies ran while one was open for 11% of the time, Pallas kernels for 14%

profile of v3, /device:TPU:0, one launch (start us, length us, event | category | flops | bytes accessed | tf_op | source)
XLA Modules:
  0.0 230.0 jit_solution(5584627985513845024)
XLA Ops:
  2.8 2.2 copy-done.3
  5.0 3.3 %sections.2 = f32[64,64,128]{2,1,0:T(8,128)S(1)} custom-call(f32[64,16384]{1,0:T(8,128)S(1)} %bitcast.42, f32[64,128]{1,0:T(8,128)S(1)} %broadcast_in_dim.74.scale_ref, bf16[64,128]{1,0:T(8,128)(2,1)S(1)} %get-tuple-element.39.high_ref, bf16[64,128]{1,0:T(8,128)(2,1)S(1)} %get-tuple-element.38.low_ref), custom_call_target="tpu_custom_call" | custom-call | tf_op jit(solution)/shard_map/sections/pallas_call | solution.py:88
  9.6 5.3 %all-to-all-start = ((f32[64,64,128]{2,1,0:T(8,128)}), f32[64,64,128]{2,1,0:T(8,128)S(1)}, u32[]{:S(2)}, u32[]{:S(2)}) async-start(f32[64,64,128]{2,1,0:T(8,128)} %copy-done.6), calls=%async_computation | async-start | bytes 4194304 | tf_op jit(solution)/shard_map/all_to_all | solution.py:396
  14.9 2.2 copy-done.4
  17.1 3.2 %sections.3 = f32[64,64,128]{2,1,0:T(8,128)S(1)} custom-call(f32[64,16384]{1,0:T(8,128)S(1)} %bitcast.43, f32[64,128]{1,0:T(8,128)S(1)} %broadcast_in_dim.74.scale_ref, bf16[64,128]{1,0:T(8,128)(2,1)S(1)} %get-tuple-element.37.high_ref, bf16[64,128]{1,0:T(8,128)(2,1)S(1)} %get-tuple-element.36.low_ref), custom_call_target="tpu_custom_call" | custom-call | tf_op jit(solution)/shard_map/sections/pallas_call | solution.py:88
  21.7 18.9 %all-to-all-done = f32[64,64,128]{2,1,0:T(8,128)S(1)} async-done(((f32[64,64,128]{2,1,0:T(8,128)}), f32[64,64,128]{2,1,0:T(8,128)S(1)}, u32[]{:S(2)}, u32[]{:S(2)}) %all-to-all-start) | async-done | bytes 2097184 | tf_op jit(solution)/shard_map/all_to_all | solution.py:396
  41.9 3.6 %all-to-all-start.1 = ((f32[64,64,128]{2,1,0:T(8,128)}), f32[64,64,128]{2,1,0:T(8,128)S(1)}, u32[]{:S(2)}, u32[]{:S(2)}) async-start(f32[64,64,128]{2,1,0:T(8,128)} %copy-done.5), calls=%async_computation.1 | async-start | bytes 4194304 | tf_op jit(solution)/shard_map/all_to_all | solution.py:396
  50.5 3.4 %collective-permute-start = (f32[8,256,128]{2,1,0:T(8,128)S(1)}, f32[8,256,128]{2,1,0:T(8,128)S(1)}, u32[]{:S(2)}, u32[]{:S(2)}) collective-permute-start(f32[8,256,128]{2,1,0:T(8,128)S(1)} %coefficients.2.refs_0_), channel_id=1, source_target_pairs={{0,12},{1,13},{2,14},{3,15},{4,8},{5,9},{6,10},{7,11},{12,0},{13,1... | collective-permute-start | bytes 3145736 | tf_op jit(solution)/shard_map/ppermute | solution.py:403
  54.0 41.4 %collective-permute-done.refs_1_ = f32[8,256,128]{2,1,0:T(8,128)S(1)} collective-permute-done((f32[8,256,128]{2,1,0:T(8,128)S(1)}, f32[8,256,128]{2,1,0:T(8,128)S(1)}, u32[]{:S(2)}, u32[]{:S(2)}) %collective-permute-start) | collective-permute-done | bytes 1048608 | tf_op jit(solution)/shard_map/ppermute | solution.py:403
  95.4 3.4 %corrected.2 = f32[8,8,64,128]{3,2,1,0:T(8,128)S(1)} custom-call(f32[8,8,64,128]{3,2,1,0:T(8,128)} %bitcast.40, f32[8,256,128]{2,1,0:T(8,128)S(1)} %coefficients.2.refs_0_, f32[8,256,128]{2,1,0:T(8,128)S(1)} %collective-permute-done.refs_1_, bf16[512,256]{1,0:T(8,128)(2,1)S(1)} %get-tuple-element.23.refs_2_, bf16[512,256]{1,0:T(8,128)(2,1)S(1)} %get-tuple-element.22.refs_3_), custom_call_target="tpu_custom_call" | custom-call | flops 805306368 | bytes 6291456 | tf_op jit(solution)/shard_map/corrected/pallas_call | solution.py:152
  100.1 7.6 %all-to-all-start.2 = ((f32[64,64,128]{2,1,0:T(8,128)}), f32[64,64,128]{2,1,0:T(8,128)}, u32[]{:S(2)}, u32[]{:S(2)}) async-start(f32[64,64,128]{2,1,0:T(8,128)} %bitcast.44), calls=%async_computation.2 | async-start | bytes 4194304 | tf_op jit(solution)/shard_map/all_to_all | solution.py:396
  109.6 2.7 %collective-permute-start.1 = (f32[8,256,128]{2,1,0:T(8,128)S(1)}, f32[8,256,128]{2,1,0:T(8,128)S(1)}, u32[]{:S(2)}, u32[]{:S(2)}) collective-permute-start(f32[8,256,128]{2,1,0:T(8,128)S(1)} %coefficients.3.refs_0_), channel_id=1, source_target_pairs={{0,12},{1,13},{2,14},{3,15},{4,8},{5,9},{6,10},{7,11},{12,0},{13,1... | collective-permute-start | bytes 3145736 | tf_op jit(solution)/shard_map/ppermute | solution.py:403
  112.4 44.7 %collective-permute-done.1.refs_1_ = f32[8,256,128]{2,1,0:T(8,128)S(1)} collective-permute-done((f32[8,256,128]{2,1,0:T(8,128)S(1)}, f32[8,256,128]{2,1,0:T(8,128)S(1)}, u32[]{:S(2)}, u32[]{:S(2)}) %collective-permute-start.1) | collective-permute-done | bytes 1048608 | tf_op jit(solution)/shard_map/ppermute | solution.py:403
  157.0 4.5 %corrected.3 = f32[8,8,64,128]{3,2,1,0:T(8,128)} custom-call(f32[8,8,64,128]{3,2,1,0:T(8,128)} %bitcast.39, f32[8,256,128]{2,1,0:T(8,128)S(1)} %coefficients.3.refs_0_, f32[8,256,128]{2,1,0:T(8,128)S(1)} %collective-permute-done.1.refs_1_, bf16[512,256]{1,0:T(8,128)(2,1)S(1)} %get-tuple-element.23.refs_2_, bf16[512,256]{1,0:T(8,128)(2,1)S(1)} %get-tuple-element.22.refs_3_), custom_call_target="tpu_custom_call" | custom-call | flops 805306368 | bytes 6291456 | tf_op jit(solution)/shard_map/corrected/pallas_call | solution.py:152
  161.6 4.6 %all-to-all-start.3 = ((f32[64,64,128]{2,1,0:T(8,128)}), f32[64,64,128]{2,1,0:T(8,128)}, u32[]{:S(2)}, u32[]{:S(2)}) async-start(f32[64,64,128]{2,1,0:T(8,128)} %bitcast.18), calls=%async_computation.3 | async-start | bytes 4194304 | tf_op jit(solution)/shard_map/all_to_all | solution.py:396
  166.6 4.9 %copy.35 = f32[8,8,128,128]{3,2,1,0:T(8,128)} copy(f32[8,8,128,128]{3,1,2,0:T(8,128)} %bitcast.51) | data formatting | bytes 8388608
  171.6 5.4 %copy.28 = f32[64,128,128]{1,0,2:T(8,128)} copy(f32[64,128,128]{2,1,0:T(8,128)} %bitcast.50) | data formatting | bytes 8388608 | tf_op jit(solution)/shard_map/reshape | solution.py:374
  176.9 3.1 %slice.60 = f32[63,64,128]{2,1,0:T(8,128)} slice(f32[128,64,128]{2,1,0:T(8,128)} %bitcast.47), slice={[65:128], [0:64], [0:128]} | slice | bytes 4128768 | tf_op jit(solution)/shard_map/slice | solution.py:375
  180.1 3.2 %rev.3 = f32[63,64,128]{2,1,0:T(8,128)S(1)} reverse(f32[63,64,128]{2,1,0:T(8,128)} %slice.60), dimensions={0,2} | reverse | bytes 4128768 | tf_op jit(solution)/shard_map/rev | solution.py:375
  190.1 9.4 %synth.2 = (f32[8192,128]{1,0:T(8,128)S(1)}, f32[256,256]{1,0:T(8,128)S(1)}) custom-call(f32[64,64,128]{2,1,0:T(8,128)} %all-to-all-done.2.z_ref, f32[64,64,128]{2,1,0:T(8,128)} %pad_maximum_fusion.w_ref, f32[64,128]{1,0:T(8,128)S(1)} %get-tuple-element.16.extra_ref, f32[72,256]{1,0:T(8,128)S(1)} %pad_maximum_fusion.7.turn_ref, ...), custom_call_target="tpu_custom_call" | custom-call | flops 2147483648 | bytes 8388608 | tf_op jit(solution)/shard_map/synth/pallas_call | solution.py:294
  201.5 10.0 %synth.3 = (f32[8,512,128]{2,1,0:T(8,128)S(1)}, f32[16,24,256]{2,1,0:T(8,128)}) custom-call(f32[64,64,128]{2,1,0:T(8,128)} %all-to-all-done.3.z_ref, f32[64,64,128]{2,1,0:T(8,128)} %pad_maximum_fusion.w_ref, f32[64,128]{1,0:T(8,128)S(1)} %get-tuple-element.16.extra_ref, f32[72,256]{1,0:T(8,128)S(1)} %pad_maximum_fusion.7.turn_ref, ...), custom_call_target="tpu_custom_call" | custom-call | flops 2147483648 | bytes 6291456 | tf_op jit(solution)/shard_map/synth/pallas_call | solution.py:294
  211.5 5.6 %all-to-all-start.4 = ((f32[16,24,256]{2,1,0:T(8,128)}), f32[16,24,256]{2,1,0:T(8,128)S(1)}, u32[]{:S(2)}, u32[]{:S(2)}) async-start(f32[16,24,256]{2,1,0:T(8,128)} %get-tuple-element.15), calls=%async_computation.4 | async-start | bytes 786432 | tf_op jit(solution)/shard_map/all_to_all | solution.py:413
  217.1 7.5 %emit.1 = f32[64,16384]{1,0:T(8,128)} custom-call(f32[8192,128]{1,0:T(8,128)} %copy-done.8, f32[8,512,128]{2,1,0:T(8,128)S(1)} %get-tuple-element.14.held_ref, bf16[128,192]{1,0:T(8,128)(2,1)S(1)} %pad_maximum_fusion.9.section_ref), custom_call_target="tpu_custom_call" | custom-call | flops 134217728 | bytes 10485760 | tf_op jit(solution)/shard_map/emit/pallas_call | solution.py:330
  224.6 4.7 %all-to-all-done.4 = f32[16,24,256]{2,1,0:T(8,128)S(1)} async-done(((f32[16,24,256]{2,1,0:T(8,128)}), f32[16,24,256]{2,1,0:T(8,128)S(1)}, u32[]{:S(2)}, u32[]{:S(2)}) %all-to-all-start.4) | async-done | bytes 393248 | tf_op jit(solution)/shard_map/all_to_all | solution.py:413
  (71 shorter events, 24.2 us)
Async XLA Ops:
  2.8 2.2 copy-start.3
  8.3 1.3 copy-start.6
  9.6 31.0 %all-to-all-start = ((f32[64,64,128]{2,1,0:T(8,128)}), f32[64,64,128]{2,1,0:T(8,128)S(1)}, u32[]{:S(2)}, u32[]{:S(2)}) async-start(f32[64,64,128]{2,1,0:T(8,128)} %copy-done.6), calls=%async_computation | async-start | bytes 4194304 | tf_op jit(solution)/shard_map/all_to_all | solution.py:396
  14.9 2.2 copy-start.4
  20.3 1.4 copy-start.5
  40.6 1.3 copy-start.1
  41.9 58.2 %all-to-all-start.1 = ((f32[64,64,128]{2,1,0:T(8,128)}), f32[64,64,128]{2,1,0:T(8,128)S(1)}, u32[]{:S(2)}, u32[]{:S(2)}) async-start(f32[64,64,128]{2,1,0:T(8,128)} %copy-done.5), calls=%async_computation.1 | async-start | bytes 4194304 | tf_op jit(solution)/shard_map/all_to_all | solution.py:396
  46.9 7.0 %copy-start.9 = (f32[1024,256]{1,0:T(8,128)S(1)}, f32[1024,256]{1,0:T(8,128)}, u32[]{:S(2)}) copy-start(f32[1024,256]{1,0:T(8,128)} %param.10) | copy-start | bytes 3145732
  47.0 1.7 copy-start.2
  50.5 44.9 %collective-permute-start = (f32[8,256,128]{2,1,0:T(8,128)S(1)}, f32[8,256,128]{2,1,0:T(8,128)S(1)}, u32[]{:S(2)}, u32[]{:S(2)}) collective-permute-start(f32[8,256,128]{2,1,0:T(8,128)S(1)} %coefficients.2.refs_0_), channel_id=1, source_target_pairs={{0,12},{1,13},{2,14},{3,15},{4,8},{5,9},{6,10},{7,11},{12,0},{13,1... | collective-permute-start | bytes 3145736 | tf_op jit(solution)/shard_map/ppermute | solution.py:403
  98.8 1.3 copy-start.7
  100.1 7.6 %copy-start = (f32[64,64,128]{2,1,0:T(8,128)}, f32[64,64,128]{2,1,0:T(8,128)S(1)}, u32[]{:S(2)}) copy-start(f32[64,64,128]{2,1,0:T(8,128)S(1)} %all-to-all-done.1) | copy-start | bytes 6291460
  100.1 61.5 %all-to-all-start.2 = ((f32[64,64,128]{2,1,0:T(8,128)}), f32[64,64,128]{2,1,0:T(8,128)}, u32[]{:S(2)}, u32[]{:S(2)}) async-start(f32[64,64,128]{2,1,0:T(8,128)} %bitcast.44), calls=%async_computation.2 | async-start | bytes 4194304 | tf_op jit(solution)/shard_map/all_to_all | solution.py:396
  109.6 47.4 %collective-permute-start.1 = (f32[8,256,128]{2,1,0:T(8,128)S(1)}, f32[8,256,128]{2,1,0:T(8,128)S(1)}, u32[]{:S(2)}, u32[]{:S(2)}) collective-permute-start(f32[8,256,128]{2,1,0:T(8,128)S(1)} %coefficients.3.refs_0_), channel_id=1, source_target_pairs={{0,12},{1,13},{2,14},{3,15},{4,8},{5,9},{6,10},{7,11},{12,0},{13,1... | collective-permute-start | bytes 3145736 | tf_op jit(solution)/shard_map/ppermute | solution.py:403
  161.6 4.8 %copy-start.11 = (s32[1,64,64]{2,1,0:T(8,128)S(1)}, s32[1,64,64]{2,1,0:T(8,128)}, u32[]{:S(2)}) copy-start(s32[1,64,64]{2,1,0:T(8,128)} %param.14) | copy-start | bytes 49156
  161.6 39.9 %all-to-all-start.3 = ((f32[64,64,128]{2,1,0:T(8,128)}), f32[64,64,128]{2,1,0:T(8,128)}, u32[]{:S(2)}, u32[]{:S(2)}) async-start(f32[64,64,128]{2,1,0:T(8,128)} %bitcast.18), calls=%async_computation.3 | async-start | bytes 4194304 | tf_op jit(solution)/shard_map/all_to_all | solution.py:396
  180.1 3.2 %copy-start.10 = (s32[1,64,64]{2,1,0:T(8,128)S(1)}, s32[1,64,64]{2,1,0:T(8,128)}, u32[]{:S(2)}) copy-start(s32[1,64,64]{2,1,0:T(8,128)} %param.13) | copy-start | bytes 49156
  180.1 3.3 %copy-start.12 = (s32[256]{0:T(256)S(1)}, s32[256]{0:T(256)}, u32[]{:S(2)}) copy-start(s32[256]{0:T(256)} %param.15) | copy-start | bytes 3076
  199.5 2.0 copy-start.8
  211.5 17.8 %all-to-all-start.4 = ((f32[16,24,256]{2,1,0:T(8,128)}), f32[16,24,256]{2,1,0:T(8,128)S(1)}, u32[]{:S(2)}, u32[]{:S(2)}) async-start(f32[16,24,256]{2,1,0:T(8,128)} %get-tuple-element.15), calls=%async_computation.4 | async-start | bytes 786432 | tf_op jit(solution)/shard_map/all_to_all | solution.py:413

commit v4 on v3

--- a/solution.py
+++ b/solution.py
@@ -102,11 +102,26 @@
     return pl.CostEstimate(flops=2 * passes * rows * depth * columns, bytes_accessed=moved, transcendentals=0)
 
 
-def coeff_kernel(z_ref, high_ref, low_ref, out_ref, z_high, z_low):
-    blocks, rows, dets, side = z_ref.shape
+def block_reader(me_ref, z_refs):
+    if len(z_refs) > 1:
+        return lambda b, k: z_refs[b][k]
+    return lambda b, k: z_refs[0][me_ref[0] ^ b, k]
+
+
+def slab_specs(slab, step):
+    if len(slab) > 1:
+        return [pl.BlockSpec((step,) + piece.shape[1:], lambda i: (i, 0, 0)) for piece in slab]
+    blocks, _, dets, side = slab[0].shape
+    return [pl.BlockSpec((blocks, step, dets, side), lambda i: (0, i, 0, 0))]
+
+
+def coeff_kernel(blocks, me_ref, *refs):
+    *z_refs, high_ref, low_ref, out_ref, z_high, z_low = refs
+    rows, dets, side = z_refs[0].shape[-3:]
+    block = block_reader(me_ref, z_refs)
     for b in range(blocks):
         for k in range(rows):
-            high, low = halves(z_ref[b, k])
+            high, low = halves(block(b, k))
             z_high[b * dets : (b + 1) * dets, k * side : (k + 1) * side] = high
             z_low[b * dets : (b + 1) * dets, k * side : (k + 1) * side] = low
     total = mm3((high_ref[...], low_ref[...]), (z_high[...], z_low[...]))
@@ -114,51 +129,68 @@
         out_ref[k] = total[:, k * side : (k + 1) * side]
 
 
-def coefficients(slab, weights):
-    blocks, rows, dets, side = slab.shape
-    rank = weights[0].shape[0]
+SCALAR = pl.BlockSpec(memory_space=pltpu.SMEM)
+
+
+def coefficients(me, slab, weights):
+    rows, dets, side = slab[0].shape[-3:]
+    rank, depth = weights[0].shape
     out = jax.ShapeDtypeStruct((rows, rank, side), F32)
     step = math.gcd(2, rows)
-    whole = pl.BlockSpec((rank, blocks * dets), lambda i: (0, 0))
+    whole = pl.BlockSpec((rank, depth), lambda i: (0, 0))
     return pl.pallas_call(
-        coeff_kernel,
+        functools.partial(coeff_kernel, depth // dets),
         grid=(rows // step,),
-        in_specs=[pl.BlockSpec((blocks, step, dets, side), lambda i: (0, i, 0, 0)), whole, whole],
+        in_specs=[SCALAR] + slab_specs(slab, step) + [whole, whole],
         out_specs=pl.BlockSpec((step, rank, side), lambda i: (i, 0, 0)),
         out_shape=out,
-        scratch_shapes=[pltpu.VMEM((blocks * dets, step * side), BF16)] * 2,
+        scratch_shapes=[pltpu.VMEM((depth, step * side), BF16)] * 2,
         compiler_params=LIMIT,
-        cost_estimate=cost(3, rank, blocks * dets, rows * side, slab, out),
+        cost_estimate=cost(3, rank, depth, rows * side, out, *slab),
         name="coefficients",
-    )(slab, *weights)
-
-
-def correct_kernel(terms, z_ref, *refs):
-    c_refs, (high_ref, low_ref, out_ref) = refs[:terms], refs[terms:]
-    blocks, rows, dets, side = z_ref.shape
+    )(me, *slab, *weights)
+
+
+def correct_kernel(pieces, terms, me_ref, *refs):
+    z_refs, c_refs = refs[:pieces], refs[pieces : pieces + terms]
+    high_ref, low_ref, *out_refs = refs[pieces + terms :]
+    rows, dets, side = z_refs[0].shape[-3:]
+    block = block_reader(me_ref, z_refs)
     coeff = halves(jnp.concatenate([sum(c_ref[k] for c_ref in c_refs) for k in range(rows)], axis=1))
     share = mm3((high_ref[...], low_ref[...]), coeff)
-    for b in range(blocks):
+    for b in range(share.shape[0] // dets):
         for k in range(rows):
-            out_ref[b, k] = z_ref[b, k] - share[b * dets : (b + 1) * dets, k * side : (k + 1) * side]
-
-
-def corrected(slab, coeffs, pattern):
-    blocks, rows, dets, side = slab.shape
-    rank = pattern[0].shape[1]
+            value = block(b, k) - share[b * dets : (b + 1) * dets, k * side : (k + 1) * side]
+            if len(out_refs) > 1:
+                out_refs[b][k] = value
+            else:
+                out_refs[0][me_ref[0] ^ b, k] = value
+
+
+def corrected(me, slab, coeffs, pattern, apart):
+    rows, dets, side = slab[0].shape[-3:]
+    depth, rank = pattern[0].shape
+    blocks = depth // dets
     step = math.gcd(2, rows)
-    whole = pl.BlockSpec((blocks * dets, rank), lambda i: (0, 0))
-    block = pl.BlockSpec((blocks, step, dets, side), lambda i: (0, i, 0, 0))
+    whole = pl.BlockSpec((depth, rank), lambda i: (0, 0))
+    if apart:
+        out = [jax.ShapeDtypeStruct((rows, dets, side), F32)] * blocks
+    else:
+        out = [jax.ShapeDtypeStruct((blocks, rows, dets, side), F32)]
+        slab = slab[:]
     return pl.pallas_call(
-        functools.partial(correct_kernel, len(coeffs)),
+        functools.partial(correct_kernel, len(slab), len(coeffs)),
         grid=(rows // step,),
-        in_specs=[block] + [pl.BlockSpec((step, rank, side), lambda i: (i, 0, 0)) for _ in coeffs] + [whole, whole],
-        out_specs=block,
-        out_shape=jax.ShapeDtypeStruct(slab.shape, F32),
+        in_specs=[SCALAR]
+        + slab_specs(slab, step)
+        + [pl.BlockSpec((step, rank, side), lambda i: (i, 0, 0)) for _ in coeffs]
+        + [whole, whole],
+        out_specs=slab_specs(out, step),
+        out_shape=out,
         compiler_params=LIMIT,
-        cost_estimate=cost(3, rank, blocks * dets, rows * side, slab, slab, *coeffs),
+        cost_estimate=cost(3, rank, depth, rows * side, *slab, *out, *coeffs),
         name="corrected",
-    )(pltpu.with_memory_space_constraint(slab, pltpu.HBM), *coeffs, *pattern)
+    )(me, *[pltpu.with_memory_space_constraint(a, pltpu.HBM) for a in slab], *coeffs, *pattern)
 
 
 def section_lines(group, section_ref, d, rows):
@@ -167,46 +199,44 @@
     return mm(section_ref[...], jnp.concatenate([high, low, high], axis=0))
 
 
-def synth_kernel(base, count, steps, z_ref, w_ref, extra_ref, turn_ref, tables_ref, section_ref, rows_ref, hits_ref, *refs):
+def synth_kernel(base, count, steps, pieces, me_ref, *refs):
+    z_refs, refs = refs[:pieces], refs[pieces:]
+    w_ref, extra_ref, turn_ref, tables_ref, section_ref, rows_ref, hits_ref, *refs = refs
     *ends, t_high, t_low, result, held, tile_high, tile_low, total_ref, one = refs
     ending = len(ends) == 4
-    _, dets, side = z_ref.shape
+    dets, side = z_refs[0].shape[-2:]
     step = pl.program_id(0)
-
-    @pl.when(step < steps)
-    def _():
-        first = base + step * count
-        has_zero = base == 0
-
-        def turn(unit):
-            pair = turn_ref[pl.ds(unit, 1), :]
-            return pair[:, :side], pair[:, side:]
-
+    has_zero = base == 0
+
+    def turn(unit):
+        pair = turn_ref[pl.ds(unit, 1), :]
+        return pair[:, :side], pair[:, side:]
+
+    def put(slot, real, imag):
+        for part, value in ((0, real), (1, imag)):
+            high, low = halves(value)
+            t_high[slot * dets : (slot + 1) * dets, part * side : (part + 1) * side] = high
+            t_low[slot * dets : (slot + 1) * dets, part * side : (part + 1) * side] = low
+
+    def transform(high, low):
+        table = lambda i: tables_ref[i * 2 * side : (i + 1) * 2 * side, :]
+        middle = result.shape[0] // 2 // 16 * 16
+        for at in (slice(0, middle), slice(middle, result.shape[0])):
+            result[at] = mm3((t_high[at], t_low[at]), (table(high), table(low)))
+
+    def weigh(units, read):
         half_cos, half_sin = turn(side // 2)
-        turns = [turn(first + i) for i in range(count)]
-        table = lambda i: tables_ref[i * 2 * side : (i + 1) * 2 * side, :]
-
-        def put(slot, real, imag):
-            for part, value in ((0, real), (1, imag)):
-                high, low = halves(value)
-                t_high[slot * dets : (slot + 1) * dets, part * side : (part + 1) * side] = high
-                t_low[slot * dets : (slot + 1) * dets, part * side : (part + 1) * side] = low
-
-        def transform(high, low):
-            middle = result.shape[0] // 2 // 16 * 16
-            for at in (slice(0, middle), slice(middle, result.shape[0])):
-                result[at] = mm3((t_high[at], t_low[at]), (table(high), table(low)))
-
+        turns = [turn(base + unit) for unit in units]
         for i in range(count):
-            real, imag = z_ref[2 * i], z_ref[2 * i + 1]
+            real, imag = read(i)
             if has_zero and i == 0:
                 put(count, imag * half_cos, -imag * half_sin)
-                imag = jnp.where(first == 0, 0.0, imag)
+                imag = jnp.where(units[0] == 0, 0.0, imag)
             cos, sin = turns[i]
             put(i, real * cos + imag * sin, imag * cos - real * sin)
         transform(0, 1)
         for i in range(count + has_zero):
-            weight = extra_ref[...] if i == count else w_ref[i]
+            weight = extra_ref[...] if i == count else w_ref[i if pieces == 1 else units[i]]
             at = slice(i * dets, (i + 1) * dets)
             put(i, result[at, :side] * weight, result[at, side:] * weight)
         transform(2, 3)
@@ -218,11 +248,30 @@
             if has_zero and i == 0:
                 at = slice(count * dets, (count + 1) * dets)
                 nyquist = result[at, :side] * half_cos - result[at, side:] * half_sin
-                turned = jnp.where(first == 0, nyquist, turned)
+                turned = jnp.where(units[0] == 0, nyquist, turned)
             for part, value in ((0, real * cos - imag * sin), (1, turned)):
-                row = pl.multiple_of((2 * (step * count + i) + part) * ROWS, ROWS)
+                row = pl.multiple_of((2 * units[i] + part) * ROWS, ROWS)
                 for group in range(dets // ROWS):
                     held[group, pl.ds(row, ROWS), :] = value[group * ROWS : (group + 1) * ROWS]
+
+    if pieces == 1:
+
+        @pl.when(step < steps)
+        def _():
+            z_ref = z_refs[0]
+            weigh([step * count + i for i in range(count)], lambda i: (z_ref[2 * i], z_ref[2 * i + 1]))
+
+    else:
+        each = z_refs[0].shape[0] // 2
+        for at in range(steps):
+
+            @pl.when(step == at)
+            def _(at=at):
+                slots = [divmod(at * count + i, each) for i in range(count)]
+                weigh(
+                    [(me_ref[0] ^ piece) * each + unit for piece, unit in slots],
+                    lambda i: (z_refs[slots[i][0]][2 * slots[i][1]], z_refs[slots[i][0]][2 * slots[i][1] + 1]),
+                )
 
     @pl.when(step >= steps)
     def _():
@@ -264,8 +313,9 @@
     return jnp.concatenate([high, high, low], axis=1)
 
 
-def synth(base, slab, weight, extra, turns, tables, section, rows, hits, blocks, ending=()):
-    lines, dets, side = slab.shape
+def synth(me, base, slab, weight, extra, turns, tables, section, rows, hits, blocks, ending=()):
+    pieces = len(slab)
+    lines, dets, side = pieces * slab[0].shape[0], *slab[0].shape[1:]
     tiles = rows.size // dets
     count = math.gcd(lines // 2, UNITS)
     steps, groups = lines // (2 * count), dets // ROWS
@@ -273,12 +323,21 @@
     whole = lambda a: pl.BlockSpec(a.shape, lambda i: (0,) * a.ndim)
     later = lambda i: jnp.maximum(i - steps, 0)
     line = pl.BlockSpec((1, 1, ROWS * tiles), lambda i: (later(i), 0, 0))
-    slab, weight = [pltpu.with_memory_space_constraint(a, pltpu.HBM) for a in (slab, weight)]
-    operands = [slab, weight, extra, turns, tables, section, rows.reshape(groups, 1, -1), hits.reshape(groups, 1, -1), *ending]
+    weight = pltpu.with_memory_space_constraint(weight, pltpu.HBM)
+    others = [extra, turns, tables, section]
+    if pieces == 1:
+        slab = [pltpu.with_memory_space_constraint(slab[0], pltpu.HBM)]
+        z_specs = [pl.BlockSpec((2 * count, dets, side), lambda i: (jnp.minimum(i, steps - 1), 0, 0))]
+        w_spec = pl.BlockSpec((count, dets, side), lambda i: (base // count + jnp.minimum(i, steps - 1), 0, 0))
+    else:
+        z_specs = [whole(piece) for piece in slab]
+        w_spec = pl.BlockSpec((lines // 2, dets, side), lambda i: (2 * base // lines, 0, 0))
+    operands = [me, *slab, weight, *others, rows.reshape(groups, 1, -1), hits.reshape(groups, 1, -1), *ending]
     in_specs = [
-        pl.BlockSpec((2 * count, dets, side), lambda i: (jnp.minimum(i, steps - 1), 0, 0)),
-        pl.BlockSpec((count, dets, side), lambda i: (base // count + jnp.minimum(i, steps - 1), 0, 0)),
-        *[whole(a) for a in operands[2:6]],
+        SCALAR,
+        *z_specs,
+        w_spec,
+        *[whole(a) for a in others],
         line,
         line,
         *[whole(a) for a in ending],
@@ -292,7 +351,7 @@
         out = [jax.ShapeDtypeStruct((dets * side, side), F32), jax.ShapeDtypeStruct((blocks, 2 * side), F32)]
         out_specs = [pl.BlockSpec((ROWS * side, side), lambda i: (later(i), 0)), whole(out[1])]
     return pl.pallas_call(
-        functools.partial(synth_kernel, base, count, steps),
+        functools.partial(synth_kernel, base, count, steps, pieces),
         grid=(steps + groups,),
         in_specs=in_specs,
         out_specs=out_specs,
@@ -306,7 +365,7 @@
             pltpu.VMEM((ROWS * side, side), F32),
         ],
         compiler_params=LIMIT,
-        cost_estimate=cost(8, lines // 2 * dets, 2 * side, 2 * side, slab, slab, out[0]),
+        cost_estimate=cost(8, lines // 2 * dets, 2 * side, 2 * side, *slab, *slab, out[0]),
         name="synth",
     )(*operands)
 
@@ -355,22 +414,26 @@
     opposite = [*zip(groups[0], groups[1]), *zip(groups[1], groups[0])]
     mine = lax.axis_index("det") // half
 
+    position = (lax.axis_index("det") % half + mine * quarter) % half
+    me = position.reshape(1)
+
     scale = jnp.broadcast_to(1.0 / gains.reshape(dets, 1), (dets, side))
+    share, each = side // 2, units // size
+    number = lax.iota(jnp.int32, units // 2)
     table = section_table(side, lax.iota(jnp.int32, units))
-    share = side // 2
-    parts = [table[:share], table[share:]]
-    stacks = [stacked(part.T / samples) for part in parts]
+    stacks = [stacked(part.T / samples) for part in (table[:share], table[share:])]
+    parts = [section_table(side, (position ^ (number // each)) * each + number % each), table[share:]]
     z = []
     for part in parts:
         z += sections(timestream.reshape(dets, samples), scale, part, [share])
 
-    def of_half(modes):
-        modes = modes.reshape(4, quarter * dets, -1)
-        parts = [lax.dynamic_index_in_dim(modes, at, 0, keepdims=False) for at in (3 * mine, 1 + mine)]
-        return jnp.concatenate(parts, axis=0)
-
-    weights = table_halves(of_half(mode_weights).T)
-    pattern = table_halves(of_half(mode_pattern))
+    def ordered(modes):
+        modes = modes.reshape(size, dets, -1)
+        at = [mine * half + (mine * quarter + (position ^ k)) % half for k in range(half)]
+        return jnp.concatenate([lax.dynamic_index_in_dim(modes, i, 0, keepdims=False) for i in at], axis=0)
+
+    weights = table_halves(ordered(mode_weights).T)
+    pattern = table_halves(ordered(mode_pattern))
     w = jnp.transpose(noise_weight.reshape(dets, side, side), (2, 0, 1))
     mirror = w[:units:-1, :, ::-1]
     weight = jnp.concatenate([w[:1], w[1:units] + mirror], axis=0)
@@ -396,15 +459,33 @@
         last[0] = lax.all_to_all(value, "det", split_axis=0, concat_axis=0, axis_index_groups=groups, tiled=True)
         return last[0]
 
+    reverse = lambda k: sum((half >> 1 >> bit) for bit in range(half.bit_length() - 1) if k >> bit & 1)
+
+    def trade(pieces):
+        found = list(pieces)
+        for k in map(reverse, range(1, half)):
+            pairs = [(group[p], group[p ^ k]) for group in groups for p in range(half)]
+            found[k] = lax.ppermute(pieces[k], "det", pairs)
+        return found
+
     slabs, coeffs, others = [], [], []
     for c in (0, 1):
-        slabs.append(exchange(z[c]).reshape(half, share // half, dets, side))
-        coeffs.append(coefficients(slabs[c], weights))
+        if c == 0:
+            slab = trade([z[0][2 * each * k : 2 * each * (k + 1)] for k in range(half)])
+            last[0] = slab[half - 1]
+        else:
+            slab = [exchange(z[1]).reshape(half, 2 * each, dets, side)]
+        slabs.append(slab)
+        coeffs.append(coefficients(me, slab, weights))
         others.append(lax.ppermute(coeffs[c], "det", opposite))
     for c in (0, 1):
-        slab = corrected(slabs[c], [coeffs[c], others[c]], pattern)
-        back = exchange(slab.reshape(share, dets, side))
-        operands = [c * units // 2, back, weight, extra, turns, tables, stacks[c], rows, hit, blocks]
+        slab = corrected(me, slabs[c], [coeffs[c], others[c]], pattern, apart=c == 1)
+        if c == 0:
+            back = [exchange(slab[0].reshape(share, dets, side))]
+        else:
+            slab, _ = lax.optimization_barrier((slab, last[0]))
+            back = trade(slab)
+        operands = [me, c * units // 2, back, weight, extra, turns, tables, stacks[c], rows, hit, blocks]
         if c == 0:
             lines, sums = synth(*operands)
         else:

time: 231 us -> 269 us (1.16)
  starting transfers between devices: 32.9 us -> 78.5 us
  waiting for transfers between devices: 110 us -> 71.6 us
  local copies, waits for them, and re-layouts: 32.7 us -> 52.9 us
  other arithmetic: 8.75 us -> 17.7 us
    ppermute x2, waiting for transfers between devices: 86 us -> 40.7 us  [shards(): others.append(lax.ppermute(coeffs[c], 'det', opposite))]
    ppermute x0 -> x14, starting transfers between devices: none -> 39.8 us  [trade(): found[k] = lax.ppermute(pieces[k], 'det', pairs)]
    ppermute x0 -> x14, waiting for transfers between devices: none -> 26.2 us  [trade(): found[k] = lax.ppermute(pieces[k], 'det', pairs)]
    all_to_all x4 -> x2, waiting for transfers between devices: 18.9 us -> 0.01 us  [exchange(): lax.all_to_all(value, 'det', split_axis=0, concat_axis=0, axis_index_grou...]
    unnamed x29 -> x84, local copies, waits for them, and re-layouts: 18.5 us -> 31.3 us
    all_to_all x4 -> x2, starting transfers between devices: 21.2 us -> 27.7 us  [exchange(): lax.all_to_all(value, 'det', split_axis=0, concat_axis=0, axis_index_grou...]
  transfers between devices with their start and end apart: 7 -> 19, of which waited for: 4 -> 9; matrix products, arithmetic and copies ran while one was open for 11% -> 20% of each run, Pallas kernels for 14% -> 12%
where the time goes in v4:
time: 269 us; the launch traced here: 267 us
  starting transfers between devices  78.5 us (29%)
  waiting for transfers between devices  71.6 us (27%)
  local copies, waits for them, and re-layouts  52.9 us (20%)
  Pallas kernels  44.9 us (17%)
  other arithmetic  17.7 us (7%)
    ppermute x2, waiting for transfers between devices, shards(): others.append(lax.ppermute(coeffs[c], 'det', opposite))  40.7 us
    ppermute x14, starting transfers between devices, trade(): found[k] = lax.ppermute(pieces[k], 'det', pairs)  39.8 us
    unnamed x84, local copies, waits for them, and re-layouts  31.3 us
    all_to_all x2, starting transfers between devices, exchange(): lax.all_to_all(value, 'det', split_axis=0, concat_axis=0, axis_index_grou...  27.7 us
    ppermute x14, waiting for transfers between devices, trade(): found[k] = lax.ppermute(pieces[k], 'det', pairs)  26.2 us
    pallas_call x2, Pallas kernels, synth(): pl.pallas_call(functools.partial(synth_kernel, base, count, steps, pieces...  19.1 us
    pallas_call x1, Pallas kernels, emit(): pl.pallas_call(emit_kernel, grid=(groups,), in_specs=[pl.BlockSpec((ROWS...  7.45 us
    pallas_call x2, Pallas kernels, corrected(): pl.pallas_call(functools.partial(correct_kernel, len(slab), len(coeffs)),...  6.82 us
  transfers between devices with their start and end apart: 19, of which 9 were waited for; matrix products, arithmetic and copies ran while one was open for 20% of the time, Pallas kernels for 12%

profile of v4, /device:TPU:0, one launch (start us, length us, event | category | flops | bytes accessed | tf_op | source)
XLA Modules:
  0.0 266.7 jit_solution(13739590246992252138)
XLA Ops:
  4.5 3.3 %sections.2 = f32[64,64,128]{2,1,0:T(8,128)S(1)} custom-call(f32[64,16384]{1,0:T(8,128)S(1)} %bitcast.58, f32[64,128]{1,0:T(8,128)S(1)} %broadcast_in_dim.89.scale_ref, bf16[64,128]{1,0:T(8,128)(2,1)S(1)} %get-tuple-element.81.high_ref, bf16[64,128]{1,0:T(8,128)(2,1)S(1)} %get-tuple-element.80.low_ref), custom_call_target="tpu_custom_call" | custom-call | tf_op jit(solution)/shard_map/sections/pallas_call | solution.py:88
  9.0 3.4 %collective-permute-start.6 = (f32[8,64,128]{2,1,0:T(8,128)S(1)}, f32[8,64,128]{2,1,0:T(8,128)S(1)}, u32[]{:S(2)}, u32[]{:S(2)}) collective-permute-start(f32[8,64,128]{2,1,0:T(8,128)S(1)} %get-tuple-element.48), channel_id=1, source_target_pairs={{0,7},{1,6},{2,5},{3,4},{4,3},{5,2},{6,1},{7,0},{12,11},{13,10},{1... | collective-permute-start | bytes 786440 | tf_op jit(solution)/shard_map/ppermute | solution.py:468
  15.1 3.2 %sections.3 = f32[64,64,128]{2,1,0:T(8,128)S(1)} custom-call(f32[64,16384]{1,0:T(8,128)S(1)} %bitcast.59, f32[64,128]{1,0:T(8,128)S(1)} %broadcast_in_dim.89.scale_ref, bf16[64,128]{1,0:T(8,128)(2,1)S(1)} %get-tuple-element.79.high_ref, bf16[64,128]{1,0:T(8,128)(2,1)S(1)} %get-tuple-element.78.low_ref), custom_call_target="tpu_custom_call" | custom-call | tf_op jit(solution)/shard_map/sections/pallas_call | solution.py:88
  19.7 4.1 %all-to-all-start = ((f32[64,64,128]{2,1,0:T(8,128)}), f32[64,64,128]{2,1,0:T(8,128)S(1)}, u32[]{:S(2)}, u32[]{:S(2)}) async-start(f32[64,64,128]{2,1,0:T(8,128)} %copy-done.3), calls=%async_computation | async-start | bytes 4194304 | tf_op jit(solution)/shard_map/all_to_all | solution.py:459
  47.8 7.8 %collective-permute-done.1.refs_2_ = f32[8,64,128]{2,1,0:T(8,128)S(1)} collective-permute-done((f32[8,64,128]{2,1,0:T(8,128)}, f32[8,64,128]{2,1,0:T(8,128)S(1)}, u32[]{:S(2)}, u32[]{:S(2)}) %collective-permute-start.1) | collective-permute-done | bytes 262176 | tf_op jit(solution)/shard_map/ppermute | solution.py:468
  55.6 4.5 %collective-permute-done.2.refs_3_ = f32[8,64,128]{2,1,0:T(8,128)S(1)} collective-permute-done((f32[8,64,128]{2,1,0:T(8,128)}, f32[8,64,128]{2,1,0:T(8,128)S(1)}, u32[]{:S(2)}, u32[]{:S(2)}) %collective-permute-start.2) | collective-permute-done | bytes 262176 | tf_op jit(solution)/shard_map/ppermute | solution.py:468
  60.2 7.1 %collective-permute-done.5.refs_6_ = f32[8,64,128]{2,1,0:T(8,128)} collective-permute-done((f32[8,64,128]{2,1,0:T(8,128)}, f32[8,64,128]{2,1,0:T(8,128)}, u32[]{:S(2)}, u32[]{:S(2)}) %collective-permute-start.5) | collective-permute-done | bytes 262176 | tf_op jit(solution)/shard_map/ppermute | solution.py:468
  70.5 3.4 %collective-permute-start.7 = (f32[8,256,128]{2,1,0:T(8,128)S(1)}, f32[8,256,128]{2,1,0:T(8,128)S(1)}, u32[]{:S(2)}, u32[]{:S(2)}) collective-permute-start(f32[8,256,128]{2,1,0:T(8,128)S(1)} %coefficients.2.refs_8_), channel_id=1, source_target_pairs={{0,12},{1,13},{2,14},{3,15},{4,8},{5,9},{6,10},{7,11},{12,0},{13,1... | collective-permute-start | bytes 3145736 | tf_op jit(solution)/shard_map/ppermute | solution.py:480
  74.1 22.9 %collective-permute-done.7.refs_9_ = f32[8,256,128]{2,1,0:T(8,128)S(1)} collective-permute-done((f32[8,256,128]{2,1,0:T(8,128)S(1)}, f32[8,256,128]{2,1,0:T(8,128)S(1)}, u32[]{:S(2)}, u32[]{:S(2)}) %collective-permute-start.7) | collective-permute-done | bytes 1048608 | tf_op jit(solution)/shard_map/ppermute | solution.py:480
  97.0 3.5 %corrected.2 = f32[8,8,64,128]{3,2,1,0:T(8,128)S(1)} custom-call(s32[1]{0:T(128)} %bitcast.me_ref, f32[8,64,128]{2,1,0:T(8,128)} %copy-done.8, f32[8,64,128]{2,1,0:T(8,128)} %copy-done.14, f32[8,64,128]{2,1,0:T(8,128)} %copy-done.15, f32[8,64,128]{2,1,0:T(8,128)} %copy-done.16, f32[8,64,128]{2,1,0:T(8,128)} %collective-permute-done.3.refs_4_, ...), custom_call_target="tpu_custom_call" | custom-call | flops 805306368 | bytes 6291456 | tf_op jit(solution)/shard_map/corrected/pallas_call | solution.py:181
  102.6 23.6 %all-to-all-start.1 = ((f32[64,64,128]{2,1,0:T(8,128)}), f32[64,64,128]{2,1,0:T(8,128)}, u32[]{:S(2)}, u32[]{:S(2)}) async-start(f32[64,64,128]{2,1,0:T(8,128)} %bitcast.60), calls=%async_computation.1 | async-start | bytes 4194304 | tf_op jit(solution)/shard_map/all_to_all | solution.py:459
  126.3 4.9 %copy.62 = f32[8,8,128,128]{3,2,1,0:T(8,128)} copy(f32[8,8,128,128]{3,1,2,0:T(8,128)} %bitcast.67) | data formatting | bytes 8388608
  131.2 5.4 %copy.50 = f32[64,128,128]{1,0,2:T(8,128)} copy(f32[64,128,128]{2,1,0:T(8,128)} %bitcast.66) | data formatting | bytes 8388608 | tf_op jit(solution)/shard_map/reshape | solution.py:437
  139.7 4.1 %rev.3 = f32[63,64,128]{2,1,0:T(8,128)} reverse(f32[63,64,128]{2,1,0:T(8,128)} %slice.89), dimensions={0,2} | reverse | bytes 4128768 | tf_op jit(solution)/shard_map/rev | solution.py:438
  145.5 4.2 %slice_add_fusion = f32[63,64,128]{2,1,0:T(8,128)} fusion(f32[63,64,128]{2,1,0:T(8,128)} %rev.3, f32[128,64,128]{2,1,0:T(8,128)} %bitcast.64), kind=kLoop, calls=%fused_computation.5 | loop fusion | flops 516096 | bytes 6193152 | tf_op jit(solution)/shard_map/add | solution.py:439
  161.3 17.8 %collective-permute-done.8.refs_2_ = f32[8,256,128]{2,1,0:T(8,128)S(1)} collective-permute-done((f32[8,256,128]{2,1,0:T(8,128)S(1)}, f32[8,256,128]{2,1,0:T(8,128)S(1)}, u32[]{:S(2)}, u32[]{:S(2)}) %collective-permute-start.8) | collective-permute-done | bytes 1048608 | tf_op jit(solution)/shard_map/ppermute | solution.py:480
  179.1 3.3 %corrected.3 = (f32[8,64,128]{2,1,0:T(8,128)S(1)}, f32[8,64,128]{2,1,0:T(8,128)S(1)}, f32[8,64,128]{2,1,0:T(8,128)S(1)}, f32[8,64,128]{2,1,0:T(8,128)S(1)}, f32[...) custom-call(s32[1]{0:T(128)} %bitcast.me_ref, ...), custom_call_target="tpu_custom_call" | custom-call | flops 805306368 | bytes 6291456 | tf_op jit(solution)/shard_map/corrected/pallas_call | solution.py:181
  191.9 22.1 %collective-permute-start.12 = (f32[8,64,128]{2,1,0:T(8,128)}, f32[8,64,128]{2,1,0:T(8,128)S(1)}, u32[]{:S(2)}, u32[]{:S(2)}) collective-permute-start(f32[8,64,128]{2,1,0:T(8,128)} %copy-done.25), channel_id=1, source_target_pairs={{0,4},{1,5},{2,6},{3,7},{4,0},{5,1},{6,2},{7,3},{12,8},{13,9},{14,... | collective-permute-start | bytes 786440 | tf_op jit(solution)/shard_map/ppermute | solution.py:468
  220.2 9.4 %synth.2 = (f32[8192,128]{1,0:T(8,128)S(1)}, f32[256,256]{1,0:T(8,128)S(1)}) custom-call(s32[1]{0:T(128)} %bitcast.me_ref, f32[64,64,128]{2,1,0:T(8,128)} %all-to-all-done.1.refs_0_, f32[64,64,128]{2,1,0:T(8,128)} %pad_maximum_fusion.refs_1_.refs_8_, f32[64,128]{1,0:T(8,128)S(1)} %get-tuple-element.46.refs_2_.refs_9_, ...), custom_call_target="tpu_custom_call" | custom-call | flops 2147483648 | bytes 8388608 | tf_op jit(solution)/shard_map/synth/pallas_call | solution.py:353
  232.2 6.0 %collective-permute-done.15.refs_7_ = f32[8,64,128]{2,1,0:T(8,128)S(1)} collective-permute-done((f32[8,64,128]{2,1,0:T(8,128)}, f32[8,64,128]{2,1,0:T(8,128)S(1)}, u32[]{:S(2)}, u32[]{:S(2)}) %collective-permute-start.15) | collective-permute-done | bytes 262176 | tf_op jit(solution)/shard_map/ppermute | solution.py:468
  239.2 9.8 %synth.3 = (f32[8,512,128]{2,1,0:T(8,128)S(1)}, f32[16,24,256]{2,1,0:T(8,128)}) custom-call(s32[1]{0:T(128)} %bitcast.me_ref, f32[8,64,128]{2,1,0:T(8,128)S(1)} %copy-done.20, f32[8,64,128]{2,1,0:T(8,128)S(1)} %collective-permute-done.9.refs_1_, f32[8,64,128]{2,1,0:T(8,128)S(1)} %collective-permute-done.10.refs_2_, ...), custom_call_target="tpu_custom_call" | custom-call | flops 2147483648 | bytes 6291456 | tf_op jit(solution)/shard_map/synth/pallas_call | solution.py:353
  248.9 4.9 %all-to-all-start.2 = ((f32[16,24,256]{2,1,0:T(8,128)}), f32[16,24,256]{2,1,0:T(8,128)S(1)}, u32[]{:S(2)}, u32[]{:S(2)}) async-start(f32[16,24,256]{2,1,0:T(8,128)} %get-tuple-element.45), calls=%async_computation.2 | async-start | bytes 786432 | tf_op jit(solution)/shard_map/all_to_all | solution.py:494
  253.8 7.5 %emit.1 = f32[64,16384]{1,0:T(8,128)} custom-call(f32[8192,128]{1,0:T(8,128)} %copy-done.5, f32[8,512,128]{2,1,0:T(8,128)S(1)} %get-tuple-element.44.held_ref, bf16[128,192]{1,0:T(8,128)(2,1)S(1)} %pad_maximum_fusion.8.refs_12_.section_ref), custom_call_target="tpu_custom_call" | custom-call | flops 134217728 | bytes 10485760 | tf_op jit(solution)/shard_map/emit/pallas_call | solution.py:389
  261.3 4.7 %all-to-all-done.2 = f32[16,24,256]{2,1,0:T(8,128)S(1)} async-done(((f32[16,24,256]{2,1,0:T(8,128)}), f32[16,24,256]{2,1,0:T(8,128)S(1)}, u32[]{:S(2)}, u32[]{:S(2)}) %all-to-all-start.2) | async-done | bytes 393248 | tf_op jit(solution)/shard_map/all_to_all | solution.py:494
  (164 shorter events, 74.7 us)
Async XLA Ops:
  9.0 58.3 %copy-start.8 = (f32[8,64,128]{2,1,0:T(8,128)}, f32[8,64,128]{2,1,0:T(8,128)S(1)}, u32[]{:S(2)}) copy-start(f32[8,64,128]{2,1,0:T(8,128)S(1)} %get-tuple-element.55.refs_0_) | copy-start | bytes 786436
  9.0 10.7 %collective-permute-start.6 = (f32[8,64,128]{2,1,0:T(8,128)S(1)}, f32[8,64,128]{2,1,0:T(8,128)S(1)}, u32[]{:S(2)}, u32[]{:S(2)}) collective-permute-start(f32[8,64,128]{2,1,0:T(8,128)S(1)} %get-tuple-element.48), channel_id=1, source_target_pairs={{0,7},{1,6},{2,5},{3,4},{4,3},{5,2},{6,1},{7,0},{12,11},{13,10},{1... | collective-permute-start | bytes 786440 | tf_op jit(solution)/shard_map/ppermute | solution.py:468
  19.6 47.7 %copy-start.13 = (f32[8,64,128]{2,1,0:T(8,128)}, f32[8,64,128]{2,1,0:T(8,128)S(1)}, u32[]{:S(2)}) copy-start(f32[8,64,128]{2,1,0:T(8,128)S(1)} %collective-permute-done.6.refs_7_) | copy-start | bytes 786436
  19.7 83.0 %all-to-all-start = ((f32[64,64,128]{2,1,0:T(8,128)}), f32[64,64,128]{2,1,0:T(8,128)S(1)}, u32[]{:S(2)}, u32[]{:S(2)}) async-start(f32[64,64,128]{2,1,0:T(8,128)} %copy-done.3), calls=%async_computation | async-start | bytes 4194304 | tf_op jit(solution)/shard_map/all_to_all | solution.py:459
  23.7 4.0 %collective-permute-start = (f32[8,64,128]{2,1,0:T(8,128)}, f32[8,64,128]{2,1,0:T(8,128)S(1)}, u32[]{:S(2)}, u32[]{:S(2)}) collective-permute-start(f32[8,64,128]{2,1,0:T(8,128)} %get-tuple-element.54), channel_id=1, source_target_pairs={{0,1},{1,0},{2,3},{3,2},{4,5},{5,4},{6,7},{7,6},{12,13},{13,12},{1... | collective-permute-start | bytes 786440 | tf_op jit(solution)/shard_map/ppermute | solution.py:468
  24.2 31.3 %collective-permute-start.1 = (f32[8,64,128]{2,1,0:T(8,128)}, f32[8,64,128]{2,1,0:T(8,128)S(1)}, u32[]{:S(2)}, u32[]{:S(2)}) collective-permute-start(f32[8,64,128]{2,1,0:T(8,128)} %get-tuple-element.53), channel_id=1, source_target_pairs={{0,2},{1,3},{2,0},{3,1},{4,6},{5,7},{6,4},{7,5},{12,14},{13,15},{1... | collective-permute-start | bytes 786440 | tf_op jit(solution)/shard_map/ppermute | solution.py:468
  25.9 34.2 %collective-permute-start.2 = (f32[8,64,128]{2,1,0:T(8,128)}, f32[8,64,128]{2,1,0:T(8,128)S(1)}, u32[]{:S(2)}, u32[]{:S(2)}) collective-permute-start(f32[8,64,128]{2,1,0:T(8,128)} %get-tuple-element.52), channel_id=1, source_target_pairs={{0,3},{1,2},{2,1},{3,0},{4,7},{5,6},{6,5},{7,4},{12,15},{13,14},{1... | collective-permute-start | bytes 786440 | tf_op jit(solution)/shard_map/ppermute | solution.py:468
  25.9 34.2 %collective-permute-start.3 = (f32[8,64,128]{2,1,0:T(8,128)}, f32[8,64,128]{2,1,0:T(8,128)}, u32[]{:S(2)}, u32[]{:S(2)}) collective-permute-start(f32[8,64,128]{2,1,0:T(8,128)} %get-tuple-element.51), channel_id=1, source_target_pairs={{0,4},{1,5},{2,6},{3,7},{4,0},{5,1},{6,2},{7,3},{12,8},{13,9},{14,... | collective-permute-start | bytes 786440 | tf_op jit(solution)/shard_map/ppermute | solution.py:468
  27.6 32.6 %collective-permute-start.4 = (f32[8,64,128]{2,1,0:T(8,128)}, f32[8,64,128]{2,1,0:T(8,128)}, u32[]{:S(2)}, u32[]{:S(2)}) collective-permute-start(f32[8,64,128]{2,1,0:T(8,128)} %get-tuple-element.50), channel_id=1, source_target_pairs={{0,5},{1,4},{2,7},{3,6},{4,1},{5,0},{6,3},{7,2},{12,9},{13,8},{14,... | collective-permute-start | bytes 786440 | tf_op jit(solution)/shard_map/ppermute | solution.py:468
  27.7 39.6 %collective-permute-start.5 = (f32[8,64,128]{2,1,0:T(8,128)}, f32[8,64,128]{2,1,0:T(8,128)}, u32[]{:S(2)}, u32[]{:S(2)}) collective-permute-start(f32[8,64,128]{2,1,0:T(8,128)} %get-tuple-element.49), channel_id=1, source_target_pairs={{0,6},{1,7},{2,4},{3,5},{4,2},{5,3},{6,0},{7,1},{12,10},{13,11},{1... | collective-permute-start | bytes 786440 | tf_op jit(solution)/shard_map/ppermute | solution.py:468
  47.7 49.3 %copy-start.9 = (bf16[256,512]{1,0:T(8,128)(2,1)}, bf16[256,512]{1,0:T(8,128)(2,1)S(1)}, u32[]{:S(2)}) copy-start(bf16[256,512]{1,0:T(8,128)(2,1)S(1)} %get-tuple-element.66.refs_9_.refs_2_) | copy-start | bytes 786436
  47.7 49.3 %copy-start.11 = (bf16[256,512]{1,0:T(8,128)(2,1)}, bf16[256,512]{1,0:T(8,128)(2,1)S(1)}, u32[]{:S(2)}) copy-start(bf16[256,512]{1,0:T(8,128)(2,1)S(1)} %get-tuple-element.67.refs_8_.refs_1_) | copy-start | bytes 786436
  70.5 26.6 %collective-permute-start.7 = (f32[8,256,128]{2,1,0:T(8,128)S(1)}, f32[8,256,128]{2,1,0:T(8,128)S(1)}, u32[]{:S(2)}, u32[]{:S(2)}) collective-permute-start(f32[8,256,128]{2,1,0:T(8,128)S(1)} %coefficients.2.refs_8_), channel_id=1, source_target_pairs={{0,12},{1,13},{2,14},{3,15},{4,8},{5,9},{6,10},{7,11},{12,0},{13,1... | collective-permute-start | bytes 3145736 | tf_op jit(solution)/shard_map/ppermute | solution.py:480
  102.6 84.8 %all-to-all-start.1 = ((f32[64,64,128]{2,1,0:T(8,128)}), f32[64,64,128]{2,1,0:T(8,128)}, u32[]{:S(2)}, u32[]{:S(2)}) async-start(f32[64,64,128]{2,1,0:T(8,128)} %bitcast.60), calls=%async_computation.1 | async-start | bytes 4194304 | tf_op jit(solution)/shard_map/all_to_all | solution.py:459
  151.6 27.5 %collective-permute-start.8 = (f32[8,256,128]{2,1,0:T(8,128)S(1)}, f32[8,256,128]{2,1,0:T(8,128)S(1)}, u32[]{:S(2)}, u32[]{:S(2)}) collective-permute-start(f32[8,256,128]{2,1,0:T(8,128)S(1)} %coefficients.3.refs_1_), channel_id=1, source_target_pairs={{0,12},{1,13},{2,14},{3,15},{4,8},{5,9},{6,10},{7,11},{12,0},{13,1... | collective-permute-start | bytes 3145736 | tf_op jit(solution)/shard_map/ppermute | solution.py:480
  156.1 64.1 %copy-start.17 = (bf16[1024,256]{1,0:T(8,128)(2,1)S(1)}, bf16[1024,256]{1,0:T(8,128)(2,1)}, u32[]{:S(2)}) copy-start(bf16[1024,256]{1,0:T(8,128)(2,1)} %pad_maximum_fusion.1.refs_4_.refs_11_) | copy-start | bytes 1572868
  187.5 29.4 %collective-permute-start.10 = (f32[8,64,128]{2,1,0:T(8,128)}, f32[8,64,128]{2,1,0:T(8,128)S(1)}, u32[]{:S(2)}, u32[]{:S(2)}) collective-permute-start(f32[8,64,128]{2,1,0:T(8,128)} %copy-done.27), channel_id=1, source_target_pairs={{0,2},{1,3},{2,0},{3,1},{4,6},{5,7},{6,4},{7,5},{12,14},{13,15},{1... | collective-permute-start | bytes 786440 | tf_op jit(solution)/shard_map/ppermute | solution.py:468
  189.1 27.8 %collective-permute-start.11 = (f32[8,64,128]{2,1,0:T(8,128)}, f32[8,64,128]{2,1,0:T(8,128)S(1)}, u32[]{:S(2)}, u32[]{:S(2)}) collective-permute-start(f32[8,64,128]{2,1,0:T(8,128)} %copy-done.26), channel_id=1, source_target_pairs={{0,3},{1,2},{2,1},{3,0},{4,7},{5,6},{6,5},{7,4},{12,15},{13,14},{1... | collective-permute-start | bytes 786440 | tf_op jit(solution)/shard_map/ppermute | solution.py:468
  191.9 39.7 %collective-permute-start.12 = (f32[8,64,128]{2,1,0:T(8,128)}, f32[8,64,128]{2,1,0:T(8,128)S(1)}, u32[]{:S(2)}, u32[]{:S(2)}) collective-permute-start(f32[8,64,128]{2,1,0:T(8,128)} %copy-done.25), channel_id=1, source_target_pairs={{0,4},{1,5},{2,6},{3,7},{4,0},{5,1},{6,2},{7,3},{12,8},{13,9},{14,... | collective-permute-start | bytes 786440 | tf_op jit(solution)/shard_map/ppermute | solution.py:468
  214.0 17.6 %collective-permute-start.13 = (f32[8,64,128]{2,1,0:T(8,128)}, f32[8,64,128]{2,1,0:T(8,128)S(1)}, u32[]{:S(2)}, u32[]{:S(2)}) collective-permute-start(f32[8,64,128]{2,1,0:T(8,128)} %copy-done.24), channel_id=1, source_target_pairs={{0,5},{1,4},{2,7},{3,6},{4,1},{5,0},{6,3},{7,2},{12,9},{13,8},{14,... | collective-permute-start | bytes 786440 | tf_op jit(solution)/shard_map/ppermute | solution.py:468
  214.3 17.9 %collective-permute-start.14 = (f32[8,64,128]{2,1,0:T(8,128)}, f32[8,64,128]{2,1,0:T(8,128)S(1)}, u32[]{:S(2)}, u32[]{:S(2)}) collective-permute-start(f32[8,64,128]{2,1,0:T(8,128)} %copy-done.23), channel_id=1, source_target_pairs={{0,6},{1,7},{2,4},{3,5},{4,2},{5,3},{6,0},{7,1},{12,10},{13,11},{1... | collective-permute-start | bytes 786440 | tf_op jit(solution)/shard_map/ppermute | solution.py:468
  216.9 21.3 %collective-permute-start.15 = (f32[8,64,128]{2,1,0:T(8,128)}, f32[8,64,128]{2,1,0:T(8,128)S(1)}, u32[]{:S(2)}, u32[]{:S(2)}) collective-permute-start(f32[8,64,128]{2,1,0:T(8,128)} %copy-done.22), channel_id=1, source_target_pairs={{0,7},{1,6},{2,5},{3,4},{4,3},{5,2},{6,1},{7,0},{12,11},{13,10},{1... | collective-permute-start | bytes 786440 | tf_op jit(solution)/shard_map/ppermute | solution.py:468
  216.9 21.3 %collective-permute-start.9 = (f32[8,64,128]{2,1,0:T(8,128)}, f32[8,64,128]{2,1,0:T(8,128)S(1)}, u32[]{:S(2)}, u32[]{:S(2)}) collective-permute-start(f32[8,64,128]{2,1,0:T(8,128)} %copy-done.21), channel_id=1, source_target_pairs={{0,1},{1,0},{2,3},{3,2},{4,5},{5,4},{6,7},{7,6},{12,13},{13,12},{1... | collective-permute-start | bytes 786440 | tf_op jit(solution)/shard_map/ppermute | solution.py:468
  248.9 17.0 %all-to-all-start.2 = ((f32[16,24,256]{2,1,0:T(8,128)}), f32[16,24,256]{2,1,0:T(8,128)S(1)}, u32[]{:S(2)}, u32[]{:S(2)}) async-start(f32[16,24,256]{2,1,0:T(8,128)} %get-tuple-element.45), calls=%async_computation.2 | async-start | bytes 786432 | tf_op jit(solution)/shard_map/all_to_all | solution.py:494
  (29 other events, 353.9 us)

commit v5 on v4

--- a/solution.py
+++ b/solution.py
@@ -12,6 +12,7 @@
 F32, BF16 = jnp.float32, jnp.bfloat16
 ROWS = 8
 UNITS = 8
+ALL = pltpu.CompilerParams(vmem_limit_bytes=60 << 20)
 LIMIT = pltpu.CompilerParams(vmem_limit_bytes=16 << 20)
 
 
@@ -136,7 +137,7 @@
     rows, dets, side = slab[0].shape[-3:]
     rank, depth = weights[0].shape
     out = jax.ShapeDtypeStruct((rows, rank, side), F32)
-    step = math.gcd(2, rows)
+    step = math.gcd(8, rows)
     whole = pl.BlockSpec((rank, depth), lambda i: (0, 0))
     return pl.pallas_call(
         functools.partial(coeff_kernel, depth // dets),
@@ -171,7 +172,7 @@
     rows, dets, side = slab[0].shape[-3:]
     depth, rank = pattern[0].shape
     blocks = depth // dets
-    step = math.gcd(2, rows)
+    step = math.gcd(4, rows)
     whole = pl.BlockSpec((depth, rank), lambda i: (0, 0))
     if apart:
         out = [jax.ShapeDtypeStruct((rows, dets, side), F32)] * blocks
@@ -187,7 +188,7 @@
         + [whole, whole],
         out_specs=slab_specs(out, step),
         out_shape=out,
-        compiler_params=LIMIT,
+        compiler_params=ALL if apart else LIMIT,
         cost_estimate=cost(3, rank, depth, rows * side, *slab, *out, *coeffs),
         name="corrected",
     )(me, *[pltpu.with_memory_space_constraint(a, pltpu.HBM) for a in slab], *coeffs, *pattern)
@@ -199,13 +200,8 @@
     return mm(section_ref[...], jnp.concatenate([high, low, high], axis=0))
 
 
-def synth_kernel(base, count, steps, pieces, me_ref, *refs):
-    z_refs, refs = refs[:pieces], refs[pieces:]
-    w_ref, extra_ref, turn_ref, tables_ref, section_ref, rows_ref, hits_ref, *refs = refs
-    *ends, t_high, t_low, result, held, tile_high, tile_low, total_ref, one = refs
-    ending = len(ends) == 4
-    dets, side = z_refs[0].shape[-2:]
-    step = pl.program_id(0)
+def unit_filter(base, count, single, w_ref, extra_ref, turn_ref, tables_ref, t_high, t_low, result, held):
+    dets, side = w_ref.shape[-2:]
     has_zero = base == 0
 
     def turn(unit):
@@ -236,7 +232,7 @@
             put(i, real * cos + imag * sin, imag * cos - real * sin)
         transform(0, 1)
         for i in range(count + has_zero):
-            weight = extra_ref[...] if i == count else w_ref[i if pieces == 1 else units[i]]
+            weight = extra_ref[...] if i == count else w_ref[i if single else units[i]]
             at = slice(i * dets, (i + 1) * dets)
             put(i, result[at, :side] * weight, result[at, side:] * weight)
         transform(2, 3)
@@ -254,7 +250,68 @@
                 for group in range(dets // ROWS):
                     held[group, pl.ds(row, ROWS), :] = value[group * ROWS : (group + 1) * ROWS]
 
-    if pieces == 1:
+    return weigh
+
+
+def weigh_pieces(weigh, me_ref, z_refs, first, count, steps):
+    step = pl.program_id(0)
+    each = z_refs[0].shape[0] // 2
+    for at in range(steps):
+
+        @pl.when(step == at)
+        def _(at=at):
+            slots = [divmod(at * count + i, each) for i in range(count)]
+            weigh(
+                [(me_ref[0] ^ (first + piece)) * each + unit for piece, unit in slots],
+                lambda i: (z_refs[slots[i][0]][2 * slots[i][1]], z_refs[slots[i][0]][2 * slots[i][1] + 1]),
+            )
+
+
+def early_kernel(base, count, steps, pieces, me_ref, *refs):
+    z_refs, (w_ref, turn_ref, tables_ref, out_ref, t_high, t_low, result) = refs[:pieces], refs[pieces:]
+    weigh = unit_filter(base, count, False, w_ref, None, turn_ref, tables_ref, t_high, t_low, result, out_ref)
+    weigh_pieces(weigh, me_ref, z_refs, 0, count, steps)
+
+
+def early(me, base, pieces, weight, turns, tables, count, lines):
+    _, dets, side = pieces[0].shape
+    steps = len(pieces) * pieces[0].shape[0] // (2 * count)
+    out = jax.ShapeDtypeStruct((dets // ROWS, lines * ROWS, side), F32)
+    whole = lambda a: pl.BlockSpec(a.shape, lambda i: (0,) * a.ndim)
+    return pl.pallas_call(
+        functools.partial(early_kernel, base, count, steps, len(pieces)),
+        grid=(steps,),
+        in_specs=[SCALAR]
+        + [whole(piece) for piece in pieces]
+        + [pl.BlockSpec((lines // 2, dets, side), lambda i: (2 * base // lines, 0, 0)), whole(turns), whole(tables)],
+        out_specs=whole(out),
+        out_shape=out,
+        scratch_shapes=[pltpu.VMEM((count * dets, 2 * side), BF16)] * 2 + [pltpu.VMEM((count * dets, 2 * side), F32)],
+        compiler_params=LIMIT,
+        cost_estimate=cost(6, steps * count * dets, 2 * side, 2 * side, out, *pieces),
+        name="early",
+    )(me, *pieces, weight, turns, tables)
+
+
+def synth_kernel(base, count, steps, first, pieces, me_ref, *refs):
+    z_refs, refs = refs[:pieces], refs[pieces:]
+    w_ref, extra_ref, turn_ref, tables_ref, section_ref, rows_ref, hits_ref, *refs = refs
+    *ends, t_high, t_low, result, held, tile_high, tile_low, total_ref, one = refs
+    if first:
+        before_ref, *ends = ends
+    ending = len(ends) == 4
+    _, side = z_refs[0].shape[-2:]
+    step = pl.program_id(0)
+    weigh = unit_filter(
+        base, count, pieces == 1 and not first, w_ref, extra_ref, turn_ref, tables_ref, t_high, t_low, result, held
+    )
+    if first:
+
+        @pl.when(step == 0)
+        def _():
+            held[...] = before_ref[...]
+
+    if pieces == 1 and not first:
 
         @pl.when(step < steps)
         def _():
@@ -262,20 +319,11 @@
             weigh([step * count + i for i in range(count)], lambda i: (z_ref[2 * i], z_ref[2 * i + 1]))
 
     else:
-        each = z_refs[0].shape[0] // 2
-        for at in range(steps):
-
-            @pl.when(step == at)
-            def _(at=at):
-                slots = [divmod(at * count + i, each) for i in range(count)]
-                weigh(
-                    [(me_ref[0] ^ piece) * each + unit for piece, unit in slots],
-                    lambda i: (z_refs[slots[i][0]][2 * slots[i][1]], z_refs[slots[i][0]][2 * slots[i][1] + 1]),
-                )
+        weigh_pieces(weigh, me_ref, z_refs, first, count, steps)
 
     @pl.when(step >= steps)
     def _():
-        rows = 2 * count * steps
+        rows = held.shape[1] // ROWS
         tiles = tile_high.shape[0] // ROWS
         group = held.at[step - steps]
         lines_ref = one if ending else ends[0]
@@ -319,13 +367,18 @@
     tiles = rows.size // dets
     count = math.gcd(lines // 2, UNITS)
     steps, groups = lines // (2 * count), dets // ROWS
+    first = 0
+    if pieces > 1 and steps > 1:
+        first = pieces // steps * (steps - 1)
+        ending = (early(me, base, slab[:first], weight, turns, tables, count, lines), *ending)
+        slab, pieces, steps = slab[first:], pieces - first, 1
     room = (count + (base == 0)) * dets
     whole = lambda a: pl.BlockSpec(a.shape, lambda i: (0,) * a.ndim)
     later = lambda i: jnp.maximum(i - steps, 0)
     line = pl.BlockSpec((1, 1, ROWS * tiles), lambda i: (later(i), 0, 0))
     weight = pltpu.with_memory_space_constraint(weight, pltpu.HBM)
     others = [extra, turns, tables, section]
-    if pieces == 1:
+    if pieces == 1 and not first:
         slab = [pltpu.with_memory_space_constraint(slab[0], pltpu.HBM)]
         z_specs = [pl.BlockSpec((2 * count, dets, side), lambda i: (jnp.minimum(i, steps - 1), 0, 0))]
         w_spec = pl.BlockSpec((count, dets, side), lambda i: (base // count + jnp.minimum(i, steps - 1), 0, 0))
@@ -343,7 +396,7 @@
         *[whole(a) for a in ending],
     ]
     if ending:
-        _, tail = ending
+        tail = ending[-1]
         parcel = (tail.shape[0], blocks // tail.shape[0] + tail.shape[1], tail.shape[2])
         out = [jax.ShapeDtypeStruct((groups, lines * ROWS, side), F32), jax.ShapeDtypeStruct(parcel, F32)]
         out_specs = [pl.BlockSpec((1, lines * ROWS, side), lambda i: (later(i), 0, 0)), whole(out[1])]
@@ -351,7 +404,7 @@
         out = [jax.ShapeDtypeStruct((dets * side, side), F32), jax.ShapeDtypeStruct((blocks, 2 * side), F32)]
         out_specs = [pl.BlockSpec((ROWS * side, side), lambda i: (later(i), 0)), whole(out[1])]
     return pl.pallas_call(
-        functools.partial(synth_kernel, base, count, steps, pieces),
+        functools.partial(synth_kernel, base, count, steps, first, pieces),
         grid=(steps + groups,),
         in_specs=in_specs,
         out_specs=out_specs,

time: 269 us -> 258 us (0.959)
  local copies, waits for them, and re-layouts: 52.9 us -> 41.5 us
  waiting for transfers between devices: 71.6 us -> 80.3 us
  other arithmetic: 17.7 us -> 12.2 us
    unnamed x84, local copies, waits for them, and re-layouts: 31.3 us -> 22 us
    ppermute x14, waiting for transfers between devices: 26.2 us -> 31.4 us  [trade(): found[k] = lax.ppermute(pieces[k], 'det', pairs)]
    ppermute x2, waiting for transfers between devices: 40.7 us -> 45.8 us  [shards(): others.append(lax.ppermute(coeffs[c], 'det', opposite))]
    pallas_call x2 -> x3, Pallas kernels: 19.1 us -> 19.1 us  [the longest x2 16.8 us: synth(): pl.pallas_call(functools.partial(synth_kernel, base, count, steps, first,...]
  transfers between devices with their start and end apart: 19 -> 19, of which waited for: 9 -> 7; matrix products, arithmetic and copies ran while one was open for 20% -> 15% of each run, Pallas kernels for 12% -> 13%
where the time goes in v5:
time: 258 us; the launch traced here: 257 us
  waiting for transfers between devices  80.3 us (31%)
  starting transfers between devices  78 us (30%)
  Pallas kernels  43.3 us (17%)
  local copies, waits for them, and re-layouts  41.5 us (16%)
  other arithmetic  12.2 us (5%)
    ppermute x2, waiting for transfers between devices, shards(): others.append(lax.ppermute(coeffs[c], 'det', opposite))  45.8 us
    ppermute x14, starting transfers between devices, trade(): found[k] = lax.ppermute(pieces[k], 'det', pairs)  39.2 us
    ppermute x14, waiting for transfers between devices, trade(): found[k] = lax.ppermute(pieces[k], 'det', pairs)  31.4 us
    all_to_all x2, starting transfers between devices, exchange(): lax.all_to_all(value, 'det', split_axis=0, concat_axis=0, axis_index_grou...  28.3 us
    unnamed x84, local copies, waits for them, and re-layouts  22 us
    pallas_call x2, Pallas kernels, synth(): pl.pallas_call(functools.partial(synth_kernel, base, count, steps, first,...  16.8 us
    pallas_call x1, Pallas kernels, emit(): pl.pallas_call(emit_kernel, grid=(groups,), in_specs=[pl.BlockSpec((ROWS...  7.44 us
    pallas_call x2, Pallas kernels, corrected(): pl.pallas_call(functools.partial(correct_kernel, len(slab), len(coeffs)),...  6.55 us
  transfers between devices with their start and end apart: 19, of which 7 were waited for; matrix products, arithmetic and copies ran while one was open for 15% of the time, Pallas kernels for 13%

profile of v5, /device:TPU:0, one launch (start us, length us, event | category | flops | bytes accessed | tf_op | source)
XLA Modules:
  0.0 256.7 jit_solution(3625279924122204280)
XLA Ops:
  4.5 3.2 %sections.2 = f32[64,64,128]{2,1,0:T(8,128)S(1)} custom-call(f32[64,16384]{1,0:T(8,128)S(1)} %bitcast.58, f32[64,128]{1,0:T(8,128)S(1)} %broadcast_in_dim.89.scale_ref, bf16[64,128]{1,0:T(8,128)(2,1)S(1)} %get-tuple-element.81.high_ref, bf16[64,128]{1,0:T(8,128)(2,1)S(1)} %get-tuple-element.80.low_ref), custom_call_target="tpu_custom_call" | custom-call | tf_op jit(solution)/shard_map/sections/pallas_call | solution.py:89
  8.9 3.5 %collective-permute-start.6 = (f32[8,64,128]{2,1,0:T(8,128)S(1)}, f32[8,64,128]{2,1,0:T(8,128)S(1)}, u32[]{:S(2)}, u32[]{:S(2)}) collective-permute-start(f32[8,64,128]{2,1,0:T(8,128)S(1)} %get-tuple-element.48), channel_id=1, source_target_pairs={{0,7},{1,6},{2,5},{3,4},{4,3},{5,2},{6,1},{7,0},{12,11},{13,10},{1... | collective-permute-start | bytes 786440 | tf_op jit(solution)/shard_map/ppermute | solution.py:521
  14.4 3.3 %sections.3 = f32[64,64,128]{2,1,0:T(8,128)S(1)} custom-call(f32[64,16384]{1,0:T(8,128)S(1)} %bitcast.59, f32[64,128]{1,0:T(8,128)S(1)} %broadcast_in_dim.89.scale_ref, bf16[64,128]{1,0:T(8,128)(2,1)S(1)} %get-tuple-element.79.high_ref, bf16[64,128]{1,0:T(8,128)(2,1)S(1)} %get-tuple-element.78.low_ref), custom_call_target="tpu_custom_call" | custom-call | tf_op jit(solution)/shard_map/sections/pallas_call | solution.py:89
  19.0 4.6 %all-to-all-start = ((f32[64,64,128]{2,1,0:T(8,128)}), f32[64,64,128]{2,1,0:T(8,128)S(1)}, u32[]{:S(2)}, u32[]{:S(2)}) async-start(f32[64,64,128]{2,1,0:T(8,128)} %copy-done.3), calls=%async_computation | async-start | bytes 4194304 | tf_op jit(solution)/shard_map/all_to_all | solution.py:512
  41.3 14.3 %collective-permute-done.1.refs_2_ = f32[8,64,128]{2,1,0:T(8,128)} collective-permute-done((f32[8,64,128]{2,1,0:T(8,128)}, f32[8,64,128]{2,1,0:T(8,128)}, u32[]{:S(2)}, u32[]{:S(2)}) %collective-permute-start.1) | collective-permute-done | bytes 262176 | tf_op jit(solution)/shard_map/ppermute | solution.py:521
  55.6 4.5 %collective-permute-done.2.refs_3_ = f32[8,64,128]{2,1,0:T(8,128)} collective-permute-done((f32[8,64,128]{2,1,0:T(8,128)}, f32[8,64,128]{2,1,0:T(8,128)}, u32[]{:S(2)}, u32[]{:S(2)}) %collective-permute-start.2) | collective-permute-done | bytes 262176 | tf_op jit(solution)/shard_map/ppermute | solution.py:521
  60.1 7.1 %collective-permute-done.5.refs_6_ = f32[8,64,128]{2,1,0:T(8,128)} collective-permute-done((f32[8,64,128]{2,1,0:T(8,128)}, f32[8,64,128]{2,1,0:T(8,128)}, u32[]{:S(2)}, u32[]{:S(2)}) %collective-permute-start.5) | collective-permute-done | bytes 262176 | tf_op jit(solution)/shard_map/ppermute | solution.py:521
  69.7 3.4 %collective-permute-start.7 = (f32[8,256,128]{2,1,0:T(8,128)S(1)}, f32[8,256,128]{2,1,0:T(8,128)S(1)}, u32[]{:S(2)}, u32[]{:S(2)}) collective-permute-start(f32[8,256,128]{2,1,0:T(8,128)S(1)} %coefficients.2.refs_8_), channel_id=1, source_target_pairs={{0,12},{1,13},{2,14},{3,15},{4,8},{5,9},{6,10},{7,11},{12,0},{13,1... | collective-permute-start | bytes 3145736 | tf_op jit(solution)/shard_map/ppermute | solution.py:533
  73.4 22.9 %collective-permute-done.7.refs_9_ = f32[8,256,128]{2,1,0:T(8,128)S(1)} collective-permute-done((f32[8,256,128]{2,1,0:T(8,128)S(1)}, f32[8,256,128]{2,1,0:T(8,128)S(1)}, u32[]{:S(2)}, u32[]{:S(2)}) %collective-permute-start.7) | collective-permute-done | bytes 1048608 | tf_op jit(solution)/shard_map/ppermute | solution.py:533
  100.4 23.7 %all-to-all-start.1 = ((f32[64,64,128]{2,1,0:T(8,128)}), f32[64,64,128]{2,1,0:T(8,128)}, u32[]{:S(2)}, u32[]{:S(2)}) async-start(f32[64,64,128]{2,1,0:T(8,128)} %bitcast.60), calls=%async_computation.1 | async-start | bytes 4194304 | tf_op jit(solution)/shard_map/all_to_all | solution.py:512
  124.4 4.9 %copy.62 = f32[8,8,128,128]{3,2,1,0:T(8,128)} copy(f32[8,8,128,128]{3,1,2,0:T(8,128)} %bitcast.67) | data formatting | bytes 8388608
  129.4 5.4 %copy.50 = f32[64,128,128]{1,0,2:T(8,128)} copy(f32[64,128,128]{2,1,0:T(8,128)} %bitcast.66) | data formatting | bytes 8388608 | tf_op jit(solution)/shard_map/reshape | solution.py:490
  134.8 3.1 %slice.89 = f32[63,64,128]{2,1,0:T(8,128)} slice(f32[128,64,128]{2,1,0:T(8,128)} %bitcast.63), slice={[65:128], [0:64], [0:128]} | slice | bytes 4128768 | tf_op jit(solution)/shard_map/slice | solution.py:491
  137.9 4.2 %rev.3 = f32[63,64,128]{2,1,0:T(8,128)} reverse(f32[63,64,128]{2,1,0:T(8,128)} %slice.89), dimensions={0,2} | reverse | bytes 4128768 | tf_op jit(solution)/shard_map/rev | solution.py:491
  151.1 22.9 %collective-permute-done.8.refs_2_ = f32[8,256,128]{2,1,0:T(8,128)S(1)} collective-permute-done((f32[8,256,128]{2,1,0:T(8,128)S(1)}, f32[8,256,128]{2,1,0:T(8,128)S(1)}, u32[]{:S(2)}, u32[]{:S(2)}) %collective-permute-start.8) | collective-permute-done | bytes 1048608 | tf_op jit(solution)/shard_map/ppermute | solution.py:533
  175.0 3.8 %corrected.3 = (f32[8,64,128]{2,1,0:T(8,128)}, f32[8,64,128]{2,1,0:T(8,128)}, f32[8,64,128]{2,1,0:T(8,128)}, f32[8,64,128]{2,1,0:T(8,128)}, f32[8,64,128]{2,1,0:...) custom-call(s32[1]{0:T(128)} %bitcast.me_ref, f32[8,8,64,128]{3,2,1,0:T(8,128)} %bitcast.57, ...), custom_call_target="tpu_custom_call" | custom-call | flops 805306368 | bytes 6291456 | tf_op jit(solution)/shard_map/corrected/pallas_call | solution.py:182
  180.6 3.2 %pad_maximum_fusion.refs_1_.refs_6_.refs_2_ = f32[64,64,128]{2,1,0:T(8,128)} fusion(f32[63,64,128]{2,1,0:T(8,128)} %slice_add_fusion, f32[1,64,128]{2,1,0:T(8,128)S(1)} %get-tuple-element.47), kind=kLoop, calls=%fused_computation.4 | loop fusion | flops 524288 | bytes 4194304 | tf_op jit(solution)/shard_map/concatenate | solution.py:492
  184.0 22.2 %collective-permute-start.14 = (f32[8,64,128]{2,1,0:T(8,128)S(1)}, f32[8,64,128]{2,1,0:T(8,128)S(1)}, u32[]{:S(2)}, u32[]{:S(2)}) collective-permute-start(f32[8,64,128]{2,1,0:T(8,128)S(1)} %copy-done.32), channel_id=1, source_target_pairs={{0,4},{1,5},{2,6},{3,7},{4,0},{5,1},{6,2},{7,3},{12,8},{13,9},{14,... | collective-permute-start | bytes 786440 | tf_op jit(solution)/shard_map/ppermute | solution.py:521
  211.5 9.5 %synth.2 = (f32[8192,128]{1,0:T(8,128)S(1)}, f32[256,256]{1,0:T(8,128)S(1)}) custom-call(s32[1]{0:T(128)} %bitcast.me_ref, f32[64,64,128]{2,1,0:T(8,128)} %all-to-all-done.1.refs_0_, f32[64,64,128]{2,1,0:T(8,128)} %pad_maximum_fusion.refs_1_.refs_6_.refs_2_, f32[64,128]{1,0:T(8,128)S(1)} %get-tuple-element.46.refs_2_.refs_3_, ...), custom_call_target="tpu_custom_call" | custom-call | flops 2147483648 | bytes 8388608 | tf_op jit(solution)/shard_map/synth/pallas_call | solution.py:406
  225.4 5.4 %collective-permute-done.9.refs_0_ = f32[8,64,128]{2,1,0:T(8,128)S(1)} collective-permute-done((f32[8,64,128]{2,1,0:T(8,128)S(1)}, f32[8,64,128]{2,1,0:T(8,128)S(1)}, u32[]{:S(2)}, u32[]{:S(2)}) %collective-permute-start.9) | collective-permute-done | bytes 262176 | tf_op jit(solution)/shard_map/ppermute | solution.py:521
  230.9 7.3 %synth.3 = (f32[8,512,128]{2,1,0:T(8,128)S(1)}, f32[16,24,256]{2,1,0:T(8,128)}) custom-call(s32[1]{0:T(128)} %bitcast.me_ref, f32[8,64,128]{2,1,0:T(8,128)S(1)} %collective-permute-done.9.refs_0_, f32[8,64,128]{2,1,0:T(8,128)S(1)} %collective-permute-done.10.refs_1_, f32[64,64,128]{2,1,0:T(8,128)} %pad_maximum_fusion.refs_1_.refs_6_.refs_2_, ...), custom_call_target="tpu_custom_call" | custom-call | flops 2147483648 | bytes 3145728 | tf_op jit(solution)/shard_map/synth/pallas_call | solution.py:406
  239.5 4.3 %all-to-all-start.2 = ((f32[16,24,256]{2,1,0:T(8,128)}), f32[16,24,256]{2,1,0:T(8,128)S(1)}, u32[]{:S(2)}, u32[]{:S(2)}) async-start(f32[16,24,256]{2,1,0:T(8,128)} %get-tuple-element.45), calls=%async_computation.2 | async-start | bytes 786432 | tf_op jit(solution)/shard_map/all_to_all | solution.py:547
  245.4 7.4 %emit.1 = f32[64,16384]{1,0:T(8,128)} custom-call(f32[8192,128]{1,0:T(8,128)} %copy-done.6, f32[8,512,128]{2,1,0:T(8,128)S(1)} %copy-done.14, bf16[128,192]{1,0:T(8,128)(2,1)S(1)} %pad_maximum_fusion.8.refs_6_.section_ref), custom_call_target="tpu_custom_call" | custom-call | flops 134217728 | bytes 10485760 | tf_op jit(solution)/shard_map/emit/pallas_call | solution.py:442
  252.8 3.1 %all-to-all-done.2 = f32[16,24,256]{2,1,0:T(8,128)S(1)} async-done(((f32[16,24,256]{2,1,0:T(8,128)}), f32[16,24,256]{2,1,0:T(8,128)S(1)}, u32[]{:S(2)}, u32[]{:S(2)}) %all-to-all-start.2) | async-done | bytes 393248 | tf_op jit(solution)/shard_map/all_to_all | solution.py:547
  (165 shorter events, 57.9 us)
Async XLA Ops:
  8.9 58.4 %copy-start.10 = (f32[8,64,128]{2,1,0:T(8,128)}, f32[8,64,128]{2,1,0:T(8,128)S(1)}, u32[]{:S(2)}) copy-start(f32[8,64,128]{2,1,0:T(8,128)S(1)} %get-tuple-element.55.refs_0_) | copy-start | bytes 786436
  8.9 10.2 %collective-permute-start.6 = (f32[8,64,128]{2,1,0:T(8,128)S(1)}, f32[8,64,128]{2,1,0:T(8,128)S(1)}, u32[]{:S(2)}, u32[]{:S(2)}) collective-permute-start(f32[8,64,128]{2,1,0:T(8,128)S(1)} %get-tuple-element.48), channel_id=1, source_target_pairs={{0,7},{1,6},{2,5},{3,4},{4,3},{5,2},{6,1},{7,0},{12,11},{13,10},{1... | collective-permute-start | bytes 786440 | tf_op jit(solution)/shard_map/ppermute | solution.py:521
  19.0 48.2 %copy-start.15 = (f32[8,64,128]{2,1,0:T(8,128)}, f32[8,64,128]{2,1,0:T(8,128)S(1)}, u32[]{:S(2)}) copy-start(f32[8,64,128]{2,1,0:T(8,128)S(1)} %collective-permute-done.6.refs_7_) | copy-start | bytes 786436
  19.0 81.4 %all-to-all-start = ((f32[64,64,128]{2,1,0:T(8,128)}), f32[64,64,128]{2,1,0:T(8,128)S(1)}, u32[]{:S(2)}, u32[]{:S(2)}) async-start(f32[64,64,128]{2,1,0:T(8,128)} %copy-done.3), calls=%async_computation | async-start | bytes 4194304 | tf_op jit(solution)/shard_map/all_to_all | solution.py:512
  23.6 4.0 %collective-permute-start = (f32[8,64,128]{2,1,0:T(8,128)S(1)}, f32[8,64,128]{2,1,0:T(8,128)S(1)}, u32[]{:S(2)}, u32[]{:S(2)}) collective-permute-start(f32[8,64,128]{2,1,0:T(8,128)S(1)} %get-tuple-element.54), channel_id=1, source_target_pairs={{0,1},{1,0},{2,3},{3,2},{4,5},{5,4},{6,7},{7,6},{12,13},{13,12},{1... | collective-permute-start | bytes 786440 | tf_op jit(solution)/shard_map/ppermute | solution.py:521
  24.2 31.5 %collective-permute-start.1 = (f32[8,64,128]{2,1,0:T(8,128)}, f32[8,64,128]{2,1,0:T(8,128)}, u32[]{:S(2)}, u32[]{:S(2)}) collective-permute-start(f32[8,64,128]{2,1,0:T(8,128)} %get-tuple-element.53), channel_id=1, source_target_pairs={{0,2},{1,3},{2,0},{3,1},{4,6},{5,7},{6,4},{7,5},{12,14},{13,15},{1... | collective-permute-start | bytes 786440 | tf_op jit(solution)/shard_map/ppermute | solution.py:521
  25.8 34.3 %collective-permute-start.2 = (f32[8,64,128]{2,1,0:T(8,128)}, f32[8,64,128]{2,1,0:T(8,128)}, u32[]{:S(2)}, u32[]{:S(2)}) collective-permute-start(f32[8,64,128]{2,1,0:T(8,128)} %get-tuple-element.52), channel_id=1, source_target_pairs={{0,3},{1,2},{2,1},{3,0},{4,7},{5,6},{6,5},{7,4},{12,15},{13,14},{1... | collective-permute-start | bytes 786440 | tf_op jit(solution)/shard_map/ppermute | solution.py:521
  25.8 34.3 %collective-permute-start.3 = (f32[8,64,128]{2,1,0:T(8,128)}, f32[8,64,128]{2,1,0:T(8,128)}, u32[]{:S(2)}, u32[]{:S(2)}) collective-permute-start(f32[8,64,128]{2,1,0:T(8,128)} %get-tuple-element.51), channel_id=1, source_target_pairs={{0,4},{1,5},{2,6},{3,7},{4,0},{5,1},{6,2},{7,3},{12,8},{13,9},{14,... | collective-permute-start | bytes 786440 | tf_op jit(solution)/shard_map/ppermute | solution.py:521
  27.5 32.6 %collective-permute-start.4 = (f32[8,64,128]{2,1,0:T(8,128)}, f32[8,64,128]{2,1,0:T(8,128)}, u32[]{:S(2)}, u32[]{:S(2)}) collective-permute-start(f32[8,64,128]{2,1,0:T(8,128)} %get-tuple-element.50), channel_id=1, source_target_pairs={{0,5},{1,4},{2,7},{3,6},{4,1},{5,0},{6,3},{7,2},{12,9},{13,8},{14,... | collective-permute-start | bytes 786440 | tf_op jit(solution)/shard_map/ppermute | solution.py:521
  27.7 39.6 %copy-start.16 = (f32[8,64,128]{2,1,0:T(8,128)}, f32[8,64,128]{2,1,0:T(8,128)S(1)}, u32[]{:S(2)}) copy-start(f32[8,64,128]{2,1,0:T(8,128)S(1)} %collective-permute-done.refs_1_) | copy-start | bytes 786436
  27.7 39.6 %collective-permute-start.5 = (f32[8,64,128]{2,1,0:T(8,128)}, f32[8,64,128]{2,1,0:T(8,128)}, u32[]{:S(2)}, u32[]{:S(2)}) collective-permute-start(f32[8,64,128]{2,1,0:T(8,128)} %get-tuple-element.49), channel_id=1, source_target_pairs={{0,6},{1,7},{2,4},{3,5},{4,2},{5,3},{6,0},{7,1},{12,10},{13,11},{1... | collective-permute-start | bytes 786440 | tf_op jit(solution)/shard_map/ppermute | solution.py:521
  41.3 31.9 %copy-start.11 = (bf16[256,512]{1,0:T(8,128)(2,1)}, bf16[256,512]{1,0:T(8,128)(2,1)S(1)}, u32[]{:S(2)}) copy-start(bf16[256,512]{1,0:T(8,128)(2,1)S(1)} %get-tuple-element.67.refs_8_.refs_1_) | copy-start | bytes 786436
  69.7 26.6 %collective-permute-start.7 = (f32[8,256,128]{2,1,0:T(8,128)S(1)}, f32[8,256,128]{2,1,0:T(8,128)S(1)}, u32[]{:S(2)}, u32[]{:S(2)}) collective-permute-start(f32[8,256,128]{2,1,0:T(8,128)S(1)} %coefficients.2.refs_8_), channel_id=1, source_target_pairs={{0,12},{1,13},{2,14},{3,15},{4,8},{5,9},{6,10},{7,11},{12,0},{13,1... | collective-permute-start | bytes 3145736 | tf_op jit(solution)/shard_map/ppermute | solution.py:533
  100.4 44.8 %copy-start = (f32[64,64,128]{2,1,0:T(8,128)}, f32[64,64,128]{2,1,0:T(8,128)S(1)}, u32[]{:S(2)}) copy-start(f32[64,64,128]{2,1,0:T(8,128)S(1)} %all-to-all-done) | copy-start | bytes 6291460
  100.4 78.4 %all-to-all-start.1 = ((f32[64,64,128]{2,1,0:T(8,128)}), f32[64,64,128]{2,1,0:T(8,128)}, u32[]{:S(2)}, u32[]{:S(2)}) async-start(f32[64,64,128]{2,1,0:T(8,128)} %bitcast.60), calls=%async_computation.1 | async-start | bytes 4194304 | tf_op jit(solution)/shard_map/all_to_all | solution.py:512
  146.5 27.5 %collective-permute-start.8 = (f32[8,256,128]{2,1,0:T(8,128)S(1)}, f32[8,256,128]{2,1,0:T(8,128)S(1)}, u32[]{:S(2)}, u32[]{:S(2)}) collective-permute-start(f32[8,256,128]{2,1,0:T(8,128)S(1)} %coefficients.3.refs_1_), channel_id=1, source_target_pairs={{0,12},{1,13},{2,14},{3,15},{4,8},{5,9},{6,10},{7,11},{12,0},{13,1... | collective-permute-start | bytes 3145736 | tf_op jit(solution)/shard_map/ppermute | solution.py:533
  178.8 27.6 %collective-permute-start.11 = (f32[8,64,128]{2,1,0:T(8,128)}, f32[8,64,128]{2,1,0:T(8,128)S(1)}, u32[]{:S(2)}, u32[]{:S(2)}) collective-permute-start(f32[8,64,128]{2,1,0:T(8,128)} %get-tuple-element.38), channel_id=1, source_target_pairs={{0,1},{1,0},{2,3},{3,2},{4,5},{5,4},{6,7},{7,6},{12,13},{13,12},{1... | collective-permute-start | bytes 786440 | tf_op jit(solution)/shard_map/ppermute | solution.py:521
  178.9 30.2 %collective-permute-start.12 = (f32[8,64,128]{2,1,0:T(8,128)}, f32[8,64,128]{2,1,0:T(8,128)S(1)}, u32[]{:S(2)}, u32[]{:S(2)}) collective-permute-start(f32[8,64,128]{2,1,0:T(8,128)} %get-tuple-element.39), channel_id=1, source_target_pairs={{0,2},{1,3},{2,0},{3,1},{4,6},{5,7},{6,4},{7,5},{12,14},{13,15},{1... | collective-permute-start | bytes 786440 | tf_op jit(solution)/shard_map/ppermute | solution.py:521
  183.9 39.1 %collective-permute-start.13 = (f32[8,64,128]{2,1,0:T(8,128)S(1)}, f32[8,64,128]{2,1,0:T(8,128)S(1)}, u32[]{:S(2)}, u32[]{:S(2)}) collective-permute-start(f32[8,64,128]{2,1,0:T(8,128)S(1)} %copy-done.33), channel_id=1, source_target_pairs={{0,3},{1,2},{2,1},{3,0},{4,7},{5,6},{6,5},{7,4},{12,15},{13,14},{1... | collective-permute-start | bytes 786440 | tf_op jit(solution)/shard_map/ppermute | solution.py:521
  184.0 39.0 %collective-permute-start.14 = (f32[8,64,128]{2,1,0:T(8,128)S(1)}, f32[8,64,128]{2,1,0:T(8,128)S(1)}, u32[]{:S(2)}, u32[]{:S(2)}) collective-permute-start(f32[8,64,128]{2,1,0:T(8,128)S(1)} %copy-done.32), channel_id=1, source_target_pairs={{0,4},{1,5},{2,6},{3,7},{4,0},{5,1},{6,2},{7,3},{12,8},{13,9},{14,... | collective-permute-start | bytes 786440 | tf_op jit(solution)/shard_map/ppermute | solution.py:521
  206.3 16.8 %collective-permute-start.15 = (f32[8,64,128]{2,1,0:T(8,128)S(1)}, f32[8,64,128]{2,1,0:T(8,128)S(1)}, u32[]{:S(2)}, u32[]{:S(2)}) collective-permute-start(f32[8,64,128]{2,1,0:T(8,128)S(1)} %copy-done.31), channel_id=1, source_target_pairs={{0,5},{1,4},{2,7},{3,6},{4,1},{5,0},{6,3},{7,2},{12,9},{13,8},{14,... | collective-permute-start | bytes 786440 | tf_op jit(solution)/shard_map/ppermute | solution.py:521
  206.4 19.0 %collective-permute-start.10 = (f32[8,64,128]{2,1,0:T(8,128)S(1)}, f32[8,64,128]{2,1,0:T(8,128)S(1)}, u32[]{:S(2)}, u32[]{:S(2)}) collective-permute-start(f32[8,64,128]{2,1,0:T(8,128)S(1)} %copy-done.30), channel_id=1, source_target_pairs={{0,7},{1,6},{2,5},{3,4},{4,3},{5,2},{6,1},{7,0},{12,11},{13,10},{1... | collective-permute-start | bytes 786440 | tf_op jit(solution)/shard_map/ppermute | solution.py:521
  209.1 21.7 %collective-permute-start.9 = (f32[8,64,128]{2,1,0:T(8,128)S(1)}, f32[8,64,128]{2,1,0:T(8,128)S(1)}, u32[]{:S(2)}, u32[]{:S(2)}) collective-permute-start(f32[8,64,128]{2,1,0:T(8,128)S(1)} %copy-done.29), channel_id=1, source_target_pairs={{0,6},{1,7},{2,4},{3,5},{4,2},{5,3},{6,0},{7,1},{12,10},{13,11},{1... | collective-permute-start | bytes 786440 | tf_op jit(solution)/shard_map/ppermute | solution.py:521
  239.5 16.5 %all-to-all-start.2 = ((f32[16,24,256]{2,1,0:T(8,128)}), f32[16,24,256]{2,1,0:T(8,128)S(1)}, u32[]{:S(2)}, u32[]{:S(2)}) async-start(f32[16,24,256]{2,1,0:T(8,128)} %get-tuple-element.45), calls=%async_computation.2 | async-start | bytes 786432 | tf_op jit(solution)/shard_map/all_to_all | solution.py:547
  (29 other events, 303.5 us)

commit v6 on v5

--- a/solution.py
+++ b/solution.py
@@ -477,8 +477,10 @@
     stacks = [stacked(part.T / samples) for part in (table[:share], table[share:])]
     parts = [section_table(side, (position ^ (number // each)) * each + number % each), table[share:]]
     z = []
-    for part in parts:
-        z += sections(timestream.reshape(dets, samples), scale, part, [share])
+    for c, part in enumerate(parts):
+        signal = timestream.reshape(dets, samples)
+        signal = pltpu.with_memory_space_constraint(signal, pltpu.HBM) if c else signal
+        z += sections(signal, scale, part, [share])
 
     def ordered(modes):
         modes = modes.reshape(size, dets, -1)

time: 258 us -> 259 us (level)
  Pallas kernels: 43.3 us -> 46.3 us
  starting transfers between devices: 78 us -> 75 us
    pallas_call x2, Pallas kernels: 6.52 us -> 9.56 us  [sections(): pl.pallas_call(functools.partial(section_kernel, side), grid=(dets // ROW...]
    unnamed x84 -> x82, local copies, waits for them, and re-layouts: 22 us -> 22 us
  transfers between devices with their start and end apart: 19 -> 19, of which waited for: 7 -> 8; matrix products, arithmetic and copies ran while one was open for 15% -> 15% of each run, Pallas kernels for 13% -> 14%
where the time goes in v6:
time: 259 us; the launch traced here: 258 us
  waiting for transfers between devices  81.3 us (31%)
  starting transfers between devices  75 us (29%)
  Pallas kernels  46.3 us (18%)
  local copies, waits for them, and re-layouts  41.5 us (16%)
  other arithmetic  12.2 us (5%)
    ppermute x2, waiting for transfers between devices, shards(): others.append(lax.ppermute(coeffs[c], 'det', opposite))  46.8 us
    ppermute x14, starting transfers between devices, trade(): found[k] = lax.ppermute(pieces[k], 'det', pairs)  39.2 us
    ppermute x14, waiting for transfers between devices, trade(): found[k] = lax.ppermute(pieces[k], 'det', pairs)  31.4 us
    all_to_all x2, starting transfers between devices, exchange(): lax.all_to_all(value, 'det', split_axis=0, concat_axis=0, axis_index_grou...  26.6 us
    unnamed x82, local copies, waits for them, and re-layouts  22 us
    pallas_call x2, Pallas kernels, synth(): pl.pallas_call(functools.partial(synth_kernel, base, count, steps, first,...  16.8 us
    pallas_call x2, Pallas kernels, sections(): pl.pallas_call(functools.partial(section_kernel, side), grid=(dets // ROW...  9.56 us
    pallas_call x1, Pallas kernels, emit(): pl.pallas_call(emit_kernel, grid=(groups,), in_specs=[pl.BlockSpec((ROWS...  7.44 us
  transfers between devices with their start and end apart: 19, of which 8 were waited for; matrix products, arithmetic and copies ran while one was open for 15% of the time, Pallas kernels for 14%

profile of v6, /device:TPU:0, one launch (start us, length us, event | category | flops | bytes accessed | tf_op | source)
XLA Modules:
  0.0 257.6 jit_solution(8450736902267979909)
XLA Ops:
  4.5 3.2 %sections.2 = f32[64,64,128]{2,1,0:T(8,128)S(1)} custom-call(f32[64,16384]{1,0:T(8,128)S(1)} %bitcast.59, f32[64,128]{1,0:T(8,128)S(1)} %broadcast_in_dim.89.scale_ref, bf16[64,128]{1,0:T(8,128)(2,1)S(1)} %get-tuple-element.81.high_ref, bf16[64,128]{1,0:T(8,128)(2,1)S(1)} %get-tuple-element.80.low_ref), custom_call_target="tpu_custom_call" | custom-call | tf_op jit(solution)/shard_map/sections/pallas_call | solution.py:89
  8.9 3.5 %collective-permute-start.6 = (f32[8,64,128]{2,1,0:T(8,128)S(1)}, f32[8,64,128]{2,1,0:T(8,128)S(1)}, u32[]{:S(2)}, u32[]{:S(2)}) collective-permute-start(f32[8,64,128]{2,1,0:T(8,128)S(1)} %get-tuple-element.48), channel_id=1, source_target_pairs={{0,7},{1,6},{2,5},{3,4},{4,3},{5,2},{6,1},{7,0},{12,11},{13,10},{1... | collective-permute-start | bytes 786440 | tf_op jit(solution)/shard_map/ppermute | solution.py:523
  14.4 6.3 %sections.3 = f32[64,64,128]{2,1,0:T(8,128)S(1)} custom-call(f32[64,16384]{1,0:T(8,128)} %bitcast.58, f32[64,128]{1,0:T(8,128)S(1)} %broadcast_in_dim.89.scale_ref, bf16[64,128]{1,0:T(8,128)(2,1)S(1)} %get-tuple-element.79.high_ref, bf16[64,128]{1,0:T(8,128)(2,1)S(1)} %get-tuple-element.78.low_ref), custom_call_target="tpu_custom_call" | custom-call | tf_op jit(solution)/shard_map/sections/pallas_call | solution.py:89
  22.0 3.6 %all-to-all-start = ((f32[64,64,128]{2,1,0:T(8,128)}), f32[64,64,128]{2,1,0:T(8,128)S(1)}, u32[]{:S(2)}, u32[]{:S(2)}) async-start(f32[64,64,128]{2,1,0:T(8,128)} %copy-done.2), calls=%async_computation | async-start | bytes 4194304 | tf_op jit(solution)/shard_map/all_to_all | solution.py:514
  43.2 14.3 %collective-permute-done.1.refs_2_ = f32[8,64,128]{2,1,0:T(8,128)} collective-permute-done((f32[8,64,128]{2,1,0:T(8,128)}, f32[8,64,128]{2,1,0:T(8,128)}, u32[]{:S(2)}, u32[]{:S(2)}) %collective-permute-start.1) | collective-permute-done | bytes 262176 | tf_op jit(solution)/shard_map/ppermute | solution.py:523
  57.5 4.5 %collective-permute-done.2.refs_3_ = f32[8,64,128]{2,1,0:T(8,128)} collective-permute-done((f32[8,64,128]{2,1,0:T(8,128)}, f32[8,64,128]{2,1,0:T(8,128)}, u32[]{:S(2)}, u32[]{:S(2)}) %collective-permute-start.2) | collective-permute-done | bytes 262176 | tf_op jit(solution)/shard_map/ppermute | solution.py:523
  62.0 7.1 %collective-permute-done.5.refs_6_ = f32[8,64,128]{2,1,0:T(8,128)} collective-permute-done((f32[8,64,128]{2,1,0:T(8,128)}, f32[8,64,128]{2,1,0:T(8,128)}, u32[]{:S(2)}, u32[]{:S(2)}) %collective-permute-start.5) | collective-permute-done | bytes 262176 | tf_op jit(solution)/shard_map/ppermute | solution.py:523
  74.4 23.8 %collective-permute-done.7.refs_9_ = f32[8,256,128]{2,1,0:T(8,128)S(1)} collective-permute-done((f32[8,256,128]{2,1,0:T(8,128)S(1)}, f32[8,256,128]{2,1,0:T(8,128)S(1)}, u32[]{:S(2)}, u32[]{:S(2)}) %collective-permute-start.7) | collective-permute-done | bytes 1048608 | tf_op jit(solution)/shard_map/ppermute | solution.py:535
  98.2 2.7 %corrected.2 = f32[8,8,64,128]{3,2,1,0:T(8,128)S(1)} custom-call(s32[1]{0:T(128)} %bitcast.me_ref, f32[8,64,128]{2,1,0:T(8,128)} %copy-done.9, f32[8,64,128]{2,1,0:T(8,128)} %copy-done.15, f32[8,64,128]{2,1,0:T(8,128)} %collective-permute-done.1.refs_2_, f32[8,64,128]{2,1,0:T(8,128)} %collective-permute-done.2.refs_3_, ...), custom_call_target="tpu_custom_call" | custom-call | flops 805306368 | bytes 6291456 | tf_op jit(solution)/shard_map/corrected/pallas_call | solution.py:182
  102.3 23.0 %all-to-all-start.1 = ((f32[64,64,128]{2,1,0:T(8,128)}), f32[64,64,128]{2,1,0:T(8,128)}, u32[]{:S(2)}, u32[]{:S(2)}) async-start(f32[64,64,128]{2,1,0:T(8,128)} %bitcast.60), calls=%async_computation.1 | async-start | bytes 4194304 | tf_op jit(solution)/shard_map/all_to_all | solution.py:514
  125.7 4.9 %copy.62 = f32[8,8,128,128]{3,2,1,0:T(8,128)} copy(f32[8,8,128,128]{3,1,2,0:T(8,128)} %bitcast.67) | data formatting | bytes 8388608
  130.6 5.4 %copy.50 = f32[64,128,128]{1,0,2:T(8,128)} copy(f32[64,128,128]{2,1,0:T(8,128)} %bitcast.66) | data formatting | bytes 8388608 | tf_op jit(solution)/shard_map/reshape | solution.py:492
  136.0 3.1 %slice.89 = f32[63,64,128]{2,1,0:T(8,128)} slice(f32[128,64,128]{2,1,0:T(8,128)} %bitcast.63), slice={[65:128], [0:64], [0:128]} | slice | bytes 4128768 | tf_op jit(solution)/shard_map/slice | solution.py:493
  139.1 4.2 %rev.3 = f32[63,64,128]{2,1,0:T(8,128)} reverse(f32[63,64,128]{2,1,0:T(8,128)} %slice.89), dimensions={0,2} | reverse | bytes 4128768 | tf_op jit(solution)/shard_map/rev | solution.py:493
  152.2 23.1 %collective-permute-done.8.refs_2_ = f32[8,256,128]{2,1,0:T(8,128)S(1)} collective-permute-done((f32[8,256,128]{2,1,0:T(8,128)S(1)}, f32[8,256,128]{2,1,0:T(8,128)S(1)}, u32[]{:S(2)}, u32[]{:S(2)}) %collective-permute-start.8) | collective-permute-done | bytes 1048608 | tf_op jit(solution)/shard_map/ppermute | solution.py:535
  176.2 3.8 %corrected.3 = (f32[8,64,128]{2,1,0:T(8,128)}, f32[8,64,128]{2,1,0:T(8,128)}, f32[8,64,128]{2,1,0:T(8,128)}, f32[8,64,128]{2,1,0:T(8,128)}, f32[8,64,128]{2,1,0:...) custom-call(s32[1]{0:T(128)} %bitcast.me_ref, f32[8,8,64,128]{3,2,1,0:T(8,128)} %bitcast.57, ...), custom_call_target="tpu_custom_call" | custom-call | flops 805306368 | bytes 6291456 | tf_op jit(solution)/shard_map/corrected/pallas_call | solution.py:182
  181.8 3.2 %pad_maximum_fusion.refs_1_.refs_6_.refs_2_ = f32[64,64,128]{2,1,0:T(8,128)} fusion(f32[63,64,128]{2,1,0:T(8,128)} %slice_add_fusion, f32[1,64,128]{2,1,0:T(8,128)S(1)} %get-tuple-element.47), kind=kLoop, calls=%fused_computation.4 | loop fusion | flops 524288 | bytes 4194304 | tf_op jit(solution)/shard_map/concatenate | solution.py:494
  185.2 22.2 %collective-permute-start.14 = (f32[8,64,128]{2,1,0:T(8,128)S(1)}, f32[8,64,128]{2,1,0:T(8,128)S(1)}, u32[]{:S(2)}, u32[]{:S(2)}) collective-permute-start(f32[8,64,128]{2,1,0:T(8,128)S(1)} %copy-done.31), channel_id=1, source_target_pairs={{0,4},{1,5},{2,6},{3,7},{4,0},{5,1},{6,2},{7,3},{12,8},{13,9},{14,... | collective-permute-start | bytes 786440 | tf_op jit(solution)/shard_map/ppermute | solution.py:523
  212.7 9.5 %synth.2 = (f32[8192,128]{1,0:T(8,128)S(1)}, f32[256,256]{1,0:T(8,128)S(1)}) custom-call(s32[1]{0:T(128)} %bitcast.me_ref, f32[64,64,128]{2,1,0:T(8,128)} %all-to-all-done.1.refs_0_, f32[64,64,128]{2,1,0:T(8,128)} %pad_maximum_fusion.refs_1_.refs_6_.refs_2_, f32[64,128]{1,0:T(8,128)S(1)} %get-tuple-element.46.refs_2_.refs_3_, ...), custom_call_target="tpu_custom_call" | custom-call | flops 2147483648 | bytes 8388608 | tf_op jit(solution)/shard_map/synth/pallas_call | solution.py:406
  226.6 5.4 %collective-permute-done.9.refs_0_ = f32[8,64,128]{2,1,0:T(8,128)S(1)} collective-permute-done((f32[8,64,128]{2,1,0:T(8,128)S(1)}, f32[8,64,128]{2,1,0:T(8,128)S(1)}, u32[]{:S(2)}, u32[]{:S(2)}) %collective-permute-start.9) | collective-permute-done | bytes 262176 | tf_op jit(solution)/shard_map/ppermute | solution.py:523
  232.0 7.3 %synth.3 = (f32[8,512,128]{2,1,0:T(8,128)S(1)}, f32[16,24,256]{2,1,0:T(8,128)}) custom-call(s32[1]{0:T(128)} %bitcast.me_ref, f32[8,64,128]{2,1,0:T(8,128)S(1)} %collective-permute-done.9.refs_0_, f32[8,64,128]{2,1,0:T(8,128)S(1)} %collective-permute-done.10.refs_1_, f32[64,64,128]{2,1,0:T(8,128)} %pad_maximum_fusion.refs_1_.refs_6_.refs_2_, ...), custom_call_target="tpu_custom_call" | custom-call | flops 2147483648 | bytes 3145728 | tf_op jit(solution)/shard_map/synth/pallas_call | solution.py:406
  240.6 4.1 %all-to-all-start.2 = ((f32[16,24,256]{2,1,0:T(8,128)}), f32[16,24,256]{2,1,0:T(8,128)S(1)}, u32[]{:S(2)}, u32[]{:S(2)}) async-start(f32[16,24,256]{2,1,0:T(8,128)} %get-tuple-element.45), calls=%async_computation.2 | async-start | bytes 786432 | tf_op jit(solution)/shard_map/all_to_all | solution.py:549
  246.3 7.4 %emit.1 = f32[64,16384]{1,0:T(8,128)} custom-call(f32[8192,128]{1,0:T(8,128)} %copy-done.5, f32[8,512,128]{2,1,0:T(8,128)S(1)} %copy-done.13, bf16[128,192]{1,0:T(8,128)(2,1)S(1)} %pad_maximum_fusion.8.refs_6_.section_ref), custom_call_target="tpu_custom_call" | custom-call | flops 134217728 | bytes 10485760 | tf_op jit(solution)/shard_map/emit/pallas_call | solution.py:442
  253.8 3.1 %all-to-all-done.2 = f32[16,24,256]{2,1,0:T(8,128)S(1)} async-done(((f32[16,24,256]{2,1,0:T(8,128)}), f32[16,24,256]{2,1,0:T(8,128)S(1)}, u32[]{:S(2)}, u32[]{:S(2)}) %all-to-all-start.2) | async-done | bytes 393248 | tf_op jit(solution)/shard_map/all_to_all | solution.py:549
  (163 shorter events, 57.4 us)
Async XLA Ops:
  8.9 60.3 %copy-start.9 = (f32[8,64,128]{2,1,0:T(8,128)}, f32[8,64,128]{2,1,0:T(8,128)S(1)}, u32[]{:S(2)}) copy-start(f32[8,64,128]{2,1,0:T(8,128)S(1)} %get-tuple-element.55.refs_0_) | copy-start | bytes 786436
  8.9 13.2 %collective-permute-start.6 = (f32[8,64,128]{2,1,0:T(8,128)S(1)}, f32[8,64,128]{2,1,0:T(8,128)S(1)}, u32[]{:S(2)}, u32[]{:S(2)}) collective-permute-start(f32[8,64,128]{2,1,0:T(8,128)S(1)} %get-tuple-element.48), channel_id=1, source_target_pairs={{0,7},{1,6},{2,5},{3,4},{4,3},{5,2},{6,1},{7,0},{12,11},{13,10},{1... | collective-permute-start | bytes 786440 | tf_op jit(solution)/shard_map/ppermute | solution.py:523
  22.0 47.1 %copy-start.14 = (f32[8,64,128]{2,1,0:T(8,128)}, f32[8,64,128]{2,1,0:T(8,128)S(1)}, u32[]{:S(2)}) copy-start(f32[8,64,128]{2,1,0:T(8,128)S(1)} %collective-permute-done.6.refs_7_) | copy-start | bytes 786436
  22.0 80.3 %all-to-all-start = ((f32[64,64,128]{2,1,0:T(8,128)}), f32[64,64,128]{2,1,0:T(8,128)S(1)}, u32[]{:S(2)}, u32[]{:S(2)}) async-start(f32[64,64,128]{2,1,0:T(8,128)} %copy-done.2), calls=%async_computation | async-start | bytes 4194304 | tf_op jit(solution)/shard_map/all_to_all | solution.py:514
  25.6 4.2 %collective-permute-start = (f32[8,64,128]{2,1,0:T(8,128)S(1)}, f32[8,64,128]{2,1,0:T(8,128)S(1)}, u32[]{:S(2)}, u32[]{:S(2)}) collective-permute-start(f32[8,64,128]{2,1,0:T(8,128)S(1)} %get-tuple-element.54), channel_id=1, source_target_pairs={{0,1},{1,0},{2,3},{3,2},{4,5},{5,4},{6,7},{7,6},{12,13},{13,12},{1... | collective-permute-start | bytes 786440 | tf_op jit(solution)/shard_map/ppermute | solution.py:523
  26.3 31.2 %collective-permute-start.1 = (f32[8,64,128]{2,1,0:T(8,128)}, f32[8,64,128]{2,1,0:T(8,128)}, u32[]{:S(2)}, u32[]{:S(2)}) collective-permute-start(f32[8,64,128]{2,1,0:T(8,128)} %get-tuple-element.53), channel_id=1, source_target_pairs={{0,2},{1,3},{2,0},{3,1},{4,6},{5,7},{6,4},{7,5},{12,14},{13,15},{1... | collective-permute-start | bytes 786440 | tf_op jit(solution)/shard_map/ppermute | solution.py:523
  27.7 34.3 %collective-permute-start.2 = (f32[8,64,128]{2,1,0:T(8,128)}, f32[8,64,128]{2,1,0:T(8,128)}, u32[]{:S(2)}, u32[]{:S(2)}) collective-permute-start(f32[8,64,128]{2,1,0:T(8,128)} %get-tuple-element.52), channel_id=1, source_target_pairs={{0,3},{1,2},{2,1},{3,0},{4,7},{5,6},{6,5},{7,4},{12,15},{13,14},{1... | collective-permute-start | bytes 786440 | tf_op jit(solution)/shard_map/ppermute | solution.py:523
  27.8 34.2 %collective-permute-start.3 = (f32[8,64,128]{2,1,0:T(8,128)}, f32[8,64,128]{2,1,0:T(8,128)}, u32[]{:S(2)}, u32[]{:S(2)}) collective-permute-start(f32[8,64,128]{2,1,0:T(8,128)} %get-tuple-element.51), channel_id=1, source_target_pairs={{0,4},{1,5},{2,6},{3,7},{4,0},{5,1},{6,2},{7,3},{12,8},{13,9},{14,... | collective-permute-start | bytes 786440 | tf_op jit(solution)/shard_map/ppermute | solution.py:523
  29.4 32.6 %collective-permute-start.4 = (f32[8,64,128]{2,1,0:T(8,128)}, f32[8,64,128]{2,1,0:T(8,128)}, u32[]{:S(2)}, u32[]{:S(2)}) collective-permute-start(f32[8,64,128]{2,1,0:T(8,128)} %get-tuple-element.50), channel_id=1, source_target_pairs={{0,5},{1,4},{2,7},{3,6},{4,1},{5,0},{6,3},{7,2},{12,9},{13,8},{14,... | collective-permute-start | bytes 786440 | tf_op jit(solution)/shard_map/ppermute | solution.py:523
  29.8 39.3 %copy-start.15 = (f32[8,64,128]{2,1,0:T(8,128)}, f32[8,64,128]{2,1,0:T(8,128)S(1)}, u32[]{:S(2)}) copy-start(f32[8,64,128]{2,1,0:T(8,128)S(1)} %collective-permute-done.refs_1_) | copy-start | bytes 786436
  29.8 39.3 %collective-permute-start.5 = (f32[8,64,128]{2,1,0:T(8,128)}, f32[8,64,128]{2,1,0:T(8,128)}, u32[]{:S(2)}, u32[]{:S(2)}) collective-permute-start(f32[8,64,128]{2,1,0:T(8,128)} %get-tuple-element.49), channel_id=1, source_target_pairs={{0,6},{1,7},{2,4},{3,5},{4,2},{5,3},{6,0},{7,1},{12,10},{13,11},{1... | collective-permute-start | bytes 786440 | tf_op jit(solution)/shard_map/ppermute | solution.py:523
  43.2 31.0 %copy-start.10 = (bf16[256,512]{1,0:T(8,128)(2,1)}, bf16[256,512]{1,0:T(8,128)(2,1)S(1)}, u32[]{:S(2)}) copy-start(bf16[256,512]{1,0:T(8,128)(2,1)S(1)} %get-tuple-element.67.refs_8_.refs_1_) | copy-start | bytes 786436
  71.6 26.6 %collective-permute-start.7 = (f32[8,256,128]{2,1,0:T(8,128)S(1)}, f32[8,256,128]{2,1,0:T(8,128)S(1)}, u32[]{:S(2)}, u32[]{:S(2)}) collective-permute-start(f32[8,256,128]{2,1,0:T(8,128)S(1)} %coefficients.2.refs_8_), channel_id=1, source_target_pairs={{0,12},{1,13},{2,14},{3,15},{4,8},{5,9},{6,10},{7,11},{12,0},{13,1... | collective-permute-start | bytes 3145736 | tf_op jit(solution)/shard_map/ppermute | solution.py:535
  102.3 44.1 %copy-start = (f32[64,64,128]{2,1,0:T(8,128)}, f32[64,64,128]{2,1,0:T(8,128)S(1)}, u32[]{:S(2)}) copy-start(f32[64,64,128]{2,1,0:T(8,128)S(1)} %all-to-all-done) | copy-start | bytes 6291460
  102.3 77.7 %all-to-all-start.1 = ((f32[64,64,128]{2,1,0:T(8,128)}), f32[64,64,128]{2,1,0:T(8,128)}, u32[]{:S(2)}, u32[]{:S(2)}) async-start(f32[64,64,128]{2,1,0:T(8,128)} %bitcast.60), calls=%async_computation.1 | async-start | bytes 4194304 | tf_op jit(solution)/shard_map/all_to_all | solution.py:514
  147.7 27.5 %collective-permute-start.8 = (f32[8,256,128]{2,1,0:T(8,128)S(1)}, f32[8,256,128]{2,1,0:T(8,128)S(1)}, u32[]{:S(2)}, u32[]{:S(2)}) collective-permute-start(f32[8,256,128]{2,1,0:T(8,128)S(1)} %coefficients.3.refs_1_), channel_id=1, source_target_pairs={{0,12},{1,13},{2,14},{3,15},{4,8},{5,9},{6,10},{7,11},{12,0},{13,1... | collective-permute-start | bytes 3145736 | tf_op jit(solution)/shard_map/ppermute | solution.py:535
  180.0 27.6 %collective-permute-start.11 = (f32[8,64,128]{2,1,0:T(8,128)}, f32[8,64,128]{2,1,0:T(8,128)S(1)}, u32[]{:S(2)}, u32[]{:S(2)}) collective-permute-start(f32[8,64,128]{2,1,0:T(8,128)} %get-tuple-element.38), channel_id=1, source_target_pairs={{0,1},{1,0},{2,3},{3,2},{4,5},{5,4},{6,7},{7,6},{12,13},{13,12},{1... | collective-permute-start | bytes 786440 | tf_op jit(solution)/shard_map/ppermute | solution.py:523
  180.1 30.2 %collective-permute-start.12 = (f32[8,64,128]{2,1,0:T(8,128)}, f32[8,64,128]{2,1,0:T(8,128)S(1)}, u32[]{:S(2)}, u32[]{:S(2)}) collective-permute-start(f32[8,64,128]{2,1,0:T(8,128)} %get-tuple-element.39), channel_id=1, source_target_pairs={{0,2},{1,3},{2,0},{3,1},{4,6},{5,7},{6,4},{7,5},{12,14},{13,15},{1... | collective-permute-start | bytes 786440 | tf_op jit(solution)/shard_map/ppermute | solution.py:523
  185.1 39.1 %collective-permute-start.13 = (f32[8,64,128]{2,1,0:T(8,128)S(1)}, f32[8,64,128]{2,1,0:T(8,128)S(1)}, u32[]{:S(2)}, u32[]{:S(2)}) collective-permute-start(f32[8,64,128]{2,1,0:T(8,128)S(1)} %copy-done.32), channel_id=1, source_target_pairs={{0,3},{1,2},{2,1},{3,0},{4,7},{5,6},{6,5},{7,4},{12,15},{13,14},{1... | collective-permute-start | bytes 786440 | tf_op jit(solution)/shard_map/ppermute | solution.py:523
  185.2 39.0 %collective-permute-start.14 = (f32[8,64,128]{2,1,0:T(8,128)S(1)}, f32[8,64,128]{2,1,0:T(8,128)S(1)}, u32[]{:S(2)}, u32[]{:S(2)}) collective-permute-start(f32[8,64,128]{2,1,0:T(8,128)S(1)} %copy-done.31), channel_id=1, source_target_pairs={{0,4},{1,5},{2,6},{3,7},{4,0},{5,1},{6,2},{7,3},{12,8},{13,9},{14,... | collective-permute-start | bytes 786440 | tf_op jit(solution)/shard_map/ppermute | solution.py:523
  207.5 16.7 %collective-permute-start.15 = (f32[8,64,128]{2,1,0:T(8,128)S(1)}, f32[8,64,128]{2,1,0:T(8,128)S(1)}, u32[]{:S(2)}, u32[]{:S(2)}) collective-permute-start(f32[8,64,128]{2,1,0:T(8,128)S(1)} %copy-done.30), channel_id=1, source_target_pairs={{0,5},{1,4},{2,7},{3,6},{4,1},{5,0},{6,3},{7,2},{12,9},{13,8},{14,... | collective-permute-start | bytes 786440 | tf_op jit(solution)/shard_map/ppermute | solution.py:523
  207.6 19.0 %collective-permute-start.10 = (f32[8,64,128]{2,1,0:T(8,128)S(1)}, f32[8,64,128]{2,1,0:T(8,128)S(1)}, u32[]{:S(2)}, u32[]{:S(2)}) collective-permute-start(f32[8,64,128]{2,1,0:T(8,128)S(1)} %copy-done.29), channel_id=1, source_target_pairs={{0,7},{1,6},{2,5},{3,4},{4,3},{5,2},{6,1},{7,0},{12,11},{13,10},{1... | collective-permute-start | bytes 786440 | tf_op jit(solution)/shard_map/ppermute | solution.py:523
  210.3 21.7 %collective-permute-start.9 = (f32[8,64,128]{2,1,0:T(8,128)S(1)}, f32[8,64,128]{2,1,0:T(8,128)S(1)}, u32[]{:S(2)}, u32[]{:S(2)}) collective-permute-start(f32[8,64,128]{2,1,0:T(8,128)S(1)} %copy-done.28), channel_id=1, source_target_pairs={{0,6},{1,7},{2,4},{3,5},{4,2},{5,3},{6,0},{7,1},{12,10},{13,11},{1... | collective-permute-start | bytes 786440 | tf_op jit(solution)/shard_map/ppermute | solution.py:523
  240.6 16.3 %all-to-all-start.2 = ((f32[16,24,256]{2,1,0:T(8,128)}), f32[16,24,256]{2,1,0:T(8,128)S(1)}, u32[]{:S(2)}, u32[]{:S(2)}) async-start(f32[16,24,256]{2,1,0:T(8,128)} %get-tuple-element.45), calls=%async_computation.2 | async-start | bytes 786432 | tf_op jit(solution)/shard_map/all_to_all | solution.py:549
  (28 other events, 298.9 us)
